TPU v7x, 32 devices: a whole 2x2x4 slice. The times are simulated.
32 devices in a mesh: batch: 4 (over z), pb: 2 (over x), ka: 4 (over y, core).
Axes of the slice: x: 2, y: 2, z: 4, core: 2. Of those that a mesh axis runs over, the one named last changes fastest.
Arguments:
- inputs: bfloat16 [16, 1024, 768], P('batch', ('pb', 'ka')), may hold values from -6 to 6
- block_place: int32 [16, 8], P('batch'), may hold values from 0 to 7, each once within a row
- ln1_gain: float32 [768], replicated, may hold values from 0.1 to 1.9
- ln1_shift: float32 [768], replicated, may hold values from -3 to 3
- w_qkv: bfloat16 [768, 2304], replicated, may hold values from -0.21875 to 0.21875
- w_out: bfloat16 [768, 768], replicated, may hold values from -1.25 to 1.25
- ln2_gain: float32 [768], replicated, may hold values from 0.1 to 1.9
- ln2_shift: float32 [768], replicated, may hold values from -3 to 3
- w_up: bfloat16 [768, 3072], replicated, may hold values from -0.21875 to 0.21875
- w_down: bfloat16 [3072, 768], replicated, may hold values from -0.109375 to 0.109375
- cotangent: bfloat16 [16, 1024, 768], P('batch', ('pb', 'ka')), may hold values from -6 to 6
Outputs:
- outputs: bfloat16 [16, 1024, 768], P('batch', ('pb', 'ka'))
- grad_inputs: bfloat16 [16, 1024, 768], P('batch', ('pb', 'ka'))
- grad_qkv: float32 [768, 2304], P('batch', ('pb', 'ka'))
- grad_proj: float32 [768, 768], P('batch', ('pb', 'ka'))
- grad_up: float32 [768, 3072], P('batch', ('pb', 'ka'))
- grad_down: float32 [3072, 768], P('batch', ('pb', 'ka'))
- grad_norms: float32 [4, 768], P(None, ('pb', 'ka'))
Inputs may be any that keep to these rules, and one draw needn't show every extreme that they name: Each row of block_place lists every number 0 to 7 exactly once.
All inputs are finite; a program needn't handle non-finite values.
Results may differ from a plain program's by a relative error of at most 0.015.
The roundings to bfloat16 on the way count: a program that leaves them out, or rounds other values in their place, can miss the bound.
Values may be sent and summed in bfloat16 or wider, within the bound.
No kernel may reach another device: no remote copies, remote signals or barrier semaphores. Data moves between devices by JAX's collectives and lax.ppermute only.
A program may use at most 192 MiB of HBM per device.

v0:
```python
import functools

import jax
import jax.numpy as jnp
from jax import lax
from jax.experimental import pallas as pl
from jax.experimental.pallas import tpu as pltpu
from jax.sharding import PartitionSpec as P

HEADS = 12
HEAD = 64
PAIR = 2 * HEAD
QTILE = 256
STRIP = 32
SCALE = HEAD ** (-0.5)
HUGE = 3e38
HIDDEN = -1e30

norm_eps = 1e-05
BF16 = jnp.bfloat16
F32 = jnp.float32


def norm_rows(values, gain_vec, shift_vec):
    average = jnp.mean(values, axis=-1, keepdims=True)
    centred = values - average
    spread = jnp.mean(centred * centred, axis=-1, keepdims=True)
    return centred * lax.rsqrt(spread + norm_eps) * gain_vec + shift_vec


def gelu_tanh(values):
    return jax.nn.gelu(values, approximate=True)


def dot(a, b, contract):
    return lax.dot_general(a, b, ((contract[:1], contract[1:]), ((), ())), preferred_element_type=F32)


def head_lanes(values, head):
    lane = lax.broadcasted_iota(jnp.int32, values.shape, 1)
    mine = lane < HEAD if head == 0 else lane >= HEAD
    return jnp.where(mine, values, jnp.zeros_like(values))


def hide_later(magnitude):
    keys = magnitude.shape[0]
    key = lax.broadcasted_iota(jnp.int32, (QTILE, QTILE), 0)
    query = lax.broadcasted_iota(jnp.int32, (QTILE, QTILE), 1)
    last = jnp.where(key <= query, magnitude[keys - QTILE :], HIDDEN)
    return last if keys == QTILE else jnp.concatenate([magnitude[: keys - QTILE], last], axis=0)


def sign_of(scores):
    return jnp.clip(scores * HUGE, -1.0, 1.0)


def attend_kernel(
    core_ref, place_ref, mine_ref, other_ref, gain_ref, shift_ref, wq_ref, wk_ref, wv_ref,
    out_ref, normed_ref, qkv_ref, sums_ref, stats_ref, o_sc,
):
    blocks, half = mine_ref.shape[0], mine_ref.shape[1]
    rows = 2 * half
    total_rows = normed_ref.shape[0]

    @pl.when(pl.program_id(0) == 0)
    def _():
        @pl.loop(0, blocks)
        def _(block):
            for ref, part in ((mine_ref, core_ref[0]), (other_ref, 1 - core_ref[0])):
                at = pl.multiple_of(place_ref[block] * rows + part * half, half)
                normed = norm_rows(ref[block].astype(F32), gain_ref[...], shift_ref[...])
                normed_ref[pl.ds(at, half), :] = normed.astype(BF16)

    weights = jnp.concatenate([wq_ref[...], wk_ref[...], wv_ref[...]], axis=1)
    qkv_ref[0] = jnp.dot(normed_ref[...], weights, preferred_element_type=F32).astype(BF16)
    v_t = qkv_ref[0, :, 2 * PAIR :].T
    for tile in range(total_rows // QTILE):
        span = slice(tile * QTILE, (tile + 1) * QTILE)
        keys = (tile + 1) * QTILE
        queries = qkv_ref[0, span, :PAIR] * SCALE
        for head in range(2):
            scores = dot(qkv_ref[0, :keys, PAIR : 2 * PAIR], head_lanes(queries, head).astype(BF16), (1, 1))
            magnitude = hide_later(jnp.abs(scores))
            peak = jnp.max(magnitude, axis=0, keepdims=True)
            exponents = jnp.exp(magnitude - peak)
            total = jnp.sum(exponents, axis=0, keepdims=True)
            weights = (exponents * sign_of(scores)).astype(BF16)
            summed = dot(v_t[head * HEAD : (head + 1) * HEAD, :keys], weights, (1, 0))
            sums_ref[0, head * HEAD : (head + 1) * HEAD, span] = summed / total
            stats_ref[0, head : head + 1, span] = peak + jnp.log(total)
        o_sc[span, :] = sums_ref[0, :, span].T
    for block in range(blocks):
        at = pl.multiple_of(place_ref[block] * rows, rows)
        out_ref[block] = o_sc[pl.ds(at, rows), :].astype(BF16)


def columns_of(width, size, kind, pairs):
    return pl.BlockSpec(
        (width, size), lambda i, core, place: (0, kind * (width // size) + core[0] * pairs + jnp.minimum(i, pairs - 1))
    )


def fixed2(shape):
    return pl.BlockSpec(shape, lambda i, *scalars, n=len(shape): (0,) * n)


def attend(core, place, mine, other, gain, shift, w_qkv):
    blocks, half, width = mine.shape
    length, pairs = 2 * half * blocks, width // PAIR // 2
    area = length * length
    return pl.pallas_call(
        attend_kernel,
        grid_spec=pltpu.PrefetchScalarGridSpec(
            num_scalar_prefetch=2,
            grid=(pairs,),
            in_specs=[fixed2(mine.shape), fixed2(mine.shape), fixed2((width,)), fixed2((width,))]
            + [columns_of(width, PAIR, kind, pairs) for kind in range(3)],
            out_specs=[
                pl.BlockSpec((blocks, 2 * half, PAIR), lambda i, c, p: (0, 0, i)),
                fixed2((length, width)),
                pl.BlockSpec((1, length, 3 * PAIR), lambda i, c, p: (i, 0, 0)),
                pl.BlockSpec((1, PAIR, length), lambda i, c, p: (i, 0, 0)),
                pl.BlockSpec((1, 8, length), lambda i, c, p: (i, 0, 0)),
            ],
            scratch_shapes=[pltpu.VMEM((length, PAIR), F32)],
        ),
        out_shape=[
            jax.ShapeDtypeStruct((blocks, 2 * half, pairs * PAIR), BF16),
            jax.ShapeDtypeStruct((length, width), BF16),
            jax.ShapeDtypeStruct((pairs, length, 3 * PAIR), BF16),
            jax.ShapeDtypeStruct((pairs, PAIR, length), F32),
            jax.ShapeDtypeStruct((pairs, 8, length), F32),
        ],
        cost_estimate=pl.CostEstimate(
            flops=pairs * 16 * area * HEAD + 3 * length * width * width,
            bytes_accessed=8 * length * width,
            transcendentals=pairs * area,
        ),
        name="attend",
    )(core, place, mine, other, gain, shift, w_qkv, w_qkv, w_qkv)


def attend_back_kernel(
    core_ref, place_ref, to_ref, qkv_ref, g_ref, sums_ref, stats_ref, normed_ref, out_ref, gq_ref, g_sc, dq_sc, dk_sc, dv_sc
):
    blocks, rows = g_ref.shape[0], g_ref.shape[1]
    for block in range(blocks):
        at = pl.multiple_of(place_ref[block] * rows, rows)
        g_sc[pl.ds(at, rows), :] = g_ref[block]
    total_rows = g_sc.shape[0]
    k_t = qkv_ref[0, :, PAIR : 2 * PAIR].T
    g_t = g_sc[...].astype(F32).T
    products = g_t * sums_ref[0]
    deltas = [
        jnp.sum(products[head * HEAD : (head + 1) * HEAD], axis=0, keepdims=True) for head in range(2)
    ]
    dk_sc[...] = jnp.zeros_like(dk_sc)
    dv_sc[...] = jnp.zeros_like(dv_sc)
    for tile in range(total_rows // QTILE):
        span = slice(tile * QTILE, (tile + 1) * QTILE)
        keys = (tile + 1) * QTILE
        queries = qkv_ref[0, span, :PAIR] * SCALE
        parts = []
        for head in range(2):
            q_head = head_lanes(queries, head).astype(BF16)
            g_head = head_lanes(g_sc[span, :], head)
            scores = dot(qkv_ref[0, :keys, PAIR : 2 * PAIR], q_head, (1, 1))
            magnitude = hide_later(jnp.abs(scores))
            sign = sign_of(scores)
            signed = jnp.exp(magnitude - stats_ref[0, head : head + 1, span]) * sign
            grad_weights = dot(qkv_ref[0, :keys, 2 * PAIR :], g_head, (1, 1))
            grad_scores = (signed * (sign * grad_weights - deltas[head][:, span])).astype(BF16)
            dv_sc[:keys, :] += dot(signed.astype(BF16), g_head, (1, 0))
            dk_sc[:keys, :] += dot(grad_scores, q_head, (1, 0))
            parts.append(dot(k_t[head * HEAD : (head + 1) * HEAD, :keys], grad_scores, (1, 0)))
        dq_sc[span, :] = jnp.concatenate(parts, axis=0).T * SCALE
    for kind, ref in enumerate((dq_sc, dk_sc, dv_sc)):
        grad = ref[...].astype(BF16)
        out_ref[:, kind * PAIR : (kind + 1) * PAIR] = grad
        turned = jnp.dot(grad.T, normed_ref[...], preferred_element_type=F32).astype(BF16)
        for strip in range(PAIR // STRIP):
            at = to_ref[(pl.program_id(0) * 3 + kind) * (PAIR // STRIP) + strip]
            at = pl.multiple_of(at * STRIP, STRIP)
            gq_ref[pl.ds(at, STRIP), :] = turned[strip * STRIP : (strip + 1) * STRIP]


def attend_back(core, place, to, qkv, grad, sums, stats, normed):
    pairs, length, _ = qkv.shape
    blocks, rows, _ = grad.shape
    width = normed.shape[1]
    area = length * length
    one = lambda i, c, p, t: (i, 0, 0)
    return pl.pallas_call(
        attend_back_kernel,
        grid_spec=pltpu.PrefetchScalarGridSpec(
            num_scalar_prefetch=3,
            grid=(pairs,),
            in_specs=[
                pl.BlockSpec((1, length, 3 * PAIR), one),
                pl.BlockSpec((blocks, rows, PAIR), lambda i, c, p, t: (0, 0, i)),
                pl.BlockSpec((1, PAIR, length), one),
                pl.BlockSpec((1, 8, length), one),
                fixed2(normed.shape),
            ],
            out_specs=[
                pl.BlockSpec((length, 3 * PAIR), lambda i, c, p, t: (0, i)),
                fixed2((pairs * 3 * PAIR, width)),
            ],
            scratch_shapes=[pltpu.VMEM((length, PAIR), BF16)] + [pltpu.VMEM((length, PAIR), F32)] * 3,
        ),
        out_shape=[
            jax.ShapeDtypeStruct((length, pairs * 3 * PAIR), BF16),
            jax.ShapeDtypeStruct((pairs * 3 * PAIR, width), BF16),
        ],
        cost_estimate=pl.CostEstimate(
            flops=pairs * 40 * area * HEAD + 3 * length * width * width,
            bytes_accessed=8 * length * width,
            transcendentals=pairs * area,
        ),
        name="attend_back",
    )(core, place, to, qkv, grad, sums, stats, normed)


def normed_back_kernel(
    core_ref, place_ref, back_ref, grad_ref, mine_ref, other_ref, norm_ref, wq_ref, wk_ref, wv_ref,
    keep_ref, send_ref, sums_ref, w_sc,
):
    step = pl.program_id(0)
    half = mine_ref.shape[1]
    pairs = wq_ref.shape[1] // PAIR

    @pl.when(step == 0)
    def _():
        sums_ref[...] = norm_ref[...]
        for pair in range(pairs):
            for kind, ref in enumerate((wq_ref, wk_ref, wv_ref)):
                w_sc[:, (pair * 3 + kind) * PAIR : (pair * 3 + kind + 1) * PAIR] = ref[
                    :, pair * PAIR : (pair + 1) * PAIR
                ]

    back = dot(grad_ref[...], w_sc[...], (1, 1))
    for at in range(grad_ref.shape[0] // (2 * half)):
        block = back_ref[step * (grad_ref.shape[0] // (2 * half)) + at]
        low = back[2 * at * half : (2 * at + 1) * half]
        high = back[(2 * at + 1) * half : (2 * at + 2) * half]
        first = core_ref[0] == 0
        mine, other = jnp.where(first, low, high), jnp.where(first, high, low)
        keep_ref[block] = mine
        send_ref[block] = other.astype(BF16)
        for grad, ref in ((mine, mine_ref), (other, other_ref)):
            x = ref[block].astype(F32)
            centred = x - jnp.mean(x, axis=-1, keepdims=True)
            unit = centred * lax.rsqrt(jnp.mean(centred * centred, axis=-1, keepdims=True) + norm_eps)
            sums_ref[0:1, :] += jnp.sum(grad * unit, axis=0, keepdims=True)
            sums_ref[1:2, :] += jnp.sum(grad, axis=0, keepdims=True)


def normed_back(core, place, back, grad, mine, other, norm, w_qkv):
    length, size = grad.shape
    blocks, half, width = mine.shape
    steps = 4
    columns = [
        pl.BlockSpec((width, size // 3), lambda i, core, p, b, kind=kind: (0, kind * 2 + core[0])) for kind in range(3)
    ]
    return pl.pallas_call(
        normed_back_kernel,
        grid_spec=pltpu.PrefetchScalarGridSpec(
            num_scalar_prefetch=3,
            grid=(steps,),
            in_specs=[
                pl.BlockSpec((length // steps, size), lambda i, c, p, b: (i, 0)),
                fixed2(mine.shape),
                fixed2(mine.shape),
                fixed2(norm.shape),
                *columns,
            ],
            out_specs=[fixed2(mine.shape), fixed2(mine.shape), fixed2(norm.shape)],
            scratch_shapes=[pltpu.VMEM((width, size), BF16)],
        ),
        out_shape=[
            jax.ShapeDtypeStruct(mine.shape, F32),
            jax.ShapeDtypeStruct(mine.shape, BF16),
            jax.ShapeDtypeStruct(norm.shape, F32),
        ],
        cost_estimate=pl.CostEstimate(
            flops=2 * length * width * size, bytes_accessed=8 * length * width, transcendentals=0
        ),
        name="normed_back",
    )(core, place, back, grad, mine, other, norm, w_qkv, w_qkv, w_qkv)


def merge_kernel(keep_ref, other_ref, norm_ref, out_ref):
    half = keep_ref.shape[1]
    block = norm_ref.shape[1] // keep_ref.shape[0]
    norms = norm_ref[...].astype(BF16)
    for at in range(keep_ref.shape[0]):
        out_ref[at, :half] = (keep_ref[at] + other_ref[at].astype(F32)).astype(BF16)
        out_ref[at, half:] = jnp.zeros_like(out_ref[at, half:])
        out_ref[at, half:, :block] = norms[:, at * block : (at + 1) * block]


def merge(keep, other, norm):
    blocks, half, width = keep.shape
    return pl.pallas_call(
        merge_kernel,
        grid=(1,),
        in_specs=[fixed2(keep.shape), fixed2(keep.shape), fixed2(norm.shape)],
        out_specs=fixed2((blocks, half + norm.shape[0], width)),
        out_shape=jax.ShapeDtypeStruct((blocks, half + norm.shape[0], width), BF16),
        cost_estimate=pl.CostEstimate(
            flops=blocks * half * width, bytes_accessed=8 * blocks * half * width, transcendentals=0
        ),
        name="merge",
    )(keep, other, norm)


@functools.lru_cache
def strips(width, plane):
    near, owned = plane // 2, 3 * width // plane // STRIP
    side, pair = width // 2 // STRIP, PAIR // STRIP
    slots = []
    for core in range(2):
        slot, count = {}, [0, 0]
        for col in range(2 * near * owned):
            if col % (2 * side) // side == core:
                away = (col // owned % 2) ^ core
                slot[col] = (away, count[away])
                count[away] += 1
        assert count == [near * owned // 2] * 2
        slots.append(slot)
    stay = near * owned // 2
    to, found = [], []
    for core in range(2):
        order = [
            kind * 2 * side + core * side + p * pair + strip
            for p in range(side // pair)
            for kind in range(3)
            for strip in range(pair)
        ]
        to.append([slots[core][col][0] * stay + slots[core][col][1] for col in order])
        row = []
        for chip in range(near):
            for strip in range(owned):
                col = (2 * chip + core) * owned + strip
                row.append(slots[core][col][1] if col in slots[core] else stay + slots[1 - core][col][1])
        found.append(row)
    return to, found


def tiles_kernel(near, owned, chip_ref, found_ref, keep_ref, given_ref, *outs):
    step = pl.program_id(0)
    stay = keep_ref.shape[0] // STRIP
    for k in range(near):

        @pl.when(step == k)
        def _():
            for strip in range(owned):
                at = found_ref[(chip_ref[0] ^ k) * owned + strip]
                here = pl.multiple_of(jnp.minimum(at, stay - 1) * STRIP, STRIP)
                there = pl.multiple_of(jnp.maximum(at - stay, 0) * STRIP, STRIP)
                outs[k][strip * STRIP : (strip + 1) * STRIP, :] = jnp.where(
                    at < stay, keep_ref[pl.ds(here, STRIP), :], given_ref[pl.ds(there, STRIP), :]
                )


def qkv_tiles(chip, found, keep, given, near):
    size, width = keep.shape
    owned = 2 * size // near // STRIP
    shape = (owned * STRIP, width)
    return pl.pallas_call(
        functools.partial(tiles_kernel, near, owned),
        grid_spec=pltpu.PrefetchScalarGridSpec(
            num_scalar_prefetch=2,
            grid=(near,),
            in_specs=[fixed2(keep.shape), fixed2(keep.shape)],
            out_specs=[fixed2(shape)] * near,
        ),
        out_shape=[jax.ShapeDtypeStruct(shape, BF16)] * near,
        cost_estimate=pl.CostEstimate(flops=size * width, bytes_accessed=8 * size * width, transcendentals=0),
        name="qkv_tiles",
    )(chip, found, keep, given)


def gelu_pair(u):
    c = 0.7978845608028654
    square = u * u
    t = jnp.tanh(c * u * (1.0 + 0.044715 * square))
    half = 0.5 * (1.0 + t)
    slope = half + 0.5 * c * u * (1.0 - t * t) * (1.0 + 3.0 * 0.044715 * square)
    return u * half, slope


def norm_back(values, gain_vec, grad):
    average = jnp.mean(values, axis=-1, keepdims=True)
    centred = values - average
    spread = jnp.mean(centred * centred, axis=-1, keepdims=True)
    scale = lax.rsqrt(spread + norm_eps)
    unit = centred * scale
    scaled = grad * gain_vec
    back = scale * (
        scaled
        - jnp.mean(scaled, axis=-1, keepdims=True)
        - unit * jnp.mean(scaled * unit, axis=-1, keepdims=True)
    )
    return back, jnp.sum(grad * unit, axis=0, keepdims=True), jnp.sum(grad, axis=0, keepdims=True)


def ff_kernel(seqs, plane, *refs):
    me_ref, x_ref, att_ref, cot_ref, w_out_ref, gain_ref, shift_ref, up_ref, down_ref, *refs = refs
    out_ref, res_ref, *refs = refs
    ga_ref, norm_ref, gu_send, gu_keep, gd_send, gd_keep, gp_send, gp_keep, *refs = refs
    att_sc, residual_sc, normed_sc, normed_t, turned_sc, acc_out, acc_grad = refs
    step = pl.program_id(0)
    tokens, width = x_ref.shape
    rows = tokens // seqs
    block = width // plane
    near = plane // 2

    def turn(values):
        turned = values.T
        for j in range(plane):
            t = me_ref[0] ^ j
            slot = (1 - (t & 1)) * near + (t >> 1)
            at = pl.multiple_of(slot * block, block)
            turned_sc[pl.ds(at, block), :] = turned[j * block : (j + 1) * block]

    @pl.when(step == 0)
    def _():
        for seq in range(seqs):
            for core in range(2):
                cols = slice(core * width // 2, (core + 1) * width // 2)
                att_sc[seq * rows : (seq + 1) * rows, cols] = att_ref[seq * 2 + core]
        residual = x_ref[...].astype(F32) + jnp.dot(att_sc[...], w_out_ref[...], preferred_element_type=F32)
        residual_sc[...] = residual
        normed = norm_rows(residual, gain_ref[...], shift_ref[...]).astype(BF16)
        normed_sc[...] = normed
        normed_t[...] = normed.T
        turn(cot_ref[...])
        acc_out[...] = jnp.zeros_like(acc_out)
        acc_grad[...] = jnp.zeros_like(acc_grad)

    pre = jnp.dot(normed_sc[...], up_ref[...], preferred_element_type=F32)
    active, slope = gelu_pair(pre)
    active = active.astype(BF16)
    grad_pre = (dot(cot_ref[...], down_ref[...], (1, 1)) * slope).astype(BF16)
    acc_out[...] += jnp.dot(active, down_ref[...], preferred_element_type=F32)
    acc_grad[...] += dot(grad_pre, up_ref[...], (1, 1))
    grad_up = jnp.dot(normed_t[...], grad_pre, preferred_element_type=F32).astype(BF16)
    grad_down = jnp.dot(turned_sc[...], active, preferred_element_type=F32).astype(BF16)
    for slot in range(near):
        gd_send[slot, 0] = grad_down[slot * block : (slot + 1) * block]
        gd_keep[slot, 0] = grad_down[(near + slot) * block : (near + slot + 1) * block]

    @pl.when(step < near)
    def _():
        gu_send[0] = grad_up

    @pl.when(step >= near)
    def _():
        gu_keep[0] = grad_up

    @pl.when(step == plane - 1)
    def _():
        residual = residual_sc[...]
        out_ref[...] = (residual + acc_out[...]).astype(BF16)
        back, gain_grad, shift_grad = norm_back(residual, gain_ref[...], acc_grad[...])
        norm_ref[...] = jnp.zeros_like(norm_ref)
        norm_ref[2:3, :] = gain_grad
        norm_ref[3:4, :] = shift_grad
        grad_res = cot_ref[...].astype(F32) + back
        res_ref[...] = grad_res
        grad_z = grad_res.astype(BF16)
        grad_att = dot(grad_z, w_out_ref[...], (1, 1)).astype(BF16)
        for seq in range(seqs):
            for core in range(2):
                cols = slice(core * width // 2, (core + 1) * width // 2)
                ga_ref[seq * 2 + core] = grad_att[seq * rows : (seq + 1) * rows, cols]
        turn(grad_z)
        grad_proj = jnp.dot(turned_sc[...], att_sc[...], preferred_element_type=F32).astype(BF16)
        for slot in range(near):
            gp_send[slot] = grad_proj[slot * block : (slot + 1) * block]
            gp_keep[slot] = grad_proj[(near + slot) * block : (near + slot + 1) * block]


def feed_forward(me, x, attended, cotangent, w_out, gain, shift, w_up, w_down, plane):
    seqs, rows, width = x.shape
    hidden = w_up.shape[1]
    tokens, near, part, block = seqs * rows, plane // 2, hidden // plane, width // plane

    def at(i, me):
        return me[0] ^ (2 * (i % near) + jnp.where(i < near, 1, 0))

    def fixed(shape):
        return pl.BlockSpec(shape, lambda i, me, n=len(shape): (0,) * n)

    joined = attended.shape
    outs = [
        ((tokens, width), BF16, fixed((tokens, width))),
        ((tokens, width), F32, fixed((tokens, width))),
        (joined, BF16, fixed(joined)),
        ((8, width), F32, fixed((8, width))),
        ((near, width, part), BF16, pl.BlockSpec((1, width, part), lambda i, me: (jnp.minimum(i, near - 1), 0, 0))),
        ((near, width, part), BF16, pl.BlockSpec((1, width, part), lambda i, me: (jnp.maximum(i - near, 0), 0, 0))),
        *[
            (
                (near, plane, block, part),
                BF16,
                pl.BlockSpec((near, 1, block, part), lambda i, me: (0, at(i, me), 0, 0)),
            )
        ]
        * 2,
        *[((near, block, width), BF16, fixed((near, block, width)))] * 2,
    ]
    return pl.pallas_call(
        functools.partial(ff_kernel, seqs, plane),
        grid_spec=pltpu.PrefetchScalarGridSpec(
            num_scalar_prefetch=1,
            grid=(plane,),
            in_specs=[fixed((tokens, width))]
            + [fixed(joined), fixed((tokens, width)), fixed((width, width)), fixed((width,)), fixed((width,))]
            + [
                pl.BlockSpec((width, part), lambda i, me: (0, at(i, me))),
                pl.BlockSpec((part, width), lambda i, me: (at(i, me), 0)),
            ],
            out_specs=[o[2] for o in outs],
            scratch_shapes=[
                pltpu.VMEM((tokens, width), BF16),
                pltpu.VMEM((tokens, width), F32),
                pltpu.VMEM((tokens, width), BF16),
                pltpu.VMEM((width, tokens), BF16),
                pltpu.VMEM((width, tokens), BF16),
                pltpu.VMEM((tokens, width), F32),
                pltpu.VMEM((tokens, width), F32),
            ],
        ),
        out_shape=[jax.ShapeDtypeStruct(o[0], o[1]) for o in outs],
        cost_estimate=pl.CostEstimate(
            flops=12 * tokens * width * hidden + 6 * tokens * width * width,
            bytes_accessed=8 * width * hidden,
            transcendentals=tokens * hidden,
        ),
        name="feed_forward",
    )(
        me,
        x.reshape(tokens, width),
        attended,
        cotangent.reshape(tokens, width),
        w_out,
        gain,
        shift,
        w_up,
        w_down,
    )


def first_norm_kernel(seqs, x_ref, gain_ref, grad_ref, res_ref, out_ref, norm_ref):
    half = x_ref.shape[0] // seqs // 2
    for piece in range(2 * seqs):
        at = slice(piece * half, (piece + 1) * half)
        values = x_ref[at].astype(F32)
        centred = values - jnp.mean(values, axis=-1, keepdims=True)
        scale = lax.rsqrt(jnp.mean(centred * centred, axis=-1, keepdims=True) + norm_eps)
        unit = centred * scale
        scaled = grad_ref[piece, :half].astype(F32) * gain_ref[...]
        back = scale * (
            scaled
            - jnp.mean(scaled, axis=-1, keepdims=True)
            - unit * jnp.mean(scaled * unit, axis=-1, keepdims=True)
        )
        out_ref[at] = (res_ref[at] + back).astype(BF16)
    norms = grad_ref[0, half:, :PAIR].astype(F32)
    for piece in range(1, 2 * seqs):
        norms = norms + grad_ref[piece, half:, :PAIR].astype(F32)
    norm_ref[...] = norms


def first_norm_back(x, gain, grad, grad_res):
    seqs, rows, width = x.shape
    tokens = seqs * rows
    return pl.pallas_call(
        functools.partial(first_norm_kernel, seqs),
        grid=(1,),
        in_specs=[fixed2((tokens, width)), fixed2((width,)), fixed2(grad.shape), fixed2((tokens, width))],
        out_specs=[fixed2((tokens, width)), fixed2((8, PAIR))],
        out_shape=[jax.ShapeDtypeStruct((tokens, width), BF16), jax.ShapeDtypeStruct((8, PAIR), F32)],
        cost_estimate=pl.CostEstimate(flops=20 * tokens * width, bytes_accessed=12 * tokens * width, transcendentals=0),
        name="first_norm_back",
    )(x.reshape(tokens, width), gain, grad, grad_res)


def exchange(blocks):
    return lax.all_to_all(blocks, ("pb", "ka"), 0, 0, tiled=True)


def swap(values, axes, size, bit):
    return lax.ppermute(values, axes, [(i, i ^ bit) for i in range(size)])


def add_pair_kernel(near, batch, *refs):
    _, up_a, up_b, down_a, down_b, proj_a, proj_b, *outs = refs
    outs, down_outs = outs[:near], outs[near:]
    step = pl.program_id(0)
    part = outs[0].shape[1]

    def both(a, b):
        return (a.astype(F32) + b.astype(F32)).astype(BF16)

    @pl.when(step < batch)
    def _():
        for k in range(near):
            outs[k][...] = both(up_a[k], up_b[k])

    for far in range(batch):

        @pl.when(step == batch + far)
        def _():
            for k in range(near):
                total = both(down_a[k], down_b[k])
                slab = total.shape[0] * total.shape[1]
                down_outs[far][k * slab : (k + 1) * slab] = total.reshape(slab, part)

    @pl.when(step == 2 * batch)
    def _():
        for k in range(near):
            total = both(proj_a[k], proj_b[k])
            outs[k][...] = jnp.concatenate([total[:, :part], total[:, part:]], axis=0)


def add_pair(mine, up, down, proj, batch):
    near, width, part = up[0].shape
    plane, block = down[0].shape[1:3]
    tall, few = width // batch, plane // batch
    up_spec = pl.BlockSpec((near, tall, part), lambda i, m: (0, jnp.minimum(i, batch - 1), 0))
    down_spec = pl.BlockSpec(
        (near, few, block, part), lambda i, m: (0, m[0] ^ jnp.clip(i - batch, 0, batch - 1), 0, 0)
    )
    proj_spec = pl.BlockSpec((near, block, width), lambda i, m: (0, 0, 0))
    last = lambda i, m: (jnp.where(i < batch, i, jnp.where(i < 2 * batch, batch - 1, batch)), 0)
    down_shape = (near * few * block, part)
    return pl.pallas_call(
        functools.partial(add_pair_kernel, near, batch),
        grid_spec=pltpu.PrefetchScalarGridSpec(
            num_scalar_prefetch=1,
            grid=(2 * batch + 1,),
            in_specs=[up_spec] * 2 + [down_spec] * 2 + [proj_spec] * 2,
            out_specs=[pl.BlockSpec((tall, part), last)] * near
            + [pl.BlockSpec(down_shape, lambda i, m: (0, 0))] * batch,
        ),
        out_shape=[jax.ShapeDtypeStruct((width + tall, part), BF16)] * near
        + [jax.ShapeDtypeStruct(down_shape, BF16)] * batch,
        cost_estimate=pl.CostEstimate(
            flops=near * 9 * tall * part, bytes_accessed=6 * near * 9 * tall * part, transcendentals=0
        ),
        name="add_pair",
    )(mine, *up, *down, *proj)


def add_all(parts):
    total = parts[0].astype(F32)
    for p in parts[1:]:
        total = total + p.astype(F32)
    return total


def over_batch(stacked):
    size = lax.axis_size("batch")
    mine = lax.axis_index("batch")
    if size > 4:
        return lax.psum_scatter(stacked, "batch", scatter_dimension=0, tiled=True)[0].astype(F32)
    parts = [lax.dynamic_index_in_dim(stacked, mine, 0, False)]
    for bit in range(1, size):
        block = lax.dynamic_index_in_dim(stacked, mine ^ bit, 0, False)
        parts.append(swap(block, "batch", size, bit))
    return add_all(parts)


def over_plane(tiles, plane):
    parts = [tiles[0]]
    for k in range(1, len(tiles)):
        parts.append(swap(tiles[k], ("pb", "ka"), plane, 2 * k))
    return add_all(parts)


def shards(
    inputs,
    block_place,
    ln1_gain,
    ln1_shift,
    w_qkv,
    w_out,
    ln2_gain,
    ln2_shift,
    w_up,
    w_down,
    cotangent,
):
    seqs, rows, width = inputs.shape
    hidden = w_up.shape[1]
    plane = lax.axis_size("pb") * lax.axis_size("ka")
    planes = ("pb", "ka")
    batch = lax.axis_size("batch")
    near = plane // 2
    few = batch <= 4
    me = lax.axis_index(planes)
    scalar = lambda value: value.astype(jnp.int32).reshape(1)
    core, chip = scalar(me & 1), scalar(me >> 1)
    part, block, slab = hidden // plane, width // plane, width // batch
    place = lax.dynamic_index_in_dim(block_place, me >> 1, 0, False)
    spots = jnp.arange(plane, dtype=jnp.int32)
    back = jnp.sum(jnp.where(place[None] == spots[:, None], spots[None], 0), axis=1)
    to, found = [jnp.where(core == 0, *(jnp.array(t, jnp.int32) for t in both)) for both in strips(width, plane)]

    mine = exchange(inputs.reshape(plane, seqs * rows // plane, width))
    other = swap(mine, planes, plane, 1)
    attended, normed1, packed, sums, stats = attend(core, place, mine, other, ln1_gain, ln1_shift, w_qkv)
    outputs, grad_res, grad_att, norm2, *grads = feed_forward(
        scalar(me), inputs, exchange(attended), cotangent, w_out, ln2_gain, ln2_shift, w_up, w_down, plane
    )
    grad_att = exchange(grad_att)
    up, down, proj = [(grads[2 * i + 1], swap(grads[2 * i], planes, plane, 1)) for i in range(3)]
    if few:
        sums_up = add_pair(scalar(lax.axis_index("batch")), up, down, proj, batch)
        grad_att, sums_up = lax.optimization_barrier((grad_att, sums_up))
        tiles, down = sums_up[:near], sums_up[near:]
    else:
        tiles = [
            jnp.concatenate(
                [add_all([t[k] for t in up])]
                + [add_all([t[k] for t in down]).reshape(width, part)]
                + [add_all([t[k] for t in proj]).reshape(block, 2, part).transpose(1, 0, 2).reshape(2 * block, part)]
            ).astype(BF16)
            for k in range(near)
        ]
    tile = over_plane(tiles, plane).astype(BF16)
    if few:
        down_parts = [down[0]] + [swap(down[bit], "batch", batch, bit) for bit in range(1, batch)]
        down_parts = [d.reshape(near, -1, part) for d in down_parts]
        down_tiles = [add_all([d[k] for d in down_parts]).astype(BF16) for k in range(near)]

    grad_packed, grad_qkv = attend_back(core, place, to, packed, grad_att, sums, stats, normed1)
    grad_packed, tile = lax.optimization_barrier((grad_packed, tile))
    stay = grad_qkv.shape[0] // 2
    given = swap(grad_qkv[stay:], planes, plane, 1)
    keep, send, norm = normed_back(
        core, place, back, grad_packed, mine, other, norm2, w_qkv
    )
    tiles = qkv_tiles(chip, found, grad_qkv[:stay], given, near)
    returned = exchange(merge(keep, swap(send, planes, plane, 1), norm))
    if few:
        returned, down_tiles = lax.optimization_barrier((returned, down_tiles))
    grad_inputs, norm = first_norm_back(inputs, ln1_gain, returned, grad_res)

    if few:
        grad_down = over_plane(down_tiles, plane)
    else:
        cut = batch // plane
        down_tile = tile[width : 2 * width].reshape(plane, block, cut, part // cut).transpose(0, 2, 1, 3)
        grad_down = over_batch(down_tile.reshape(batch, block, part // cut))
    proj_tile = tile[-2 * block :].reshape(2, block, part).transpose(1, 0, 2).reshape(block, batch, slab)
    proj_tile = proj_tile.transpose(1, 0, 2)
    up_tile = tile[:width].reshape(batch, slab, part)
    if few:
        joined = jnp.concatenate([up_tile, proj_tile.reshape(batch, block * slab // part, part)], axis=1)
        summed = over_batch(joined)
        grad_up, grad_proj = summed[:slab], summed[slab:].reshape(block, slab)
    else:
        grad_up, grad_proj = over_batch(up_tile), over_batch(proj_tile)
    grad_down = grad_down.reshape(-1, block, min(part, hidden // batch)).transpose(0, 2, 1).reshape(-1, block)
    grad_proj = grad_proj.T

    owned = 3 * width // plane
    tile = over_plane(tiles, plane).astype(BF16)
    qkv_tile = tile.reshape(owned, batch, slab).transpose(1, 0, 2)
    if few:
        norm_tile = jnp.pad(norm.astype(BF16), ((0, 8), (0, slab - PAIR)))
        norm_tile = jnp.broadcast_to(norm_tile[None], (batch, *norm_tile.shape))
        summed = over_batch(jnp.concatenate([qkv_tile, norm_tile], axis=1))
        grad_qkv, norms = summed[:owned], summed[owned:]
    else:
        grad_qkv, norms = over_batch(qkv_tile), lax.psum(norm, "batch")
    return (
        outputs.reshape(inputs.shape),
        grad_inputs.reshape(inputs.shape),
        grad_qkv.T,
        grad_proj,
        grad_up,
        grad_down,
        norms[:4, :block],
    )


def solution(mesh):
    placed = (
        P("batch", ("pb", "ka"), None),
        P("batch", None),
        P(),
        P(),
        P(),
        P(),
        P(),
        P(),
        P(),
        P(),
        P("batch", ("pb", "ka"), None),
    )
    return jax.shard_map(
        shards,
        mesh=mesh,
        in_specs=placed,
        out_specs=(
            P("batch", ("pb", "ka"), None),
            P("batch", ("pb", "ka"), None),
            P("batch", ("pb", "ka")),
            P("batch", ("pb", "ka")),
            P("batch", ("pb", "ka")),
            P("batch", ("pb", "ka")),
            P(None, ("pb", "ka")),
        ),
        check_vma=False,
    )
```

profile of v0, /device:TPU:0, one launch (start us, length us, event | category | flops | bytes accessed | tf_op | source)
XLA Modules:
  0.0 251.1 jit_solution(12350698195244742245)
XLA Ops:
  0.6 17.0 %all_to_all.20.mine_ref = bf16[8,64,768]{2,1,0:T(8,128)(2,1)S(1)} all-to-all(bf16[8,64,768]{2,1,0:T(8,128)(2,1)} %bitcast.55), channel_id=1, replica_groups=mesh['batch'=4,'pb'=2,'ka'=4] {'pb','ka'}, dimensions={0} | all-to-all | bytes 1572864 | tf_op jit(solution)/shard_map/all_to_all | solution.py:592
  17.6 0.6 fusion.20.place_ref
  18.2 1.7 collective-permute-done.other_ref
  19.9 0.9 copy-done.5
  20.8 21.8 %attend.1 = (bf16[8,128,384]{2,1,0:T(8,128)(2,1)}, bf16[1024,768]{1,0:T(8,128)(2,1)}, bf16[3,1024,384]{2,1,0:T(8,128)(2,1)}, f32[3,128,1024]{2,1,0:T(8,128)}, f32[3,8,1024]{2,1,0:T(8,128)}) custom-call(s32[1]{0:T(128)} %bitcast.2.core_ref, s32[8]{0:T(128)} %fusion.20.place_ref, bf16[8,64,768]{2,1,0:T(8,128)(2,1)} %copy-done.3, ...), custom_call_target="tpu_custom_call" | custom-call | flops 5033164800 | bytes 6291456 | tf_op jit(solution)/shard_map/attend/pallas_call | solution.py:111
  42.7 16.0 %all_to_all.21.refs_2_ = bf16[8,128,384]{2,1,0:T(8,128)(2,1)} all-to-all(bf16[8,128,384]{2,1,0:T(8,128)(2,1)} %get-tuple-element.57), channel_id=1, replica_groups=mesh['batch'=4,'pb'=2,'ka'=4] {'pb','ka'}, dimensions={0} | all-to-all | bytes 1572864 | tf_op jit(solution)/shard_map/all_to_all | solution.py:592
  58.6 31.6 %feed_forward.1 = (bf16[512,768]{1,0:T(8,128)(2,1)}, f32[512,768]{1,0:T(8,128)}, bf16[8,128,384]{2,1,0:T(8,128)(2,1)}, f32[8,768]{1,0:T(8,128)}, bf16[4,768,384]...) custom-call(s32[1]{0:T(128)} %bitcast.refs_0_, ...), custom_call_target="tpu_custom_call" | custom-call | flops 16307453952 | bytes 18874368 | tf_op jit(solution)/shard_map/feed_forward/pallas_call | solution.py:514
  90.3 0.5 collective-permute-start.2
  90.8 3.7 %all-to-all-start.2 = ((bf16[8,128,384]{2,1,0:T(8,128)(2,1)}), bf16[8,128,384]{2,1,0:T(8,128)(2,1)S(1)}, u32[]{:S(2)}, u32[]{:S(2)}) async-start(bf16[8,128,384]{2,1,0:T(8,128)(2,1)} %get-tuple-element.60), calls=%async_computation.2 | async-start | bytes 1572864 | tf_op jit(solution)/shard_map/all_to_all | solution.py:592
  94.6 0.2 collective-permute-start.3
  94.8 0.6 select_reduce_fusion.back_ref
  95.4 0.5 broadcast_select_fusion.1.to_ref
  96.0 3.6 %collective-permute-done.3.refs_6_ = bf16[4,96,768]{2,1,0:T(8,128)(2,1)} collective-permute-done((bf16[4,96,768]{2,1,0:T(8,128)(2,1)}, bf16[4,96,768]{2,1,0:T(8,128)(2,1)}, u32[]{:S(2)}, u32[]{:S(2)}) %collective-permute-start.3) | collective-permute-done | bytes 589856 | tf_op jit(solution)/shard_map/ppermute | solution.py:596
  99.6 1.4 copy-done.4
  101.0 9.7 %add_pair.1 = (bf16[960,384]{1,0:T(8,128)(2,1)}, bf16[960,384]{1,0:T(8,128)(2,1)}, bf16[960,384]{1,0:T(8,128)(2,1)}, bf16[960,384]{1,0:T(8,128)(2,1)}, bf16[768,...) custom-call(s32[1]{0:T(128)} %bitcast.8.refs_0_, ...), custom_call_target="tpu_custom_call" | custom-call | flops 2654208 | bytes 15925248 | tf_op jit(solution)/shard_map/add_pair/pallas_call | solution.py:640
  110.7 1.5 collective-permute-start.4
  112.2 0.5 collective-permute-start.5
  112.8 1.5 collective-permute-start.6
  114.3 18.5 %attend_back.1 = (bf16[1024,1152]{1,0:T(8,128)(2,1)}, bf16[1152,768]{1,0:T(8,128)(2,1)}) custom-call(s32[1]{0:T(128)} %bitcast.2.core_ref, s32[8]{0:T(128)} %fusion.20.place_ref, s32[36]{0:T(128)} %broadcast_select_fusion.1.to_ref, bf16[3,1024,384]{2,1,0:T(8,128)(2,1)} %get-tuple-element.59.qkv_ref, bf16[8,128,384]{2,1,0:T(8,128)(2,1)} %copy-done.6, ...), custom_call_target="tpu_custom_call" | custom-call | flops 9865003008 | bytes 6291456 | tf_op jit(solution)/shard_map/attend_back/pallas_call | solution.py:193
  132.9 0.8 copy-done.9
  133.7 12.9 %collective-permute-done.6 = bf16[960,384]{1,0:T(8,128)(2,1)} collective-permute-done((bf16[960,384]{1,0:T(8,128)(2,1)}, bf16[960,384]{1,0:T(8,128)(2,1)}, u32[]{:S(2)}, u32[]{:S(2)}) %collective-permute-start.6) | collective-permute-done | bytes 737312 | tf_op jit(solution)/shard_map/ppermute | solution.py:596
  146.6 1.9 add_convert_fusion
  148.6 8.1 %normed_back.1 = (f32[8,64,768]{2,1,0:T(8,128)}, bf16[8,64,768]{2,1,0:T(8,128)(2,1)}, f32[8,768]{1,0:T(8,128)}) custom-call(s32[1]{0:T(128)} %bitcast.2.core_ref, s32[8]{0:T(128)} %fusion.20.place_ref, s32[8]{0:T(128)} %select_reduce_fusion.back_ref, bf16[1024,1152]{1,0:T(8,128)(2,1)} %get-tuple-element.84.grad_ref, bf16[8,64,768]{2,1,0:T(8,128)(2,1)} %copy-done.3, ...), custom_call_target="tpu_custom_call" | custom-call | flops 1811939328 | bytes 6291456 | tf_op jit(solution)/shard_map/normed_back/pallas_call | solution.py:265
  156.7 2.5 fusion.21
  159.2 0.5 collective-permute-start.11
  159.7 3.6 %collective-permute-start.10 = (bf16[768,384]{1,0:T(8,128)(2,1)}, bf16[768,384]{1,0:T(8,128)(2,1)}, u32[]{:S(2)}, u32[]{:S(2)}) collective-permute-start(bf16[768,384]{1,0:T(8,128)(2,1)} %get-tuple-element.92), channel_id=1, source_target_pairs={{0,24},{8,16},{16,8},{24,0},{1,25},{9,17},{17,9},{25,1},{2,26},{10... | collective-permute-start | bytes 1769480 | tf_op jit(solution)/shard_map/ppermute | solution.py:596
  163.3 0.8 collective-permute-start.9
  164.1 0.9 copy-done.7
  165.0 2.8 %merge.1 = bf16[8,72,768]{2,1,0:T(8,128)(2,1)} custom-call(f32[8,64,768]{2,1,0:T(8,128)} %get-tuple-element.86.keep_ref, bf16[8,64,768]{2,1,0:T(8,128)(2,1)} %copy-done.7, f32[8,768]{1,0:T(8,128)} %get-tuple-element.88.norm_ref), custom_call_target="tpu_custom_call" | custom-call | flops 393216 | bytes 3145728 | tf_op jit(solution)/shard_map/merge/pallas_call | solution.py:304
  167.8 3.9 %all-to-all-start.3 = ((bf16[8,72,768]{2,1,0:T(8,128)(2,1)}), bf16[8,72,768]{2,1,0:T(8,128)(2,1)S(1)}, u32[]{:S(2)}, u32[]{:S(2)}) async-start(bf16[8,72,768]{2,1,0:T(8,128)(2,1)} %merge.1), calls=%async_computation.3 | async-start | bytes 1769472 | tf_op jit(solution)/shard_map/all_to_all | solution.py:592
  171.7 0.5 broadcast_select_fusion.found_ref
  172.2 3.7 %qkv_tiles.1 = (bf16[288,768]{1,0:T(8,128)(2,1)}, bf16[288,768]{1,0:T(8,128)(2,1)}, bf16[288,768]{1,0:T(8,128)(2,1)}, bf16[288,768]{1,0:T(8,128)(2,1)}) custom-call(s32[1]{0:T(128)} %bitcast.10.chip_ref, s32[36]{0:T(128)} %broadcast_select_fusion.found_ref, bf16[576,768]{1,0:T(8,128)(2,1)} %get-tuple-element.140.keep_ref, ...), custom_call_target="tpu_custom_call" | custom-call | flops 442368 | bytes 3538944 | tf_op jit(solution)/shard_map/qkv_tiles/pallas_call | solution.py:370
  175.9 1.7 collective-permute-start.12
  177.6 1.5 collective-permute-start.13
  179.1 0.4 collective-permute-start.14
  179.5 11.3 %collective-permute-done.8 = bf16[768,384]{1,0:T(8,128)(2,1)} collective-permute-done((bf16[768,384]{1,0:T(8,128)(2,1)}, bf16[768,384]{1,0:T(8,128)(2,1)}, u32[]{:S(2)}, u32[]{:S(2)}) %collective-permute-start.8) | collective-permute-done | bytes 589856 | tf_op jit(solution)/shard_map/ppermute | solution.py:596
  190.8 23.4 %collective-permute-done.9 = bf16[768,384]{1,0:T(8,128)(2,1)} collective-permute-done((bf16[768,384]{1,0:T(8,128)(2,1)}, bf16[768,384]{1,0:T(8,128)(2,1)}, u32[]{:S(2)}, u32[]{:S(2)}) %collective-permute-start.9) | collective-permute-done | bytes 589856 | tf_op jit(solution)/shard_map/ppermute | solution.py:596
  214.2 2.5 %add_convert_fusion.2 = (bf16[192,384]{1,0:T(8,128)(2,1)S(1)}, bf16[192,384]{1,0:T(8,128)(2,1)}, bf16[192,384]{1,0:T(8,128)(2,1)}, bf16[192,384]{1,0:T(8,128)(2,1)S(1)}) fusion(bf16[768,384]{1,0:T(8,128)(2,1)} %collective-permute-done.10, bf16[768,384]{1,0:T(8,128)(2,1)} %collective-permute-done.9, bf16[768,384]{1,0:T(8,128)(2,1)} %collective-permute-done.8, ...), kind=kLoop, calls=%fused_computation.27 | loop fusion | flops 2359296 | bytes 2949120 | tf_op jit(solution)/shard_map/convert_element_type | solution.py:738
  216.9 0.1 copy.47
  217.0 0.2 reshape.119
  217.2 0.2 reshape.120
  217.4 0.8 fusion.9
  218.2 3.0 %collective-permute-start.19 = (bf16[240,384]{1,0:T(8,128)(2,1)}, bf16[240,384]{1,0:T(8,128)(2,1)}, u32[]{:S(2)}, u32[]{:S(2)}) collective-permute-start(bf16[240,384]{1,0:T(8,128)(2,1)} %get-tuple-element.142), channel_id=1, source_target_pairs={{0,16},{8,24},{16,0},{24,8},{1,17},{9,25},{17,1},{25,9},{2,18},{10... | collective-permute-start | bytes 552968 | tf_op jit(solution)/shard_map/ppermute | solution.py:596
  221.2 1.3 collective-permute-start.20
  222.6 1.5 add_convert_fusion.1
  224.1 0.5 reshape.116
  224.7 0.9 copy-done.2
  225.7 3.8 %first_norm_back.1 = (bf16[512,768]{1,0:T(8,128)(2,1)}, f32[8,128]{1,0:T(8,128)}) custom-call(bf16[512,768]{1,0:T(8,128)(2,1)} %bitcast.57, f32[768]{0:T(1024)} %gain_ref.3, bf16[8,72,768]{2,1,0:T(8,128)(2,1)} %copy-done.2, f32[512,768]{1,0:T(8,128)} %get-tuple-element.94.res_ref), custom_call_target="tpu_custom_call" | custom-call | flops 7864320 | bytes 4718592 | tf_op jit(solution)/shard_map/first_norm_back/pallas_call | solution.py:580
  229.5 0.7 convert_element_type.167
  230.4 3.0 %collective-permute-start.16 = (bf16[304,192]{1,0:T(8,128)(2,1)S(1)}, bf16[304,192]{1,0:T(8,128)(2,1)S(1)}, u32[]{:S(2)}, u32[]{:S(2)}) collective-permute-start(bf16[304,192]{1,0:T(8,128)(2,1)S(1)} %get-tuple-element.145), channel_id=1, source_target_pairs={{0,16},{8,24},{16,0},{24,8},{1,17},{9,25},{17,1},{25,9},{2,18},{10... | collective-permute-start | bytes 350216 | tf_op jit(solution)/shard_map/ppermute | solution.py:596
  233.4 1.3 collective-permute-start.17
  234.7 0.5 collective-permute-done.19
  235.3 1.2 fusion.1
  236.4 0.7 slice.128
  237.2 0.1 reshape.121
  237.3 0.7 copy.40
  238.0 1.4 collective-permute-start.21
  239.4 0.6 collective-permute-start.22
  240.0 1.5 collective-permute-start.23
  241.5 7.2 %collective-permute-done.16 = bf16[304,192]{1,0:T(8,128)(2,1)S(1)} collective-permute-done((bf16[304,192]{1,0:T(8,128)(2,1)S(1)}, bf16[304,192]{1,0:T(8,128)(2,1)S(1)}, u32[]{:S(2)}, u32[]{:S(2)}) %collective-permute-start.16) | collective-permute-done | bytes 116768 | tf_op jit(solution)/shard_map/ppermute | solution.py:596
  248.7 0.1 fusion.3
  248.8 0.6 slice.129
  249.4 0.9 copy.42
  250.3 0.7 copy.43
  (66 shorter events, 0.6 us)
Async XLA Ops:
  0.6 17.0 %copy-start = (s32[4,8]{1,0:T(4,128)S(1)}, s32[4,8]{1,0:T(4,128)}, u32[]{:S(2)}) copy-start(s32[4,8]{1,0:T(4,128)} %param.16) | copy-start | bytes 388
  17.6 2.3 copy-start.3
  17.6 2.3 collective-permute-start
  19.9 0.9 copy-start.5
  58.6 36.2 %copy-start.13 = (s32[8]{0:T(128)S(1)}, s32[8]{0:T(128)}, u32[]{:S(2)}) copy-start(s32[8]{0:T(128)} %fusion.20.place_ref) | copy-start | bytes 100
  58.6 36.8 %copy-start.16 = (s32[36]{0:T(128)S(1)}, s32[36]{0:T(128)}, u32[]{:S(2)}) copy-start(s32[36]{0:T(128)} %constant.58.clone) | copy-start | bytes 436
  58.6 36.8 %copy-start.17 = (s32[36]{0:T(128)S(1)}, s32[36]{0:T(128)}, u32[]{:S(2)}) copy-start(s32[36]{0:T(128)} %constant.59.clone) | copy-start | bytes 436
  90.3 9.3 %collective-permute-start.1 = (bf16[4,768,384]{2,1,0:T(8,128)(2,1)}, bf16[4,768,384]{2,1,0:T(8,128)(2,1)S(1)}, u32[]{:S(2)}, u32[]{:S(2)}) collective-permute-start(bf16[4,768,384]{2,1,0:T(8,128)(2,1)} %get-tuple-element.62), channel_id=1, source_target_pairs={{0,1},{1,0},{2,3},{3,2},{4,5},{5,4},{6,7},{7,6},{8,9},{9,8},{10,11... | collective-permute-start | bytes 7077896 | tf_op jit(solution)/shard_map/ppermute | solution.py:596
  90.3 9.2 %collective-permute-start.2 = (bf16[4,8,96,384]{3,2,1,0:T(8,128)(2,1)}, bf16[4,8,96,384]{3,2,1,0:T(8,128)(2,1)}, u32[]{:S(2)}, u32[]{:S(2)}) collective-permute-start(bf16[4,8,96,384]{3,2,1,0:T(8,128)(2,1)} %get-tuple-element.64), channel_id=1, source_target_pairs={{0,1},{1,0},{2,3},{3,2},{4,5},{5,4},{6,7},{7,6},{8,9},{9,8},{10,11... | collective-permute-start | bytes 7077896 | tf_op jit(solution)/shard_map/ppermute | solution.py:596
  90.8 19.9 %all-to-all-start.2 = ((bf16[8,128,384]{2,1,0:T(8,128)(2,1)}), bf16[8,128,384]{2,1,0:T(8,128)(2,1)S(1)}, u32[]{:S(2)}, u32[]{:S(2)}) async-start(bf16[8,128,384]{2,1,0:T(8,128)(2,1)} %get-tuple-element.60), calls=%async_computation.2 | async-start | bytes 1572864 | tf_op jit(solution)/shard_map/all_to_all | solution.py:592
  94.6 5.0 %collective-permute-start.3 = (bf16[4,96,768]{2,1,0:T(8,128)(2,1)}, bf16[4,96,768]{2,1,0:T(8,128)(2,1)}, u32[]{:S(2)}, u32[]{:S(2)}) collective-permute-start(bf16[4,96,768]{2,1,0:T(8,128)(2,1)} %get-tuple-element.66), channel_id=1, source_target_pairs={{0,1},{1,0},{2,3},{3,2},{4,5},{5,4},{6,7},{7,6},{8,9},{9,8},{10,11... | collective-permute-start | bytes 1769480 | tf_op jit(solution)/shard_map/ppermute | solution.py:596
  99.6 1.5 copy-start.4
  110.7 3.6 %copy-start.6 = (bf16[8,128,384]{2,1,0:T(8,128)(2,1)}, bf16[8,128,384]{2,1,0:T(8,128)(2,1)S(1)}, u32[]{:S(2)}) copy-start(bf16[8,128,384]{2,1,0:T(8,128)(2,1)S(1)} %all-to-all-done.2.g_ref) | copy-start | bytes 2359300
  110.7 22.1 %collective-permute-start.4 = (bf16[960,384]{1,0:T(8,128)(2,1)}, bf16[960,384]{1,0:T(8,128)(2,1)}, u32[]{:S(2)}, u32[]{:S(2)}) collective-permute-start(bf16[960,384]{1,0:T(8,128)(2,1)} %get-tuple-element.81), channel_id=1, source_target_pairs={{0,2},{1,3},{2,0},{3,1},{4,6},{5,7},{6,4},{7,5},{8,10},{9,11},{10,... | collective-permute-start | bytes 2211848 | tf_op jit(solution)/shard_map/ppermute | solution.py:596
  112.2 20.6 %collective-permute-start.5 = (bf16[960,384]{1,0:T(8,128)(2,1)}, bf16[960,384]{1,0:T(8,128)(2,1)S(1)}, u32[]{:S(2)}, u32[]{:S(2)}) collective-permute-start(bf16[960,384]{1,0:T(8,128)(2,1)} %get-tuple-element.82), channel_id=1, source_target_pairs={{0,4},{1,5},{2,6},{3,7},{4,0},{5,1},{6,2},{7,3},{8,12},{9,13},{10,... | collective-permute-start | bytes 2211848 | tf_op jit(solution)/shard_map/ppermute | solution.py:596
  112.8 33.8 %collective-permute-start.6 = (bf16[960,384]{1,0:T(8,128)(2,1)}, bf16[960,384]{1,0:T(8,128)(2,1)}, u32[]{:S(2)}, u32[]{:S(2)}) collective-permute-start(bf16[960,384]{1,0:T(8,128)(2,1)} %get-tuple-element.83), channel_id=1, source_target_pairs={{0,6},{1,7},{2,4},{3,5},{4,2},{5,3},{6,0},{7,1},{8,14},{9,15},{10,... | collective-permute-start | bytes 2211848 | tf_op jit(solution)/shard_map/ppermute | solution.py:596
  114.3 32.3 %copy-start.8 = (bf16[960,384]{1,0:T(8,128)(2,1)S(1)}, bf16[960,384]{1,0:T(8,128)(2,1)}, u32[]{:S(2)}) copy-start(bf16[960,384]{1,0:T(8,128)(2,1)} %get-tuple-element.80) | copy-start | bytes 2211844
  132.9 0.9 copy-start.9
  156.7 7.4 %collective-permute-start.7 = (bf16[8,64,768]{2,1,0:T(8,128)(2,1)}, bf16[8,64,768]{2,1,0:T(8,128)(2,1)S(1)}, u32[]{:S(2)}, u32[]{:S(2)}) collective-permute-start(bf16[8,64,768]{2,1,0:T(8,128)(2,1)} %get-tuple-element.87), channel_id=1, source_target_pairs={{0,1},{1,0},{2,3},{3,2},{4,5},{5,4},{6,7},{7,6},{8,9},{9,8},{10,11... | collective-permute-start | bytes 2359304 | tf_op jit(solution)/shard_map/ppermute | solution.py:596
  159.2 13.0 %collective-permute-start.11 = (bf16[576,768]{1,0:T(8,128)(2,1)S(1)}, bf16[576,768]{1,0:T(8,128)(2,1)}, u32[]{:S(2)}, u32[]{:S(2)}) collective-permute-start(bf16[576,768]{1,0:T(8,128)(2,1)S(1)} %get-tuple-element.139), channel_id=1, source_target_pairs={{0,1},{1,0},{2,3},{3,2},{4,5},{5,4},{6,7},{7,6},{8,9},{9,8},{10,11... | collective-permute-start | bytes 2654216 | tf_op jit(solution)/shard_map/ppermute | solution.py:596
  159.7 19.4 %collective-permute-start.10 = (bf16[768,384]{1,0:T(8,128)(2,1)}, bf16[768,384]{1,0:T(8,128)(2,1)}, u32[]{:S(2)}, u32[]{:S(2)}) collective-permute-start(bf16[768,384]{1,0:T(8,128)(2,1)} %get-tuple-element.92), channel_id=1, source_target_pairs={{0,24},{8,16},{16,8},{24,0},{1,25},{9,17},{17,9},{25,1},{2,26},{10... | collective-permute-start | bytes 1769480 | tf_op jit(solution)/shard_map/ppermute | solution.py:596
  163.3 27.5 %collective-permute-start.8 = (bf16[768,384]{1,0:T(8,128)(2,1)}, bf16[768,384]{1,0:T(8,128)(2,1)}, u32[]{:S(2)}, u32[]{:S(2)}) collective-permute-start(bf16[768,384]{1,0:T(8,128)(2,1)} %get-tuple-element.90), channel_id=1, source_target_pairs={{0,8},{8,0},{16,24},{24,16},{1,9},{9,1},{17,25},{25,17},{2,10},{10... | collective-permute-start | bytes 1769480 | tf_op jit(solution)/shard_map/ppermute | solution.py:596
  163.3 50.9 %collective-permute-start.9 = (bf16[768,384]{1,0:T(8,128)(2,1)}, bf16[768,384]{1,0:T(8,128)(2,1)}, u32[]{:S(2)}, u32[]{:S(2)}) collective-permute-start(bf16[768,384]{1,0:T(8,128)(2,1)} %get-tuple-element.91), channel_id=1, source_target_pairs={{0,16},{8,24},{16,0},{24,8},{1,17},{9,25},{17,1},{25,9},{2,18},{10... | collective-permute-start | bytes 1769480 | tf_op jit(solution)/shard_map/ppermute | solution.py:596
  164.1 0.9 copy-start.7
  165.0 6.7 %copy-start.14 = (s32[36]{0:T(128)S(1)}, s32[36]{0:T(128)}, u32[]{:S(2)}) copy-start(s32[36]{0:T(128)} %constant.60.clone) | copy-start | bytes 436
  165.0 6.7 %copy-start.15 = (s32[36]{0:T(128)S(1)}, s32[36]{0:T(128)}, u32[]{:S(2)}) copy-start(s32[36]{0:T(128)} %constant.61.clone) | copy-start | bytes 436
  167.8 46.5 %copy-start.10 = (bf16[768,384]{1,0:T(8,128)(2,1)S(1)}, bf16[768,384]{1,0:T(8,128)(2,1)}, u32[]{:S(2)}) copy-start(bf16[768,384]{1,0:T(8,128)(2,1)} %get-tuple-element.89) | copy-start | bytes 1769476
  167.8 57.0 %all-to-all-start.3 = ((bf16[8,72,768]{2,1,0:T(8,128)(2,1)}), bf16[8,72,768]{2,1,0:T(8,128)(2,1)S(1)}, u32[]{:S(2)}, u32[]{:S(2)}) async-start(bf16[8,72,768]{2,1,0:T(8,128)(2,1)} %merge.1), calls=%async_computation.3 | async-start | bytes 1769472 | tf_op jit(solution)/shard_map/all_to_all | solution.py:592
  175.9 45.3 %collective-permute-start.12 = (bf16[288,768]{1,0:T(8,128)(2,1)}, bf16[288,768]{1,0:T(8,128)(2,1)}, u32[]{:S(2)}, u32[]{:S(2)}) collective-permute-start(bf16[288,768]{1,0:T(8,128)(2,1)} %get-tuple-element.98), channel_id=1, source_target_pairs={{0,2},{1,3},{2,0},{3,1},{4,6},{5,7},{6,4},{7,5},{8,10},{9,11},{10,... | collective-permute-start | bytes 1327112 | tf_op jit(solution)/shard_map/ppermute | solution.py:596
  177.6 45.0 %collective-permute-start.13 = (bf16[288,768]{1,0:T(8,128)(2,1)}, bf16[288,768]{1,0:T(8,128)(2,1)}, u32[]{:S(2)}, u32[]{:S(2)}) collective-permute-start(bf16[288,768]{1,0:T(8,128)(2,1)} %get-tuple-element.99), channel_id=1, source_target_pairs={{0,4},{1,5},{2,6},{3,7},{4,0},{5,1},{6,2},{7,3},{8,12},{9,13},{10,... | collective-permute-start | bytes 1327112 | tf_op jit(solution)/shard_map/ppermute | solution.py:596
  179.1 43.5 %collective-permute-start.14 = (bf16[288,768]{1,0:T(8,128)(2,1)}, bf16[288,768]{1,0:T(8,128)(2,1)}, u32[]{:S(2)}, u32[]{:S(2)}) collective-permute-start(bf16[288,768]{1,0:T(8,128)(2,1)} %get-tuple-element.100), channel_id=1, source_target_pairs={{0,6},{1,7},{2,4},{3,5},{4,2},{5,3},{6,0},{7,1},{8,14},{9,15},{10,... | collective-permute-start | bytes 1327112 | tf_op jit(solution)/shard_map/ppermute | solution.py:596
  216.8 5.8 %copy-start.11 = (bf16[288,768]{1,0:T(8,128)(2,1)S(1)}, bf16[288,768]{1,0:T(8,128)(2,1)}, u32[]{:S(2)}) copy-start(bf16[288,768]{1,0:T(8,128)(2,1)} %get-tuple-element.97) | copy-start | bytes 1327108
  218.2 15.2 %collective-permute-start.18 = (bf16[240,384]{1,0:T(8,128)(2,1)}, bf16[240,384]{1,0:T(8,128)(2,1)}, u32[]{:S(2)}, u32[]{:S(2)}) collective-permute-start(bf16[240,384]{1,0:T(8,128)(2,1)} %get-tuple-element.141), channel_id=1, source_target_pairs={{0,8},{8,0},{16,24},{24,16},{1,9},{9,1},{17,25},{25,17},{2,10},{10... | collective-permute-start | bytes 552968 | tf_op jit(solution)/shard_map/ppermute | solution.py:596
  218.2 17.1 %collective-permute-start.19 = (bf16[240,384]{1,0:T(8,128)(2,1)}, bf16[240,384]{1,0:T(8,128)(2,1)}, u32[]{:S(2)}, u32[]{:S(2)}) collective-permute-start(bf16[240,384]{1,0:T(8,128)(2,1)} %get-tuple-element.142), channel_id=1, source_target_pairs={{0,16},{8,24},{16,0},{24,8},{1,17},{9,25},{17,1},{25,9},{2,18},{10... | collective-permute-start | bytes 552968 | tf_op jit(solution)/shard_map/ppermute | solution.py:596
  221.2 14.0 %collective-permute-start.20 = (bf16[240,384]{1,0:T(8,128)(2,1)}, bf16[240,384]{1,0:T(8,128)(2,1)}, u32[]{:S(2)}, u32[]{:S(2)}) collective-permute-start(bf16[240,384]{1,0:T(8,128)(2,1)} %get-tuple-element.143), channel_id=1, source_target_pairs={{0,24},{8,16},{16,8},{24,0},{1,25},{9,17},{17,9},{25,1},{2,26},{10... | collective-permute-start | bytes 552968 | tf_op jit(solution)/shard_map/ppermute | solution.py:596
  224.7 0.9 copy-start.2
  230.2 9.3 %copy-start.12 = (bf16[192,384]{1,0:T(8,128)(2,1)S(1)}, bf16[192,384]{1,0:T(8,128)(2,1)}, u32[]{:S(2)}) copy-start(bf16[192,384]{1,0:T(8,128)(2,1)} %get-tuple-element.105) | copy-start | bytes 442372
  230.3 9.7 %collective-permute-start.15 = (bf16[304,192]{1,0:T(8,128)(2,1)S(1)}, bf16[304,192]{1,0:T(8,128)(2,1)S(1)}, u32[]{:S(2)}, u32[]{:S(2)}) collective-permute-start(bf16[304,192]{1,0:T(8,128)(2,1)S(1)} %get-tuple-element.144), channel_id=1, source_target_pairs={{0,8},{8,0},{16,24},{24,16},{1,9},{9,1},{17,25},{25,17},{2,10},{10... | collective-permute-start | bytes 350216 | tf_op jit(solution)/shard_map/ppermute | solution.py:596
  230.4 18.3 %collective-permute-start.16 = (bf16[304,192]{1,0:T(8,128)(2,1)S(1)}, bf16[304,192]{1,0:T(8,128)(2,1)S(1)}, u32[]{:S(2)}, u32[]{:S(2)}) collective-permute-start(bf16[304,192]{1,0:T(8,128)(2,1)S(1)} %get-tuple-element.145), channel_id=1, source_target_pairs={{0,16},{8,24},{16,0},{24,8},{1,17},{9,25},{17,1},{25,9},{2,18},{10... | collective-permute-start | bytes 350216 | tf_op jit(solution)/shard_map/ppermute | solution.py:596
  233.4 15.3 %collective-permute-start.17 = (bf16[304,192]{1,0:T(8,128)(2,1)S(1)}, bf16[304,192]{1,0:T(8,128)(2,1)S(1)}, u32[]{:S(2)}, u32[]{:S(2)}) collective-permute-start(bf16[304,192]{1,0:T(8,128)(2,1)S(1)} %get-tuple-element.146), channel_id=1, source_target_pairs={{0,24},{8,16},{16,8},{24,0},{1,25},{9,17},{17,9},{25,1},{2,26},{10... | collective-permute-start | bytes 350216 | tf_op jit(solution)/shard_map/ppermute | solution.py:596
  237.3 13.8 %copy-start.1 = (s32[4,8]{1,0:T(4,128)S(1)}, s32[4,8]{1,0:T(4,128)}, u32[]{:S(2)}) copy-start(s32[4,8]{1,0:T(4,128)} %param.16) | copy-start | bytes 388
  238.0 12.2 %collective-permute-start.21 = (bf16[192,384]{1,0:T(8,128)(2,1)}, bf16[192,384]{1,0:T(8,128)(2,1)S(1)}, u32[]{:S(2)}, u32[]{:S(2)}) collective-permute-start(bf16[192,384]{1,0:T(8,128)(2,1)} %get-tuple-element.104), channel_id=1, source_target_pairs={{0,2},{1,3},{2,0},{3,1},{4,6},{5,7},{6,4},{7,5},{8,10},{9,11},{10,... | collective-permute-start | bytes 442376 | tf_op jit(solution)/shard_map/ppermute | solution.py:596
  239.4 10.8 %collective-permute-start.22 = (bf16[192,384]{1,0:T(8,128)(2,1)S(1)}, bf16[192,384]{1,0:T(8,128)(2,1)S(1)}, u32[]{:S(2)}, u32[]{:S(2)}) collective-permute-start(bf16[192,384]{1,0:T(8,128)(2,1)S(1)} %copy-done.12), channel_id=1, source_target_pairs={{0,4},{1,5},{2,6},{3,7},{4,0},{5,1},{6,2},{7,3},{8,12},{9,13},{10,... | collective-permute-start | bytes 442376 | tf_op jit(solution)/shard_map/ppermute | solution.py:596
  240.0 10.2 %collective-permute-start.23 = (bf16[192,384]{1,0:T(8,128)(2,1)S(1)}, bf16[192,384]{1,0:T(8,128)(2,1)S(1)}, u32[]{:S(2)}, u32[]{:S(2)}) collective-permute-start(bf16[192,384]{1,0:T(8,128)(2,1)S(1)} %get-tuple-element.106), channel_id=1, source_target_pairs={{0,6},{1,7},{2,4},{3,5},{4,2},{5,3},{6,0},{7,1},{8,14},{9,15},{10,... | collective-permute-start | bytes 442376 | tf_op jit(solution)/shard_map/ppermute | solution.py:596
where the time goes:
time: 256 us; the launch traced here: 251 us
  Pallas kernels  100 us (39%)
  waiting for transfers between devices  60.6 us (24%)
  blocking collectives  33 us (13%)
  starting transfers between devices  32.8 us (13%)
  local copies, waits for them, and re-layouts  13.1 us (5%)
  other arithmetic  10.6 us (4%)
    ppermute x24, waiting for transfers between devices, swap(): return lax.ppermute(values, axes, [(i, i ^ bit) for i in range(size)])  60.6 us
    all_to_all x2, blocking collectives, exchange(): return lax.all_to_all(blocks, ('pb', 'ka'), 0, 0, tiled=True)  33 us
    pallas_call x1, Pallas kernels, feed_forward(): pl.pallas_call(functools.partial(ff_kernel, seqs, plane), grid_spec=pltpu...  31.6 us
    ppermute x24, starting transfers between devices, swap(): return lax.ppermute(values, axes, [(i, i ^ bit) for i in range(size)])  25.2 us
    pallas_call x1, Pallas kernels, attend(): pl.pallas_call(attend_kernel, grid_spec=pltpu.PrefetchScalarGridSpec(num_...  21.8 us
    pallas_call x1, Pallas kernels, attend_back(): pl.pallas_call(attend_back_kernel, grid_spec=pltpu.PrefetchScalarGridSpec...  18.5 us
    pallas_call x1, Pallas kernels, add_pair(): pl.pallas_call(functools.partial(add_pair_kernel, near, batch), grid_spec...  9.69 us
    pallas_call x1, Pallas kernels, normed_back(): pl.pallas_call(normed_back_kernel, grid_spec=pltpu.PrefetchScalarGridSpec...  8.13 us
  transfers between devices with their start and end apart: 26, of which 7 were waited for; matrix products, arithmetic and copies ran while one was open for 6% of the time, Pallas kernels for 15%

commit v1 on v0

--- a/solution.py
+++ b/solution.py
@@ -141,7 +141,8 @@
 
 
 def attend_back_kernel(
-    core_ref, place_ref, to_ref, qkv_ref, g_ref, sums_ref, stats_ref, normed_ref, out_ref, gq_ref, g_sc, dq_sc, dk_sc, dv_sc
+    core_ref, place_ref, to_ref, qkv_ref, g_ref, sums_ref, stats_ref, normed_ref, mine_ref, other_ref, norm_ref,
+    wq_ref, wk_ref, wv_ref, gq_ref, keep_ref, send_ref, norms_ref, g_sc, dq_sc, dk_sc, dv_sc, packed_sc, back_sc,
 ):
     blocks, rows = g_ref.shape[0], g_ref.shape[1]
     for block in range(blocks):
@@ -176,20 +177,53 @@
         dq_sc[span, :] = jnp.concatenate(parts, axis=0).T * SCALE
     for kind, ref in enumerate((dq_sc, dk_sc, dv_sc)):
         grad = ref[...].astype(BF16)
-        out_ref[:, kind * PAIR : (kind + 1) * PAIR] = grad
+        packed_sc[:, kind * PAIR : (kind + 1) * PAIR] = grad
         turned = jnp.dot(grad.T, normed_ref[...], preferred_element_type=F32).astype(BF16)
         for strip in range(PAIR // STRIP):
             at = to_ref[(pl.program_id(0) * 3 + kind) * (PAIR // STRIP) + strip]
             at = pl.multiple_of(at * STRIP, STRIP)
             gq_ref[pl.ds(at, STRIP), :] = turned[strip * STRIP : (strip + 1) * STRIP]
 
-
-def attend_back(core, place, to, qkv, grad, sums, stats, normed):
+    step, half = pl.program_id(0), mine_ref.shape[1]
+    weights = jnp.concatenate([wq_ref[...], wk_ref[...], wv_ref[...]], axis=1)
+    back = dot(packed_sc[...], weights, (1, 1))
+
+    @pl.when(step == 0)
+    def _():
+        back_sc[...] = back
+
+    @pl.when(step > 0)
+    def _():
+        back_sc[...] += back
+
+    @pl.when(step == pl.num_programs(0) - 1)
+    def _():
+        norms_ref[...] = norm_ref[...]
+
+        @pl.loop(0, blocks)
+        def _(block):
+            for ref, out_ref, part in ((mine_ref, keep_ref, core_ref[0]), (other_ref, send_ref, 1 - core_ref[0])):
+                at = pl.multiple_of(place_ref[block] * rows + part * half, half)
+                grad = back_sc[pl.ds(at, half), :]
+                out_ref[block] = grad.astype(out_ref.dtype)
+                x = ref[block].astype(F32)
+                centred = x - jnp.mean(x, axis=-1, keepdims=True)
+                unit = centred * lax.rsqrt(jnp.mean(centred * centred, axis=-1, keepdims=True) + norm_eps)
+                norms_ref[0:1, :] += jnp.sum(grad * unit, axis=0, keepdims=True)
+                norms_ref[1:2, :] += jnp.sum(grad, axis=0, keepdims=True)
+
+
+def attend_back(core, place, to, qkv, grad, sums, stats, normed, mine, other, norm, w_qkv):
     pairs, length, _ = qkv.shape
     blocks, rows, _ = grad.shape
     width = normed.shape[1]
     area = length * length
     one = lambda i, c, p, t: (i, 0, 0)
+
+    def columns(kind):
+        size = width // PAIR
+        return pl.BlockSpec((width, PAIR), lambda i, core, p, t: (0, kind * size + core[0] * pairs + i))
+
     return pl.pallas_call(
         attend_back_kernel,
         grid_spec=pltpu.PrefetchScalarGridSpec(
@@ -201,92 +235,37 @@
                 pl.BlockSpec((1, PAIR, length), one),
                 pl.BlockSpec((1, 8, length), one),
                 fixed2(normed.shape),
-            ],
-            out_specs=[
-                pl.BlockSpec((length, 3 * PAIR), lambda i, c, p, t: (0, i)),
-                fixed2((pairs * 3 * PAIR, width)),
-            ],
-            scratch_shapes=[pltpu.VMEM((length, PAIR), BF16)] + [pltpu.VMEM((length, PAIR), F32)] * 3,
-        ),
-        out_shape=[
-            jax.ShapeDtypeStruct((length, pairs * 3 * PAIR), BF16),
-            jax.ShapeDtypeStruct((pairs * 3 * PAIR, width), BF16),
-        ],
-        cost_estimate=pl.CostEstimate(
-            flops=pairs * 40 * area * HEAD + 3 * length * width * width,
-            bytes_accessed=8 * length * width,
-            transcendentals=pairs * area,
-        ),
-        name="attend_back",
-    )(core, place, to, qkv, grad, sums, stats, normed)
-
-
-def normed_back_kernel(
-    core_ref, place_ref, back_ref, grad_ref, mine_ref, other_ref, norm_ref, wq_ref, wk_ref, wv_ref,
-    keep_ref, send_ref, sums_ref, w_sc,
-):
-    step = pl.program_id(0)
-    half = mine_ref.shape[1]
-    pairs = wq_ref.shape[1] // PAIR
-
-    @pl.when(step == 0)
-    def _():
-        sums_ref[...] = norm_ref[...]
-        for pair in range(pairs):
-            for kind, ref in enumerate((wq_ref, wk_ref, wv_ref)):
-                w_sc[:, (pair * 3 + kind) * PAIR : (pair * 3 + kind + 1) * PAIR] = ref[
-                    :, pair * PAIR : (pair + 1) * PAIR
-                ]
-
-    back = dot(grad_ref[...], w_sc[...], (1, 1))
-    for at in range(grad_ref.shape[0] // (2 * half)):
-        block = back_ref[step * (grad_ref.shape[0] // (2 * half)) + at]
-        low = back[2 * at * half : (2 * at + 1) * half]
-        high = back[(2 * at + 1) * half : (2 * at + 2) * half]
-        first = core_ref[0] == 0
-        mine, other = jnp.where(first, low, high), jnp.where(first, high, low)
-        keep_ref[block] = mine
-        send_ref[block] = other.astype(BF16)
-        for grad, ref in ((mine, mine_ref), (other, other_ref)):
-            x = ref[block].astype(F32)
-            centred = x - jnp.mean(x, axis=-1, keepdims=True)
-            unit = centred * lax.rsqrt(jnp.mean(centred * centred, axis=-1, keepdims=True) + norm_eps)
-            sums_ref[0:1, :] += jnp.sum(grad * unit, axis=0, keepdims=True)
-            sums_ref[1:2, :] += jnp.sum(grad, axis=0, keepdims=True)
-
-
-def normed_back(core, place, back, grad, mine, other, norm, w_qkv):
-    length, size = grad.shape
-    blocks, half, width = mine.shape
-    steps = 4
-    columns = [
-        pl.BlockSpec((width, size // 3), lambda i, core, p, b, kind=kind: (0, kind * 2 + core[0])) for kind in range(3)
-    ]
-    return pl.pallas_call(
-        normed_back_kernel,
-        grid_spec=pltpu.PrefetchScalarGridSpec(
-            num_scalar_prefetch=3,
-            grid=(steps,),
-            in_specs=[
-                pl.BlockSpec((length // steps, size), lambda i, c, p, b: (i, 0)),
                 fixed2(mine.shape),
                 fixed2(mine.shape),
                 fixed2(norm.shape),
-                *columns,
+                *(columns(kind) for kind in range(3)),
             ],
-            out_specs=[fixed2(mine.shape), fixed2(mine.shape), fixed2(norm.shape)],
-            scratch_shapes=[pltpu.VMEM((width, size), BF16)],
+            out_specs=[
+                fixed2((pairs * 3 * PAIR, width)),
+                fixed2(mine.shape),
+                fixed2(mine.shape),
+                fixed2(norm.shape),
+            ],
+            scratch_shapes=[
+                pltpu.VMEM((length, PAIR), BF16),
+                *[pltpu.VMEM((length, PAIR), F32)] * 3,
+                pltpu.VMEM((length, 3 * PAIR), BF16),
+                pltpu.VMEM((length, width), F32),
+            ],
         ),
         out_shape=[
+            jax.ShapeDtypeStruct((pairs * 3 * PAIR, width), BF16),
             jax.ShapeDtypeStruct(mine.shape, F32),
             jax.ShapeDtypeStruct(mine.shape, BF16),
             jax.ShapeDtypeStruct(norm.shape, F32),
         ],
         cost_estimate=pl.CostEstimate(
-            flops=2 * length * width * size, bytes_accessed=8 * length * width, transcendentals=0
-        ),
-        name="normed_back",
-    )(core, place, back, grad, mine, other, norm, w_qkv, w_qkv, w_qkv)
+            flops=pairs * 40 * area * HEAD + 6 * length * width * width,
+            bytes_accessed=8 * length * width,
+            transcendentals=pairs * area,
+        ),
+        name="attend_back",
+    )(core, place, to, qkv, grad, sums, stats, normed, mine, other, norm, w_qkv, w_qkv, w_qkv)
 
 
 def merge_kernel(keep_ref, other_ref, norm_ref, out_ref):
@@ -363,8 +342,8 @@
                 )
 
 
-def qkv_tiles(chip, found, keep, given, near):
-    size, width = keep.shape
+def qkv_tiles(chip, found, grad, given, near):
+    size, width = given.shape
     owned = 2 * size // near // STRIP
     shape = (owned * STRIP, width)
     return pl.pallas_call(
@@ -372,13 +351,13 @@
         grid_spec=pltpu.PrefetchScalarGridSpec(
             num_scalar_prefetch=2,
             grid=(near,),
-            in_specs=[fixed2(keep.shape), fixed2(keep.shape)],
+            in_specs=[fixed2(given.shape), fixed2(given.shape)],
             out_specs=[fixed2(shape)] * near,
         ),
         out_shape=[jax.ShapeDtypeStruct(shape, BF16)] * near,
-        cost_estimate=pl.CostEstimate(flops=size * width, bytes_accessed=8 * size * width, transcendentals=0),
+        cost_estimate=pl.CostEstimate(flops=size * width, bytes_accessed=size * width, transcendentals=0),
         name="qkv_tiles",
-    )(chip, found, keep, given)
+    )(chip, found, grad, given)
 
 
 def gelu_pair(u):
@@ -617,7 +596,8 @@
             for k in range(near):
                 total = both(down_a[k], down_b[k])
                 slab = total.shape[0] * total.shape[1]
-                down_outs[far][k * slab : (k + 1) * slab] = total.reshape(slab, part)
+                target, at = down_outs[far in (1, 2)], (far > 1) * near * slab + k * slab
+                target[at : at + slab] = total.reshape(slab, part)
 
     @pl.when(step == 2 * batch)
     def _():
@@ -636,7 +616,7 @@
     )
     proj_spec = pl.BlockSpec((near, block, width), lambda i, m: (0, 0, 0))
     last = lambda i, m: (jnp.where(i < batch, i, jnp.where(i < 2 * batch, batch - 1, batch)), 0)
-    down_shape = (near * few * block, part)
+    down_shape = (2 * near * few * block, part)
     return pl.pallas_call(
         functools.partial(add_pair_kernel, near, batch),
         grid_spec=pltpu.PrefetchScalarGridSpec(
@@ -644,10 +624,10 @@
             grid=(2 * batch + 1,),
             in_specs=[up_spec] * 2 + [down_spec] * 2 + [proj_spec] * 2,
             out_specs=[pl.BlockSpec((tall, part), last)] * near
-            + [pl.BlockSpec(down_shape, lambda i, m: (0, 0))] * batch,
+            + [pl.BlockSpec(down_shape, lambda i, m: (0, 0))] * 2,
         ),
         out_shape=[jax.ShapeDtypeStruct((width + tall, part), BF16)] * near
-        + [jax.ShapeDtypeStruct(down_shape, BF16)] * batch,
+        + [jax.ShapeDtypeStruct(down_shape, BF16)] * 2,
         cost_estimate=pl.CostEstimate(
             flops=near * 9 * tall * part, bytes_accessed=6 * near * 9 * tall * part, transcendentals=0
         ),
@@ -700,7 +680,385 @@
     planes = ("pb", "ka")
     batch = lax.axis_size("batch")
     near = plane // 2
-    few = batch <= 4
+    few = batch == 4
+    me = lax.axis_index(planes)
+    scalar = lambda value: value.astype(jnp.int32).reshape(1)
+    core, chip = scalar(me & 1), scalar(me >> 1)
+    part, block, slab = hidden // plane, width // plane, width // batch
+    place = lax.dynamic_index_in_dim(block_place, me >> 1, 0, False)
+    to, found = [], []
+    for core in range(2):
+        order = [
+            kind * 2 * side + core * side + p * pair + strip
+            for p in range(side // pair)
+            for kind in range(3)
+            for strip in range(pair)
+        ]
+        to.append([slots[core][col][0] * stay + slots[core][col][1] for col in order])
+        row = []
+        for chip in range(near):
+            for strip in range(owned):
+                col = (2 * chip + core) * owned + strip
+                row.append(slots[core][col][1] if col in slots[core] else stay + slots[1 - core][col][1])
+        found.append(row)
+    return to, found
+
+
+def tiles_kernel(near, owned, chip_ref, found_ref, keep_ref, given_ref, *outs):
+    step = pl.program_id(0)
+    stay = keep_ref.shape[0] // STRIP
+    for k in range(near):
+
+        @pl.when(step == k)
+        def _():
+            for strip in range(owned):
+                at = found_ref[(chip_ref[0] ^ k) * owned + strip]
+                here = pl.multiple_of(jnp.minimum(at, stay - 1) * STRIP, STRIP)
+                there = pl.multiple_of(jnp.maximum(at - stay, 0) * STRIP, STRIP)
+                outs[k][strip * STRIP : (strip + 1) * STRIP, :] = jnp.where(
+                    at < stay, keep_ref[pl.ds(here, STRIP), :], given_ref[pl.ds(there, STRIP), :]
+                )
+
+
+def qkv_tiles(chip, found, grad, given, near):
+    size, width = given.shape
+    owned = 2 * size // near // STRIP
+    shape = (owned * STRIP, width)
+    return pl.pallas_call(
+        functools.partial(tiles_kernel, near, owned),
+        grid_spec=pltpu.PrefetchScalarGridSpec(
+            num_scalar_prefetch=2,
+            grid=(near,),
+            in_specs=[fixed2(given.shape), fixed2(given.shape)],
+            out_specs=[fixed2(shape)] * near,
+        ),
+        out_shape=[jax.ShapeDtypeStruct(shape, BF16)] * near,
+        cost_estimate=pl.CostEstimate(flops=size * width, bytes_accessed=size * width, transcendentals=0),
+        name="qkv_tiles",
+    )(chip, found, grad, given)
+
+
+def gelu_pair(u):
+    c = 0.7978845608028654
+    square = u * u
+    t = jnp.tanh(c * u * (1.0 + 0.044715 * square))
+    half = 0.5 * (1.0 + t)
+    slope = half + 0.5 * c * u * (1.0 - t * t) * (1.0 + 3.0 * 0.044715 * square)
+    return u * half, slope
+
+
+def norm_back(values, gain_vec, grad):
+    average = jnp.mean(values, axis=-1, keepdims=True)
+    centred = values - average
+    spread = jnp.mean(centred * centred, axis=-1, keepdims=True)
+    scale = lax.rsqrt(spread + norm_eps)
+    unit = centred * scale
+    scaled = grad * gain_vec
+    back = scale * (
+        scaled
+        - jnp.mean(scaled, axis=-1, keepdims=True)
+        - unit * jnp.mean(scaled * unit, axis=-1, keepdims=True)
+    )
+    return back, jnp.sum(grad * unit, axis=0, keepdims=True), jnp.sum(grad, axis=0, keepdims=True)
+
+
+def ff_kernel(seqs, plane, *refs):
+    me_ref, x_ref, att_ref, cot_ref, w_out_ref, gain_ref, shift_ref, up_ref, down_ref, *refs = refs
+    out_ref, res_ref, *refs = refs
+    ga_ref, norm_ref, gu_send, gu_keep, gd_send, gd_keep, gp_send, gp_keep, *refs = refs
+    att_sc, residual_sc, normed_sc, normed_t, turned_sc, acc_out, acc_grad = refs
+    step = pl.program_id(0)
+    tokens, width = x_ref.shape
+    rows = tokens // seqs
+    block = width // plane
+    near = plane // 2
+
+    def turn(values):
+        turned = values.T
+        for j in range(plane):
+            t = me_ref[0] ^ j
+            slot = (1 - (t & 1)) * near + (t >> 1)
+            at = pl.multiple_of(slot * block, block)
+            turned_sc[pl.ds(at, block), :] = turned[j * block : (j + 1) * block]
+
+    @pl.when(step == 0)
+    def _():
+        for seq in range(seqs):
+            for core in range(2):
+                cols = slice(core * width // 2, (core + 1) * width // 2)
+                att_sc[seq * rows : (seq + 1) * rows, cols] = att_ref[seq * 2 + core]
+        residual = x_ref[...].astype(F32) + jnp.dot(att_sc[...], w_out_ref[...], preferred_element_type=F32)
+        residual_sc[...] = residual
+        normed = norm_rows(residual, gain_ref[...], shift_ref[...]).astype(BF16)
+        normed_sc[...] = normed
+        normed_t[...] = normed.T
+        turn(cot_ref[...])
+        acc_out[...] = jnp.zeros_like(acc_out)
+        acc_grad[...] = jnp.zeros_like(acc_grad)
+
+    pre = jnp.dot(normed_sc[...], up_ref[...], preferred_element_type=F32)
+    active, slope = gelu_pair(pre)
+    active = active.astype(BF16)
+    grad_pre = (dot(cot_ref[...], down_ref[...], (1, 1)) * slope).astype(BF16)
+    acc_out[...] += jnp.dot(active, down_ref[...], preferred_element_type=F32)
+    acc_grad[...] += dot(grad_pre, up_ref[...], (1, 1))
+    grad_up = jnp.dot(normed_t[...], grad_pre, preferred_element_type=F32).astype(BF16)
+    grad_down = jnp.dot(turned_sc[...], active, preferred_element_type=F32).astype(BF16)
+    for slot in range(near):
+        gd_send[slot, 0] = grad_down[slot * block : (slot + 1) * block]
+        gd_keep[slot, 0] = grad_down[(near + slot) * block : (near + slot + 1) * block]
+
+    @pl.when(step < near)
+    def _():
+        gu_send[0] = grad_up
+
+    @pl.when(step >= near)
+    def _():
+        gu_keep[0] = grad_up
+
+    @pl.when(step == plane - 1)
+    def _():
+        residual = residual_sc[...]
+        out_ref[...] = (residual + acc_out[...]).astype(BF16)
+        back, gain_grad, shift_grad = norm_back(residual, gain_ref[...], acc_grad[...])
+        norm_ref[...] = jnp.zeros_like(norm_ref)
+        norm_ref[2:3, :] = gain_grad
+        norm_ref[3:4, :] = shift_grad
+        grad_res = cot_ref[...].astype(F32) + back
+        res_ref[...] = grad_res
+        grad_z = grad_res.astype(BF16)
+        grad_att = dot(grad_z, w_out_ref[...], (1, 1)).astype(BF16)
+        for seq in range(seqs):
+            for core in range(2):
+                cols = slice(core * width // 2, (core + 1) * width // 2)
+                ga_ref[seq * 2 + core] = grad_att[seq * rows : (seq + 1) * rows, cols]
+        turn(grad_z)
+        grad_proj = jnp.dot(turned_sc[...], att_sc[...], preferred_element_type=F32).astype(BF16)
+        for slot in range(near):
+            gp_send[slot] = grad_proj[slot * block : (slot + 1) * block]
+            gp_keep[slot] = grad_proj[(near + slot) * block : (near + slot + 1) * block]
+
+
+def feed_forward(me, x, attended, cotangent, w_out, gain, shift, w_up, w_down, plane):
+    seqs, rows, width = x.shape
+    hidden = w_up.shape[1]
+    tokens, near, part, block = seqs * rows, plane // 2, hidden // plane, width // plane
+
+    def at(i, me):
+        return me[0] ^ (2 * (i % near) + jnp.where(i < near, 1, 0))
+
+    def fixed(shape):
+        return pl.BlockSpec(shape, lambda i, me, n=len(shape): (0,) * n)
+
+    joined = attended.shape
+    outs = [
+        ((tokens, width), BF16, fixed((tokens, width))),
+        ((tokens, width), F32, fixed((tokens, width))),
+        (joined, BF16, fixed(joined)),
+        ((8, width), F32, fixed((8, width))),
+        ((near, width, part), BF16, pl.BlockSpec((1, width, part), lambda i, me: (jnp.minimum(i, near - 1), 0, 0))),
+        ((near, width, part), BF16, pl.BlockSpec((1, width, part), lambda i, me: (jnp.maximum(i - near, 0), 0, 0))),
+        *[
+            (
+                (near, plane, block, part),
+                BF16,
+                pl.BlockSpec((near, 1, block, part), lambda i, me: (0, at(i, me), 0, 0)),
+            )
+        ]
+        * 2,
+        *[((near, block, width), BF16, fixed((near, block, width)))] * 2,
+    ]
+    return pl.pallas_call(
+        functools.partial(ff_kernel, seqs, plane),
+        grid_spec=pltpu.PrefetchScalarGridSpec(
+            num_scalar_prefetch=1,
+            grid=(plane,),
+            in_specs=[fixed((tokens, width))]
+            + [fixed(joined), fixed((tokens, width)), fixed((width, width)), fixed((width,)), fixed((width,))]
+            + [
+                pl.BlockSpec((width, part), lambda i, me: (0, at(i, me))),
+                pl.BlockSpec((part, width), lambda i, me: (at(i, me), 0)),
+            ],
+            out_specs=[o[2] for o in outs],
+            scratch_shapes=[
+                pltpu.VMEM((tokens, width), BF16),
+                pltpu.VMEM((tokens, width), F32),
+                pltpu.VMEM((tokens, width), BF16),
+                pltpu.VMEM((width, tokens), BF16),
+                pltpu.VMEM((width, tokens), BF16),
+                pltpu.VMEM((tokens, width), F32),
+                pltpu.VMEM((tokens, width), F32),
+            ],
+        ),
+        out_shape=[jax.ShapeDtypeStruct(o[0], o[1]) for o in outs],
+        cost_estimate=pl.CostEstimate(
+            flops=12 * tokens * width * hidden + 6 * tokens * width * width,
+            bytes_accessed=8 * width * hidden,
+            transcendentals=tokens * hidden,
+        ),
+        name="feed_forward",
+    )(
+        me,
+        x.reshape(tokens, width),
+        attended,
+        cotangent.reshape(tokens, width),
+        w_out,
+        gain,
+        shift,
+        w_up,
+        w_down,
+    )
+
+
+def first_norm_kernel(seqs, x_ref, gain_ref, grad_ref, res_ref, out_ref, norm_ref):
+    half = x_ref.shape[0] // seqs // 2
+    for piece in range(2 * seqs):
+        at = slice(piece * half, (piece + 1) * half)
+        values = x_ref[at].astype(F32)
+        centred = values - jnp.mean(values, axis=-1, keepdims=True)
+        scale = lax.rsqrt(jnp.mean(centred * centred, axis=-1, keepdims=True) + norm_eps)
+        unit = centred * scale
+        scaled = grad_ref[piece, :half].astype(F32) * gain_ref[...]
+        back = scale * (
+            scaled
+            - jnp.mean(scaled, axis=-1, keepdims=True)
+            - unit * jnp.mean(scaled * unit, axis=-1, keepdims=True)
+        )
+        out_ref[at] = (res_ref[at] + back).astype(BF16)
+    norms = grad_ref[0, half:, :PAIR].astype(F32)
+    for piece in range(1, 2 * seqs):
+        norms = norms + grad_ref[piece, half:, :PAIR].astype(F32)
+    norm_ref[...] = norms
+
+
+def first_norm_back(x, gain, grad, grad_res):
+    seqs, rows, width = x.shape
+    tokens = seqs * rows
+    return pl.pallas_call(
+        functools.partial(first_norm_kernel, seqs),
+        grid=(1,),
+        in_specs=[fixed2((tokens, width)), fixed2((width,)), fixed2(grad.shape), fixed2((tokens, width))],
+        out_specs=[fixed2((tokens, width)), fixed2((8, PAIR))],
+        out_shape=[jax.ShapeDtypeStruct((tokens, width), BF16), jax.ShapeDtypeStruct((8, PAIR), F32)],
+        cost_estimate=pl.CostEstimate(flops=20 * tokens * width, bytes_accessed=12 * tokens * width, transcendentals=0),
+        name="first_norm_back",
+    )(x.reshape(tokens, width), gain, grad, grad_res)
+
+
+def exchange(blocks):
+    return lax.all_to_all(blocks, ("pb", "ka"), 0, 0, tiled=True)
+
+
+def swap(values, axes, size, bit):
+    return lax.ppermute(values, axes, [(i, i ^ bit) for i in range(size)])
+
+
+def add_pair_kernel(near, batch, *refs):
+    _, up_a, up_b, down_a, down_b, proj_a, proj_b, *outs = refs
+    outs, down_outs = outs[:near], outs[near:]
+    step = pl.program_id(0)
+    part = outs[0].shape[1]
+
+    def both(a, b):
+        return (a.astype(F32) + b.astype(F32)).astype(BF16)
+
+    @pl.when(step < batch)
+    def _():
+        for k in range(near):
+            outs[k][...] = both(up_a[k], up_b[k])
+
+    for far in range(batch):
+
+        @pl.when(step == batch + far)
+        def _():
+            for k in range(near):
+                total = both(down_a[k], down_b[k])
+                slab = total.shape[0] * total.shape[1]
+                target, at = down_outs[far in (1, 2)], (far > 1) * near * slab + k * slab
+                target[at : at + slab] = total.reshape(slab, part)
+
+    @pl.when(step == 2 * batch)
+    def _():
+        for k in range(near):
+            total = both(proj_a[k], proj_b[k])
+            outs[k][...] = jnp.concatenate([total[:, :part], total[:, part:]], axis=0)
+
+
+def add_pair(mine, up, down, proj, batch):
+    near, width, part = up[0].shape
+    plane, block = down[0].shape[1:3]
+    tall, few = width // batch, plane // batch
+    up_spec = pl.BlockSpec((near, tall, part), lambda i, m: (0, jnp.minimum(i, batch - 1), 0))
+    down_spec = pl.BlockSpec(
+        (near, few, block, part), lambda i, m: (0, m[0] ^ jnp.clip(i - batch, 0, batch - 1), 0, 0)
+    )
+    proj_spec = pl.BlockSpec((near, block, width), lambda i, m: (0, 0, 0))
+    last = lambda i, m: (jnp.where(i < batch, i, jnp.where(i < 2 * batch, batch - 1, batch)), 0)
+    down_shape = (2 * near * few * block, part)
+    return pl.pallas_call(
+        functools.partial(add_pair_kernel, near, batch),
+        grid_spec=pltpu.PrefetchScalarGridSpec(
+            num_scalar_prefetch=1,
+            grid=(2 * batch + 1,),
+            in_specs=[up_spec] * 2 + [down_spec] * 2 + [proj_spec] * 2,
+            out_specs=[pl.BlockSpec((tall, part), last)] * near
+            + [pl.BlockSpec(down_shape, lambda i, m: (0, 0))] * 2,
+        ),
+        out_shape=[jax.ShapeDtypeStruct((width + tall, part), BF16)] * near
+        + [jax.ShapeDtypeStruct(down_shape, BF16)] * 2,
+        cost_estimate=pl.CostEstimate(
+            flops=near * 9 * tall * part, bytes_accessed=6 * near * 9 * tall * part, transcendentals=0
+        ),
+        name="add_pair",
+    )(mine, *up, *down, *proj)
+
+
+def add_all(parts):
+    total = parts[0].astype(F32)
+    for p in parts[1:]:
+        total = total + p.astype(F32)
+    return total
+
+
+def over_batch(stacked):
+    size = lax.axis_size("batch")
+    mine = lax.axis_index("batch")
+    if size > 4:
+        return lax.psum_scatter(stacked, "batch", scatter_dimension=0, tiled=True)[0].astype(F32)
+    parts = [lax.dynamic_index_in_dim(stacked, mine, 0, False)]
+    for bit in range(1, size):
+        block = lax.dynamic_index_in_dim(stacked, mine ^ bit, 0, False)
+        parts.append(swap(block, "batch", size, bit))
+    return add_all(parts)
+
+
+def over_plane(tiles, plane):
+    parts = [tiles[0]]
+    for k in range(1, len(tiles)):
+        parts.append(swap(tiles[k], ("pb", "ka"), plane, 2 * k))
+    return add_all(parts)
+
+
+def shards(
+    inputs,
+    block_place,
+    ln1_gain,
+    ln1_shift,
+    w_qkv,
+    w_out,
+    ln2_gain,
+    ln2_shift,
+    w_up,
+    w_down,
+    cotangent,
+):
+    seqs, rows, width = inputs.shape
+    hidden = w_up.shape[1]
+    plane = lax.axis_size("pb") * lax.axis_size("ka")
+    planes = ("pb", "ka")
+    batch = lax.axis_size("batch")
+    near = plane // 2
+    few = batch == 4
     me = lax.axis_index(planes)
     scalar = lambda value: value.astype(jnp.int32).reshape(1)
     core, chip = scalar(me & 1), scalar(me >> 1)
@@ -733,51 +1091,45 @@
         ]
     tile = over_plane(tiles, plane).astype(BF16)
     if few:
-        down_parts = [down[0]] + [swap(down[bit], "batch", batch, bit) for bit in range(1, batch)]
-        down_parts = [d.reshape(near, -1, part) for d in down_parts]
-        down_tiles = [add_all([d[k] for d in down_parts]).astype(BF16) for k in range(near)]
-
-    grad_packed, grad_qkv = attend_back(core, place, to, packed, grad_att, sums, stats, normed1)
-    grad_packed, tile = lax.optimization_barrier((grad_packed, tile))
-    stay = grad_qkv.shape[0] // 2
-    given = swap(grad_qkv[stay:], planes, plane, 1)
-    keep, send, norm = normed_back(
-        core, place, back, grad_packed, mine, other, norm2, w_qkv
+        down = add_all([down[0], swap(down[1], "batch", batch, 1)]).astype(BF16)
+
+    grad_qkv, keep, send, norm = attend_back(
+        core, place, to, packed, grad_att, sums, stats, normed1, mine, other, norm2, w_qkv
     )
-    tiles = qkv_tiles(chip, found, grad_qkv[:stay], given, near)
+    given = swap(grad_qkv[grad_qkv.shape[0] // 2 :], planes, plane, 1)
+    if few:
+        given, tile, down = lax.optimization_barrier((given, tile, down))
+        down = jnp.split(down, 2)
+        down[1] = swap(down[1], "batch", batch, 3)
+    late = qkv_tiles(chip, found, grad_qkv, given, near)
+    keep, late = lax.optimization_barrier((keep, late))
     returned = exchange(merge(keep, swap(send, planes, plane, 1), norm))
     if few:
-        returned, down_tiles = lax.optimization_barrier((returned, down_tiles))
-    grad_inputs, norm = first_norm_back(inputs, ln1_gain, returned, grad_res)
-
-    if few:
-        grad_down = over_plane(down_tiles, plane)
+        returned, down = lax.optimization_barrier((returned, add_all(down).astype(BF16)))
+        grad_down = over_plane(jnp.split(down, near), plane)
     else:
         cut = batch // plane
         down_tile = tile[width : 2 * width].reshape(plane, block, cut, part // cut).transpose(0, 2, 1, 3)
         grad_down = over_batch(down_tile.reshape(batch, block, part // cut))
+    grad_down = grad_down.reshape(-1, block, min(part, hidden // batch)).transpose(0, 2, 1).reshape(-1, block)
+
     proj_tile = tile[-2 * block :].reshape(2, block, part).transpose(1, 0, 2).reshape(block, batch, slab)
     proj_tile = proj_tile.transpose(1, 0, 2)
     up_tile = tile[:width].reshape(batch, slab, part)
+    owned = 3 * width // plane
+    qkv_tile = over_plane(late, plane).astype(BF16).reshape(owned, batch, slab).transpose(1, 0, 2)
+    grad_inputs, norms = first_norm_back(inputs, ln1_gain, returned, grad_res)
     if few:
-        joined = jnp.concatenate([up_tile, proj_tile.reshape(batch, block * slab // part, part)], axis=1)
-        summed = over_batch(joined)
-        grad_up, grad_proj = summed[:slab], summed[slab:].reshape(block, slab)
+        joined = [t.reshape(batch, -1, part) for t in (up_tile, proj_tile, qkv_tile)]
+        summed = over_batch(jnp.concatenate(joined, axis=1))
+        grad_up, grad_proj, grad_qkv = jnp.split(summed, (slab, slab + block * slab // part))
+        grad_proj, grad_qkv = grad_proj.reshape(block, slab), grad_qkv.reshape(owned, slab)
+        for bit in (1, 2):
+            norms = norms + swap(norms, "batch", batch, bit)
     else:
-        grad_up, grad_proj = over_batch(up_tile), over_batch(proj_tile)
-    grad_down = grad_down.reshape(-1, block, min(part, hidden // batch)).transpose(0, 2, 1).reshape(-1, block)
+        grad_up, grad_proj, grad_qkv = over_batch(up_tile), over_batch(proj_tile), over_batch(qkv_tile)
+        norms = lax.psum(norms, "batch")
     grad_proj = grad_proj.T
-
-    owned = 3 * width // plane
-    tile = over_plane(tiles, plane).astype(BF16)
-    qkv_tile = tile.reshape(owned, batch, slab).transpose(1, 0, 2)
-    if few:
-        norm_tile = jnp.pad(norm.astype(BF16), ((0, 8), (0, slab - PAIR)))
-        norm_tile = jnp.broadcast_to(norm_tile[None], (batch, *norm_tile.shape))
-        summed = over_batch(jnp.concatenate([qkv_tile, norm_tile], axis=1))
-        grad_qkv, norms = summed[:owned], summed[owned:]
-    else:
-        grad_qkv, norms = over_batch(qkv_tile), lax.psum(norm, "batch")
     return (
         outputs.reshape(inputs.shape),
         grad_inputs.reshape(inputs.shape),

time: 256 us -> 218 us (0.85)
  waiting for transfers between devices: 60.6 us -> 22.1 us
  local copies, waits for them, and re-layouts: 13.1 us -> 16.5 us
    ppermute x24 -> x22, waiting for transfers between devices: 60.6 us -> 22.1 us  [swap(): return lax.ppermute(values, axes, [(i, i ^ bit) for i in range(size)])]
    pallas_call x1 -> x0, Pallas kernels: 8.13 us -> none  [normed_back(): pl.pallas_call(normed_back_kernel, grid_spec=pltpu.PrefetchScalarGridSpec...]
    pallas_call x1, Pallas kernels: 18.5 us -> 25.9 us  [attend_back(): pl.pallas_call(attend_back_kernel, grid_spec=pltpu.PrefetchScalarGridSpec...]
    convert_element_type x2 -> x3, other arithmetic: 3.24 us -> 5.54 us  [the longest x1 2.04 us: shards(): add_all(down).astype(BF16)]
    ppermute x24 -> x22, starting transfers between devices: 25.2 us -> 23.3 us  [swap(): return lax.ppermute(values, axes, [(i, i ^ bit) for i in range(size)])]
    unnamed x37 -> x36, local copies, waits for them, and re-layouts: 5.92 us -> 5.86 us
  transfers between devices with their start and end apart: 26 -> 24, of which waited for: 7 -> 6; matrix products, arithmetic and copies ran while one was open for 6% -> 10% of each run, Pallas kernels for 15% -> 21%
where the time goes in v1:
time: 218 us; the launch traced here: 215 us
  Pallas kernels  99.4 us (46%)
  blocking collectives  33 us (15%)
  starting transfers between devices  30.9 us (14%)
  waiting for transfers between devices  22.1 us (10%)
  local copies, waits for them, and re-layouts  16.5 us (8%)
  other arithmetic  12.6 us (6%)
    all_to_all x2, blocking collectives, exchange(): return lax.all_to_all(blocks, ('pb', 'ka'), 0, 0, tiled=True)  33 us
    pallas_call x1, Pallas kernels, feed_forward(): pl.pallas_call(functools.partial(ff_kernel, seqs, plane), grid_spec=pltpu...  31.6 us
    pallas_call x1, Pallas kernels, attend_back(): pl.pallas_call(attend_back_kernel, grid_spec=pltpu.PrefetchScalarGridSpec...  25.9 us
    ppermute x22, starting transfers between devices, swap(): return lax.ppermute(values, axes, [(i, i ^ bit) for i in range(size)])  23.3 us
    ppermute x22, waiting for transfers between devices, swap(): return lax.ppermute(values, axes, [(i, i ^ bit) for i in range(size)])  22.1 us
    pallas_call x1, Pallas kernels, attend(): pl.pallas_call(attend_kernel, grid_spec=pltpu.PrefetchScalarGridSpec(num_...  21.8 us
    pallas_call x1, Pallas kernels, add_pair(): pl.pallas_call(functools.partial(add_pair_kernel, near, batch), grid_spec...  9.66 us
    all_to_all x2, starting transfers between devices, exchange(): return lax.all_to_all(blocks, ('pb', 'ka'), 0, 0, tiled=True)  7.63 us
  transfers between devices with their start and end apart: 24, of which 6 were waited for; matrix products, arithmetic and copies ran while one was open for 10% of the time, Pallas kernels for 21%

profile of v1, /device:TPU:0, one launch (start us, length us, event | category | flops | bytes accessed | tf_op | source)
XLA Modules:
  0.0 215.4 jit_solution(16495525417785307713)
XLA Ops:
  0.6 17.0 %all_to_all.20.mine_ref = bf16[8,64,768]{2,1,0:T(8,128)(2,1)S(1)} all-to-all(bf16[8,64,768]{2,1,0:T(8,128)(2,1)} %bitcast.35), channel_id=1, replica_groups=mesh['batch'=4,'pb'=2,'ka'=4] {'pb','ka'}, dimensions={0} | all-to-all | bytes 1572864 | tf_op jit(solution)/shard_map/all_to_all | solution.py:949
  17.6 0.6 fusion.2.place_ref
  18.2 1.7 collective-permute-done.other_ref
  19.9 0.9 copy-done.17
  20.8 21.8 %attend.1 = (bf16[8,128,384]{2,1,0:T(8,128)(2,1)}, bf16[1024,768]{1,0:T(8,128)(2,1)}, bf16[3,1024,384]{2,1,0:T(8,128)(2,1)}, f32[3,128,1024]{2,1,0:T(8,128)}, f32[3,8,1024]{2,1,0:T(8,128)}) custom-call(s32[1]{0:T(128)} %bitcast.2.core_ref, s32[8]{0:T(128)} %fusion.2.place_ref, bf16[8,64,768]{2,1,0:T(8,128)(2,1)} %copy-done.8, ...), custom_call_target="tpu_custom_call" | custom-call | flops 5033164800 | bytes 6291456 | tf_op jit(solution)/shard_map/attend/pallas_call | solution.py:111
  42.7 16.0 %all_to_all.21.refs_2_ = bf16[8,128,384]{2,1,0:T(8,128)(2,1)} all-to-all(bf16[8,128,384]{2,1,0:T(8,128)(2,1)} %get-tuple-element.55), channel_id=1, replica_groups=mesh['batch'=4,'pb'=2,'ka'=4] {'pb','ka'}, dimensions={0} | all-to-all | bytes 1572864 | tf_op jit(solution)/shard_map/all_to_all | solution.py:949
  58.6 31.6 %feed_forward.1 = (bf16[512,768]{1,0:T(8,128)(2,1)}, f32[512,768]{1,0:T(8,128)}, bf16[8,128,384]{2,1,0:T(8,128)(2,1)}, f32[8,768]{1,0:T(8,128)}, bf16[4,768,384]...) custom-call(s32[1]{0:T(128)} %bitcast.refs_0_, ...), custom_call_target="tpu_custom_call" | custom-call | flops 16307453952 | bytes 18874368 | tf_op jit(solution)/shard_map/feed_forward/pallas_call | solution.py:871
  90.4 0.5 collective-permute-start.2
  90.9 3.7 %all-to-all-start.2 = ((bf16[8,128,384]{2,1,0:T(8,128)(2,1)}), bf16[8,128,384]{2,1,0:T(8,128)(2,1)S(1)}, u32[]{:S(2)}, u32[]{:S(2)}) async-start(bf16[8,128,384]{2,1,0:T(8,128)(2,1)} %get-tuple-element.58), calls=%async_computation.2 | async-start | bytes 1572864 | tf_op jit(solution)/shard_map/all_to_all | solution.py:949
  94.6 0.2 collective-permute-start.3
  94.8 0.5 broadcast_select_fusion.1.to_ref
  95.3 0.6 broadcast_select_fusion.found_ref
  95.9 3.7 %collective-permute-done.3.refs_6_ = bf16[4,96,768]{2,1,0:T(8,128)(2,1)} collective-permute-done((bf16[4,96,768]{2,1,0:T(8,128)(2,1)}, bf16[4,96,768]{2,1,0:T(8,128)(2,1)}, u32[]{:S(2)}, u32[]{:S(2)}) %collective-permute-start.3) | collective-permute-done | bytes 589856 | tf_op jit(solution)/shard_map/ppermute | solution.py:953
  99.6 1.4 copy-done.5
  101.0 9.7 %add_pair.1 = (bf16[960,384]{1,0:T(8,128)(2,1)}, bf16[960,384]{1,0:T(8,128)(2,1)}, bf16[960,384]{1,0:T(8,128)(2,1)}, bf16[960,384]{1,0:T(8,128)(2,1)}, bf16[1536...) custom-call(s32[1]{0:T(128)} %bitcast.8.refs_0_, bf16[4,768,384]{2,1,0:T(8,128)(2,1)} %get-tuple-element.59.refs_1_, ...), custom_call_target="tpu_custom_call" | custom-call | flops 2654208 | bytes 15925248 | tf_op jit(solution)/shard_map/add_pair/pallas_call | solution.py:998
  110.7 1.6 collective-permute-start.8
  112.4 1.4 collective-permute-start.5
  113.8 0.6 collective-permute-start.6
  114.3 1.5 collective-permute-start.7
  115.9 25.9 %attend_back.1 = (bf16[1152,768]{1,0:T(8,128)(2,1)}, f32[8,64,768]{2,1,0:T(8,128)}, bf16[8,64,768]{2,1,0:T(8,128)(2,1)}, f32[8,768]{1,0:T(8,128)}) custom-call(s32[1]{0:T(128)} %bitcast.2.core_ref, s32[8]{0:T(128)} %fusion.2.place_ref, s32[36]{0:T(128)} %broadcast_select_fusion.1.to_ref, bf16[3,1024,384]{2,1,0:T(8,128)(2,1)} %get-tuple-element.57.qkv_ref, ...), custom_call_target="tpu_custom_call" | custom-call | flops 11676942336 | bytes 6291456 | tf_op jit(solution)/shard_map/attend_back/pallas_call | solution.py:227
  141.8 1.3 slice.12
  143.2 0.5 collective-permute-start.9
  143.7 0.9 copy-done.11
  144.5 3.4 %collective-permute-done.7 = bf16[960,384]{1,0:T(8,128)(2,1)} collective-permute-done((bf16[960,384]{1,0:T(8,128)(2,1)}, bf16[960,384]{1,0:T(8,128)(2,1)}, u32[]{:S(2)}, u32[]{:S(2)}) %collective-permute-start.7) | collective-permute-done | bytes 737312 | tf_op jit(solution)/shard_map/ppermute | solution.py:953
  147.9 1.7 add_convert_fusion.1
  149.7 1.9 add_convert_fusion
  151.5 0.9 copy-done.7
  152.5 3.7 %qkv_tiles.1 = (bf16[288,768]{1,0:T(8,128)(2,1)}, bf16[288,768]{1,0:T(8,128)(2,1)}, bf16[288,768]{1,0:T(8,128)(2,1)}, bf16[288,768]{1,0:T(8,128)(2,1)}) custom-call(s32[1]{0:T(128)} %bitcast.9.chip_ref, s32[36]{0:T(128)} %broadcast_select_fusion.found_ref, bf16[1152,768]{1,0:T(8,128)(2,1)} %get-tuple-element.77.keep_ref, bf16[576,768]{1,0:T(8,128)(2,1)} %copy-done.7), custom_call_target="tpu_custom_call" | custom-call | flops 442368 | bytes 442368 | tf_op jit(solution)/shard_map/qkv_tiles/pallas_call | solution.py:727
  156.2 1.4 collective-permute-start.11
  157.6 0.6 collective-permute-start.12
  158.2 1.5 collective-permute-start.13
  159.7 0.9 split.28
  160.5 2.5 %collective-permute-start.10 = (bf16[768,384]{1,0:T(8,128)(2,1)}, bf16[768,384]{1,0:T(8,128)(2,1)}, u32[]{:S(2)}, u32[]{:S(2)}) collective-permute-start(bf16[768,384]{1,0:T(8,128)(2,1)} %split.28), channel_id=1, source_target_pairs={{0,24},{8,16},{16,8},{24,0},{1,25},{9,17},{17,9},{25,1},{2,26},{10... | collective-permute-start | bytes 1769480 | tf_op jit(solution)/shard_map/ppermute | solution.py:953
  163.0 2.8 %merge.1 = bf16[8,72,768]{2,1,0:T(8,128)(2,1)} custom-call(f32[8,64,768]{2,1,0:T(8,128)} %get-tuple-element.89.keep_ref, bf16[8,64,768]{2,1,0:T(8,128)(2,1)} %collective-permute-done.9.other_ref, f32[8,768]{1,0:T(8,128)} %get-tuple-element.91.norm_ref), custom_call_target="tpu_custom_call" | custom-call | flops 393216 | bytes 3145728 | tf_op jit(solution)/shard_map/merge/pallas_call | solution.py:283
  165.8 0.9 slice.13
  166.7 3.9 %all-to-all-start.3 = ((bf16[8,72,768]{2,1,0:T(8,128)(2,1)}), bf16[8,72,768]{2,1,0:T(8,128)(2,1)S(1)}, u32[]{:S(2)}, u32[]{:S(2)}) async-start(bf16[8,72,768]{2,1,0:T(8,128)(2,1)} %merge.1), calls=%async_computation.3 | async-start | bytes 1769472 | tf_op jit(solution)/shard_map/all_to_all | solution.py:949
  171.1 0.7 copy-done.12
  171.9 8.6 %collective-permute-done.13 = bf16[288,768]{1,0:T(8,128)(2,1)} collective-permute-done((bf16[288,768]{1,0:T(8,128)(2,1)}, bf16[288,768]{1,0:T(8,128)(2,1)}, u32[]{:S(2)}, u32[]{:S(2)}) %collective-permute-start.13) | collective-permute-done | bytes 442400 | tf_op jit(solution)/shard_map/ppermute | solution.py:953
  180.5 1.6 add_convert_fusion.3
  182.2 0.5 reshape.87
  182.8 1.1 reshape.88
  183.9 1.3 pad_maximum_fusion
  185.2 0.9 dynamic-slice_bitcast_fusion.2
  186.1 0.4 collective-permute-start.14
  186.6 2.6 %collective-permute-start.15 = (bf16[384,384]{1,0:T(8,128)(2,1)}, bf16[384,384]{1,0:T(8,128)(2,1)}, u32[]{:S(2)}, u32[]{:S(2)}) collective-permute-start(bf16[384,384]{1,0:T(8,128)(2,1)} %get-tuple-element.105), channel_id=1, source_target_pairs={{0,16},{8,24},{16,0},{24,8},{1,17},{9,25},{17,1},{25,9},{2,18},{10... | collective-permute-start | bytes 884744 | tf_op jit(solution)/shard_map/ppermute | solution.py:953
  189.2 1.3 collective-permute-start.16
  190.5 2.0 add_convert_fusion.2
  192.6 0.9 copy-done.2
  193.5 3.9 %first_norm_back.1 = (bf16[512,768]{1,0:T(8,128)(2,1)}, f32[8,128]{1,0:T(8,128)}) custom-call(bf16[512,768]{1,0:T(8,128)(2,1)} %bitcast.37, f32[768]{0:T(1024)} %gain_ref.3, bf16[8,72,768]{2,1,0:T(8,128)(2,1)} %copy-done.2, f32[512,768]{1,0:T(8,128)} %get-tuple-element.94.res_ref), custom_call_target="tpu_custom_call" | custom-call | flops 7864320 | bytes 4718592 | tf_op jit(solution)/shard_map/first_norm_back/pallas_call | solution.py:937
  197.4 1.3 collective-permute-start.20
  198.8 1.4 collective-permute-start.17
  200.2 1.0 collective-permute-done.20
  201.2 1.3 collective-permute-start.18
  202.5 0.7 add.88
  203.2 1.6 collective-permute-start.19
  204.8 3.6 %collective-permute-done.15 = bf16[384,384]{1,0:T(8,128)(2,1)} collective-permute-done((bf16[384,384]{1,0:T(8,128)(2,1)}, bf16[384,384]{1,0:T(8,128)(2,1)}, u32[]{:S(2)}, u32[]{:S(2)}) %collective-permute-start.15) | collective-permute-done | bytes 294944 | tf_op jit(solution)/shard_map/ppermute | solution.py:953
  208.4 0.9 collective-permute-start.21
  209.2 1.3 fusion.1
  210.5 0.7 split.38
  211.4 0.9 copy.34
  212.4 0.7 copy.35
  213.1 0.6 slice.15
  213.7 1.0 convert_add_fusion.1
  214.7 0.7 copy.37
  (64 shorter events, 1.1 us)
Async XLA Ops:
  0.6 17.0 %copy-start = (s32[4,8]{1,0:T(4,128)S(1)}, s32[4,8]{1,0:T(4,128)}, u32[]{:S(2)}) copy-start(s32[4,8]{1,0:T(4,128)} %param.16) | copy-start | bytes 388
  17.6 2.3 %copy-start.8 = (bf16[8,64,768]{2,1,0:T(8,128)(2,1)}, bf16[8,64,768]{2,1,0:T(8,128)(2,1)S(1)}, u32[]{:S(2)}) copy-start(bf16[8,64,768]{2,1,0:T(8,128)(2,1)S(1)} %all_to_all.20.mine_ref) | copy-start | bytes 2359300
  17.6 2.3 %collective-permute-start = (bf16[8,64,768]{2,1,0:T(8,128)(2,1)S(1)}, bf16[8,64,768]{2,1,0:T(8,128)(2,1)S(1)}, u32[]{:S(2)}, u32[]{:S(2)}) collective-permute-start(bf16[8,64,768]{2,1,0:T(8,128)(2,1)S(1)} %all_to_all.20.mine_ref), channel_id=1, source_target_pairs={{0,1},{1,0},{2,3},{3,2},{4,5},{5,4},{6,7},{7,6},{8,9},{9,8},{10,11... | collective-permute-start | bytes 2359304 | tf_op jit(solution)/shard_map/ppermute | solution.py:953
  19.9 0.9 copy-start.17
  90.2 4.6 %copy-start.15 = (s32[36]{0:T(128)S(1)}, s32[36]{0:T(128)}, u32[]{:S(2)}) copy-start(s32[36]{0:T(128)} %constant.45.clone) | copy-start | bytes 436
  90.3 4.6 %copy-start.16 = (s32[36]{0:T(128)S(1)}, s32[36]{0:T(128)}, u32[]{:S(2)}) copy-start(s32[36]{0:T(128)} %constant.46.clone) | copy-start | bytes 436
  90.3 5.1 %copy-start.13 = (s32[36]{0:T(128)S(1)}, s32[36]{0:T(128)}, u32[]{:S(2)}) copy-start(s32[36]{0:T(128)} %constant.47.clone) | copy-start | bytes 436
  90.3 5.0 %copy-start.14 = (s32[36]{0:T(128)S(1)}, s32[36]{0:T(128)}, u32[]{:S(2)}) copy-start(s32[36]{0:T(128)} %constant.48.clone) | copy-start | bytes 436
  90.3 9.3 %collective-permute-start.1 = (bf16[4,768,384]{2,1,0:T(8,128)(2,1)}, bf16[4,768,384]{2,1,0:T(8,128)(2,1)S(1)}, u32[]{:S(2)}, u32[]{:S(2)}) collective-permute-start(bf16[4,768,384]{2,1,0:T(8,128)(2,1)} %get-tuple-element.60), channel_id=1, source_target_pairs={{0,1},{1,0},{2,3},{3,2},{4,5},{5,4},{6,7},{7,6},{8,9},{9,8},{10,11... | collective-permute-start | bytes 7077896 | tf_op jit(solution)/shard_map/ppermute | solution.py:953
  90.4 9.2 %collective-permute-start.2 = (bf16[4,8,96,384]{3,2,1,0:T(8,128)(2,1)}, bf16[4,8,96,384]{3,2,1,0:T(8,128)(2,1)}, u32[]{:S(2)}, u32[]{:S(2)}) collective-permute-start(bf16[4,8,96,384]{3,2,1,0:T(8,128)(2,1)} %get-tuple-element.62), channel_id=1, source_target_pairs={{0,1},{1,0},{2,3},{3,2},{4,5},{5,4},{6,7},{7,6},{8,9},{9,8},{10,11... | collective-permute-start | bytes 7077896 | tf_op jit(solution)/shard_map/ppermute | solution.py:953
  90.9 19.8 %all-to-all-start.2 = ((bf16[8,128,384]{2,1,0:T(8,128)(2,1)}), bf16[8,128,384]{2,1,0:T(8,128)(2,1)S(1)}, u32[]{:S(2)}, u32[]{:S(2)}) async-start(bf16[8,128,384]{2,1,0:T(8,128)(2,1)} %get-tuple-element.58), calls=%async_computation.2 | async-start | bytes 1572864 | tf_op jit(solution)/shard_map/all_to_all | solution.py:949
  94.6 5.0 %collective-permute-start.3 = (bf16[4,96,768]{2,1,0:T(8,128)(2,1)}, bf16[4,96,768]{2,1,0:T(8,128)(2,1)}, u32[]{:S(2)}, u32[]{:S(2)}) collective-permute-start(bf16[4,96,768]{2,1,0:T(8,128)(2,1)} %get-tuple-element.64), channel_id=1, source_target_pairs={{0,1},{1,0},{2,3},{3,2},{4,5},{5,4},{6,7},{7,6},{8,9},{9,8},{10,11... | collective-permute-start | bytes 1769480 | tf_op jit(solution)/shard_map/ppermute | solution.py:953
  99.6 1.4 copy-start.5
  110.7 5.1 %copy-start.9 = (bf16[8,128,384]{2,1,0:T(8,128)(2,1)}, bf16[8,128,384]{2,1,0:T(8,128)(2,1)S(1)}, u32[]{:S(2)}) copy-start(bf16[8,128,384]{2,1,0:T(8,128)(2,1)S(1)} %all-to-all-done.2.g_ref) | copy-start | bytes 2359300
  110.7 38.9 %collective-permute-start.8 = (bf16[1536,384]{1,0:T(8,128)(2,1)}, bf16[1536,384]{1,0:T(8,128)(2,1)}, u32[]{:S(2)}, u32[]{:S(2)}) collective-permute-start(bf16[1536,384]{1,0:T(8,128)(2,1)} %get-tuple-element.83), channel_id=1, source_target_pairs={{0,8},{8,0},{16,24},{24,16},{1,9},{9,1},{17,25},{25,17},{2,10},{10... | collective-permute-start | bytes 3538952 | tf_op jit(solution)/shard_map/ppermute | solution.py:953
  112.4 30.8 %collective-permute-start.5 = (bf16[960,384]{1,0:T(8,128)(2,1)}, bf16[960,384]{1,0:T(8,128)(2,1)S(1)}, u32[]{:S(2)}, u32[]{:S(2)}) collective-permute-start(bf16[960,384]{1,0:T(8,128)(2,1)} %get-tuple-element.79), channel_id=1, source_target_pairs={{0,2},{1,3},{2,0},{3,1},{4,6},{5,7},{6,4},{7,5},{8,10},{9,11},{10,... | collective-permute-start | bytes 2211848 | tf_op jit(solution)/shard_map/ppermute | solution.py:953
  113.8 29.9 %collective-permute-start.6 = (bf16[960,384]{1,0:T(8,128)(2,1)}, bf16[960,384]{1,0:T(8,128)(2,1)S(1)}, u32[]{:S(2)}, u32[]{:S(2)}) collective-permute-start(bf16[960,384]{1,0:T(8,128)(2,1)} %get-tuple-element.80), channel_id=1, source_target_pairs={{0,4},{1,5},{2,6},{3,7},{4,0},{5,1},{6,2},{7,3},{8,12},{9,13},{10,... | collective-permute-start | bytes 2211848 | tf_op jit(solution)/shard_map/ppermute | solution.py:953
  114.3 33.6 %collective-permute-start.7 = (bf16[960,384]{1,0:T(8,128)(2,1)}, bf16[960,384]{1,0:T(8,128)(2,1)}, u32[]{:S(2)}, u32[]{:S(2)}) collective-permute-start(bf16[960,384]{1,0:T(8,128)(2,1)} %get-tuple-element.81), channel_id=1, source_target_pairs={{0,6},{1,7},{2,4},{3,5},{4,2},{5,3},{6,0},{7,1},{8,14},{9,15},{10,... | collective-permute-start | bytes 2211848 | tf_op jit(solution)/shard_map/ppermute | solution.py:953
  141.8 6.1 %copy-start.10 = (bf16[960,384]{1,0:T(8,128)(2,1)S(1)}, bf16[960,384]{1,0:T(8,128)(2,1)}, u32[]{:S(2)}) copy-start(bf16[960,384]{1,0:T(8,128)(2,1)} %get-tuple-element.78) | copy-start | bytes 2211844
  143.1 8.5 %collective-permute-start.4 = (bf16[576,768]{1,0:T(8,128)(2,1)S(1)}, bf16[576,768]{1,0:T(8,128)(2,1)S(1)}, u32[]{:S(2)}, u32[]{:S(2)}) collective-permute-start(bf16[576,768]{1,0:T(8,128)(2,1)S(1)} %slice.12), channel_id=1, source_target_pairs={{0,1},{1,0},{2,3},{3,2},{4,5},{5,4},{6,7},{7,6},{8,9},{9,8},{10,11... | collective-permute-start | bytes 2654216 | tf_op jit(solution)/shard_map/ppermute | solution.py:953
  143.2 6.5 %copy-start.6 = (bf16[1536,384]{1,0:T(8,128)(2,1)S(1)}, bf16[1536,384]{1,0:T(8,128)(2,1)}, u32[]{:S(2)}) copy-start(bf16[1536,384]{1,0:T(8,128)(2,1)} %get-tuple-element.82) | copy-start | bytes 3538948
  143.2 19.9 %collective-permute-start.9 = (bf16[8,64,768]{2,1,0:T(8,128)(2,1)}, bf16[8,64,768]{2,1,0:T(8,128)(2,1)}, u32[]{:S(2)}, u32[]{:S(2)}) collective-permute-start(bf16[8,64,768]{2,1,0:T(8,128)(2,1)} %get-tuple-element.90), channel_id=1, source_target_pairs={{0,1},{1,0},{2,3},{3,2},{4,5},{5,4},{6,7},{7,6},{8,9},{9,8},{10,11... | collective-permute-start | bytes 2359304 | tf_op jit(solution)/shard_map/ppermute | solution.py:953
  143.7 0.9 copy-start.11
  149.6 16.2 %copy-start.3 = (bf16[960,384]{1,0:T(8,128)(2,1)}, bf16[960,384]{1,0:T(8,128)(2,1)S(1)}, u32[]{:S(2)}) copy-start(bf16[960,384]{1,0:T(8,128)(2,1)S(1)} %add_convert_fusion.1) | copy-start | bytes 2211844
  151.5 0.9 copy-start.7
  156.2 14.9 %collective-permute-start.11 = (bf16[288,768]{1,0:T(8,128)(2,1)}, bf16[288,768]{1,0:T(8,128)(2,1)S(1)}, u32[]{:S(2)}, u32[]{:S(2)}) collective-permute-start(bf16[288,768]{1,0:T(8,128)(2,1)} %get-tuple-element.98), channel_id=1, source_target_pairs={{0,2},{1,3},{2,0},{3,1},{4,6},{5,7},{6,4},{7,5},{8,10},{9,11},{10,... | collective-permute-start | bytes 1327112 | tf_op jit(solution)/shard_map/ppermute | solution.py:953
  157.6 13.5 %collective-permute-start.12 = (bf16[288,768]{1,0:T(8,128)(2,1)}, bf16[288,768]{1,0:T(8,128)(2,1)}, u32[]{:S(2)}, u32[]{:S(2)}) collective-permute-start(bf16[288,768]{1,0:T(8,128)(2,1)} %get-tuple-element.99), channel_id=1, source_target_pairs={{0,4},{1,5},{2,6},{3,7},{4,0},{5,1},{6,2},{7,3},{8,12},{9,13},{10,... | collective-permute-start | bytes 1327112 | tf_op jit(solution)/shard_map/ppermute | solution.py:953
  158.2 22.4 %collective-permute-start.13 = (bf16[288,768]{1,0:T(8,128)(2,1)}, bf16[288,768]{1,0:T(8,128)(2,1)}, u32[]{:S(2)}, u32[]{:S(2)}) collective-permute-start(bf16[288,768]{1,0:T(8,128)(2,1)} %get-tuple-element.100), channel_id=1, source_target_pairs={{0,6},{1,7},{2,4},{3,5},{4,2},{5,3},{6,0},{7,1},{8,14},{9,15},{10,... | collective-permute-start | bytes 1327112 | tf_op jit(solution)/shard_map/ppermute | solution.py:953
  160.5 30.0 %collective-permute-start.10 = (bf16[768,384]{1,0:T(8,128)(2,1)}, bf16[768,384]{1,0:T(8,128)(2,1)}, u32[]{:S(2)}, u32[]{:S(2)}) collective-permute-start(bf16[768,384]{1,0:T(8,128)(2,1)} %split.28), channel_id=1, source_target_pairs={{0,24},{8,16},{16,8},{24,0},{1,25},{9,17},{17,9},{25,1},{2,26},{10... | collective-permute-start | bytes 1769480 | tf_op jit(solution)/shard_map/ppermute | solution.py:953
  166.7 3.9 %slice-start = ((bf16[960,384]{1,0:T(8,128)(2,1)}), bf16[192,384]{1,0:T(8,128)(2,1)S(1)}, s32[]{:S(2)}) async-start(bf16[960,384]{1,0:T(8,128)(2,1)} %copy-done.3), calls=%async_computation.4 | async-start | bytes 294912 | tf_op jit(solution)/shard_map/slice | solution.py:1116
  166.7 25.9 %all-to-all-start.3 = ((bf16[8,72,768]{2,1,0:T(8,128)(2,1)}), bf16[8,72,768]{2,1,0:T(8,128)(2,1)S(1)}, u32[]{:S(2)}, u32[]{:S(2)}) async-start(bf16[8,72,768]{2,1,0:T(8,128)(2,1)} %merge.1), calls=%async_computation.3 | async-start | bytes 1769472 | tf_op jit(solution)/shard_map/all_to_all | solution.py:949
  171.1 0.8 copy-start.12
  186.1 17.1 %collective-permute-start.14 = (bf16[384,384]{1,0:T(8,128)(2,1)}, bf16[384,384]{1,0:T(8,128)(2,1)}, u32[]{:S(2)}, u32[]{:S(2)}) collective-permute-start(bf16[384,384]{1,0:T(8,128)(2,1)} %get-tuple-element.103), channel_id=1, source_target_pairs={{0,8},{8,0},{16,24},{24,16},{1,9},{9,1},{17,25},{25,17},{2,10},{10... | collective-permute-start | bytes 884744 | tf_op jit(solution)/shard_map/ppermute | solution.py:953
  186.6 21.8 %collective-permute-start.15 = (bf16[384,384]{1,0:T(8,128)(2,1)}, bf16[384,384]{1,0:T(8,128)(2,1)}, u32[]{:S(2)}, u32[]{:S(2)}) collective-permute-start(bf16[384,384]{1,0:T(8,128)(2,1)} %get-tuple-element.105), channel_id=1, source_target_pairs={{0,16},{8,24},{16,0},{24,8},{1,17},{9,25},{17,1},{25,9},{2,18},{10... | collective-permute-start | bytes 884744 | tf_op jit(solution)/shard_map/ppermute | solution.py:953
  189.2 20.1 %collective-permute-start.16 = (bf16[384,384]{1,0:T(8,128)(2,1)S(1)}, bf16[384,384]{1,0:T(8,128)(2,1)}, u32[]{:S(2)}, u32[]{:S(2)}) collective-permute-start(bf16[384,384]{1,0:T(8,128)(2,1)S(1)} %get-tuple-element.104), channel_id=1, source_target_pairs={{0,24},{8,16},{16,8},{24,0},{1,25},{9,17},{17,9},{25,1},{2,26},{10... | collective-permute-start | bytes 884744 | tf_op jit(solution)/shard_map/ppermute | solution.py:953
  192.6 0.9 copy-start.2
  193.5 5.2 %copy-start.4 = (bf16[768,384]{1,0:T(8,128)(2,1)S(1)}, bf16[768,384]{1,0:T(8,128)(2,1)}, u32[]{:S(2)}) copy-start(bf16[768,384]{1,0:T(8,128)(2,1)} %add_convert_fusion.2) | copy-start | bytes 1769476
  197.4 3.8 %collective-permute-start.20 = (f32[8,128]{1,0:T(8,128)}, f32[8,128]{1,0:T(8,128)S(1)}, u32[]{:S(2)}, u32[]{:S(2)}) collective-permute-start(f32[8,128]{1,0:T(8,128)} %get-tuple-element.102), channel_id=1, source_target_pairs={{0,8},{8,0},{16,24},{24,16},{1,9},{9,1},{17,25},{25,17},{2,10},{10... | collective-permute-start | bytes 12296 | tf_op jit(solution)/shard_map/ppermute | solution.py:953
  198.8 14.9 %collective-permute-start.17 = (bf16[192,384]{1,0:T(8,128)(2,1)S(1)}, bf16[192,384]{1,0:T(8,128)(2,1)S(1)}, u32[]{:S(2)}, u32[]{:S(2)}) collective-permute-start(bf16[192,384]{1,0:T(8,128)(2,1)S(1)} %get-tuple-element.106), channel_id=1, source_target_pairs={{0,2},{1,3},{2,0},{3,1},{4,6},{5,7},{6,4},{7,5},{8,10},{9,11},{10,... | collective-permute-start | bytes 442376 | tf_op jit(solution)/shard_map/ppermute | solution.py:953
  201.2 12.5 %collective-permute-start.18 = (bf16[192,384]{1,0:T(8,128)(2,1)S(1)}, bf16[192,384]{1,0:T(8,128)(2,1)S(1)}, u32[]{:S(2)}, u32[]{:S(2)}) collective-permute-start(bf16[192,384]{1,0:T(8,128)(2,1)S(1)} %get-tuple-element.108), channel_id=1, source_target_pairs={{0,4},{1,5},{2,6},{3,7},{4,0},{5,1},{6,2},{7,3},{8,12},{9,13},{10,... | collective-permute-start | bytes 442376 | tf_op jit(solution)/shard_map/ppermute | solution.py:953
  203.2 10.5 %collective-permute-start.19 = (bf16[192,384]{1,0:T(8,128)(2,1)S(1)}, bf16[192,384]{1,0:T(8,128)(2,1)}, u32[]{:S(2)}, u32[]{:S(2)}) collective-permute-start(bf16[192,384]{1,0:T(8,128)(2,1)S(1)} %get-tuple-element.107), channel_id=1, source_target_pairs={{0,6},{1,7},{2,4},{3,5},{4,2},{5,3},{6,0},{7,1},{8,14},{9,15},{10,... | collective-permute-start | bytes 442376 | tf_op jit(solution)/shard_map/ppermute | solution.py:953
  208.4 4.7 %collective-permute-start.21 = (f32[8,128]{1,0:T(8,128)S(1)}, f32[8,128]{1,0:T(8,128)S(1)}, u32[]{:S(2)}, u32[]{:S(2)}) collective-permute-start(f32[8,128]{1,0:T(8,128)S(1)} %add.88), channel_id=1, source_target_pairs={{0,16},{8,24},{16,0},{24,8},{1,17},{9,25},{17,1},{25,9},{2,18},{10... | collective-permute-start | bytes 12296 | tf_op jit(solution)/shard_map/ppermute | solution.py:953
  211.3 4.1 %copy-start.1 = (s32[4,8]{1,0:T(4,128)S(1)}, s32[4,8]{1,0:T(4,128)}, u32[]{:S(2)}) copy-start(s32[4,8]{1,0:T(4,128)} %param.16) | copy-start | bytes 388

commit v2 on v0

--- a/solution.py
+++ b/solution.py
@@ -141,7 +141,8 @@
 
 
 def attend_back_kernel(
-    core_ref, place_ref, to_ref, qkv_ref, g_ref, sums_ref, stats_ref, normed_ref, out_ref, gq_ref, g_sc, dq_sc, dk_sc, dv_sc
+    core_ref, place_ref, to_ref, qkv_ref, g_ref, sums_ref, stats_ref, normed_ref, mine_ref, other_ref, norm_ref,
+    wq_ref, wk_ref, wv_ref, gq_ref, keep_ref, send_ref, norms_ref, g_sc, dq_sc, dk_sc, dv_sc, packed_sc, back_sc,
 ):
     blocks, rows = g_ref.shape[0], g_ref.shape[1]
     for block in range(blocks):
@@ -176,20 +177,53 @@
         dq_sc[span, :] = jnp.concatenate(parts, axis=0).T * SCALE
     for kind, ref in enumerate((dq_sc, dk_sc, dv_sc)):
         grad = ref[...].astype(BF16)
-        out_ref[:, kind * PAIR : (kind + 1) * PAIR] = grad
+        packed_sc[:, kind * PAIR : (kind + 1) * PAIR] = grad
         turned = jnp.dot(grad.T, normed_ref[...], preferred_element_type=F32).astype(BF16)
         for strip in range(PAIR // STRIP):
             at = to_ref[(pl.program_id(0) * 3 + kind) * (PAIR // STRIP) + strip]
             at = pl.multiple_of(at * STRIP, STRIP)
             gq_ref[pl.ds(at, STRIP), :] = turned[strip * STRIP : (strip + 1) * STRIP]
 
-
-def attend_back(core, place, to, qkv, grad, sums, stats, normed):
+    step, half = pl.program_id(0), mine_ref.shape[1]
+    weights = jnp.concatenate([wq_ref[...], wk_ref[...], wv_ref[...]], axis=1)
+    back = dot(packed_sc[...], weights, (1, 1))
+
+    @pl.when(step == 0)
+    def _():
+        back_sc[...] = back
+
+    @pl.when(step > 0)
+    def _():
+        back_sc[...] += back
+
+    @pl.when(step == pl.num_programs(0) - 1)
+    def _():
+        norms_ref[...] = norm_ref[...]
+
+        @pl.loop(0, blocks)
+        def _(block):
+            for ref, out_ref, part in ((mine_ref, keep_ref, core_ref[0]), (other_ref, send_ref, 1 - core_ref[0])):
+                at = pl.multiple_of(place_ref[block] * rows + part * half, half)
+                grad = back_sc[pl.ds(at, half), :]
+                out_ref[block] = grad.astype(out_ref.dtype)
+                x = ref[block].astype(F32)
+                centred = x - jnp.mean(x, axis=-1, keepdims=True)
+                unit = centred * lax.rsqrt(jnp.mean(centred * centred, axis=-1, keepdims=True) + norm_eps)
+                norms_ref[0:1, :] += jnp.sum(grad * unit, axis=0, keepdims=True)
+                norms_ref[1:2, :] += jnp.sum(grad, axis=0, keepdims=True)
+
+
+def attend_back(core, place, to, qkv, grad, sums, stats, normed, mine, other, norm, w_qkv):
     pairs, length, _ = qkv.shape
     blocks, rows, _ = grad.shape
     width = normed.shape[1]
     area = length * length
     one = lambda i, c, p, t: (i, 0, 0)
+
+    def columns(kind):
+        size = width // PAIR
+        return pl.BlockSpec((width, PAIR), lambda i, core, p, t: (0, kind * size + core[0] * pairs + i))
+
     return pl.pallas_call(
         attend_back_kernel,
         grid_spec=pltpu.PrefetchScalarGridSpec(
@@ -201,92 +235,37 @@
                 pl.BlockSpec((1, PAIR, length), one),
                 pl.BlockSpec((1, 8, length), one),
                 fixed2(normed.shape),
-            ],
-            out_specs=[
-                pl.BlockSpec((length, 3 * PAIR), lambda i, c, p, t: (0, i)),
-                fixed2((pairs * 3 * PAIR, width)),
-            ],
-            scratch_shapes=[pltpu.VMEM((length, PAIR), BF16)] + [pltpu.VMEM((length, PAIR), F32)] * 3,
-        ),
-        out_shape=[
-            jax.ShapeDtypeStruct((length, pairs * 3 * PAIR), BF16),
-            jax.ShapeDtypeStruct((pairs * 3 * PAIR, width), BF16),
-        ],
-        cost_estimate=pl.CostEstimate(
-            flops=pairs * 40 * area * HEAD + 3 * length * width * width,
-            bytes_accessed=8 * length * width,
-            transcendentals=pairs * area,
-        ),
-        name="attend_back",
-    )(core, place, to, qkv, grad, sums, stats, normed)
-
-
-def normed_back_kernel(
-    core_ref, place_ref, back_ref, grad_ref, mine_ref, other_ref, norm_ref, wq_ref, wk_ref, wv_ref,
-    keep_ref, send_ref, sums_ref, w_sc,
-):
-    step = pl.program_id(0)
-    half = mine_ref.shape[1]
-    pairs = wq_ref.shape[1] // PAIR
-
-    @pl.when(step == 0)
-    def _():
-        sums_ref[...] = norm_ref[...]
-        for pair in range(pairs):
-            for kind, ref in enumerate((wq_ref, wk_ref, wv_ref)):
-                w_sc[:, (pair * 3 + kind) * PAIR : (pair * 3 + kind + 1) * PAIR] = ref[
-                    :, pair * PAIR : (pair + 1) * PAIR
-                ]
-
-    back = dot(grad_ref[...], w_sc[...], (1, 1))
-    for at in range(grad_ref.shape[0] // (2 * half)):
-        block = back_ref[step * (grad_ref.shape[0] // (2 * half)) + at]
-        low = back[2 * at * half : (2 * at + 1) * half]
-        high = back[(2 * at + 1) * half : (2 * at + 2) * half]
-        first = core_ref[0] == 0
-        mine, other = jnp.where(first, low, high), jnp.where(first, high, low)
-        keep_ref[block] = mine
-        send_ref[block] = other.astype(BF16)
-        for grad, ref in ((mine, mine_ref), (other, other_ref)):
-            x = ref[block].astype(F32)
-            centred = x - jnp.mean(x, axis=-1, keepdims=True)
-            unit = centred * lax.rsqrt(jnp.mean(centred * centred, axis=-1, keepdims=True) + norm_eps)
-            sums_ref[0:1, :] += jnp.sum(grad * unit, axis=0, keepdims=True)
-            sums_ref[1:2, :] += jnp.sum(grad, axis=0, keepdims=True)
-
-
-def normed_back(core, place, back, grad, mine, other, norm, w_qkv):
-    length, size = grad.shape
-    blocks, half, width = mine.shape
-    steps = 4
-    columns = [
-        pl.BlockSpec((width, size // 3), lambda i, core, p, b, kind=kind: (0, kind * 2 + core[0])) for kind in range(3)
-    ]
-    return pl.pallas_call(
-        normed_back_kernel,
-        grid_spec=pltpu.PrefetchScalarGridSpec(
-            num_scalar_prefetch=3,
-            grid=(steps,),
-            in_specs=[
-                pl.BlockSpec((length // steps, size), lambda i, c, p, b: (i, 0)),
                 fixed2(mine.shape),
                 fixed2(mine.shape),
                 fixed2(norm.shape),
-                *columns,
+                *(columns(kind) for kind in range(3)),
             ],
-            out_specs=[fixed2(mine.shape), fixed2(mine.shape), fixed2(norm.shape)],
-            scratch_shapes=[pltpu.VMEM((width, size), BF16)],
+            out_specs=[
+                fixed2((pairs * 3 * PAIR, width)),
+                fixed2(mine.shape),
+                fixed2(mine.shape),
+                fixed2(norm.shape),
+            ],
+            scratch_shapes=[
+                pltpu.VMEM((length, PAIR), BF16),
+                *[pltpu.VMEM((length, PAIR), F32)] * 3,
+                pltpu.VMEM((length, 3 * PAIR), BF16),
+                pltpu.VMEM((length, width), F32),
+            ],
         ),
         out_shape=[
+            jax.ShapeDtypeStruct((pairs * 3 * PAIR, width), BF16),
             jax.ShapeDtypeStruct(mine.shape, F32),
             jax.ShapeDtypeStruct(mine.shape, BF16),
             jax.ShapeDtypeStruct(norm.shape, F32),
         ],
         cost_estimate=pl.CostEstimate(
-            flops=2 * length * width * size, bytes_accessed=8 * length * width, transcendentals=0
-        ),
-        name="normed_back",
-    )(core, place, back, grad, mine, other, norm, w_qkv, w_qkv, w_qkv)
+            flops=pairs * 40 * area * HEAD + 6 * length * width * width,
+            bytes_accessed=8 * length * width,
+            transcendentals=pairs * area,
+        ),
+        name="attend_back",
+    )(core, place, to, qkv, grad, sums, stats, normed, mine, other, norm, w_qkv, w_qkv, w_qkv)
 
 
 def merge_kernel(keep_ref, other_ref, norm_ref, out_ref):
@@ -363,8 +342,8 @@
                 )
 
 
-def qkv_tiles(chip, found, keep, given, near):
-    size, width = keep.shape
+def qkv_tiles(chip, found, grad, given, near):
+    size, width = given.shape
     owned = 2 * size // near // STRIP
     shape = (owned * STRIP, width)
     return pl.pallas_call(
@@ -372,13 +351,13 @@
         grid_spec=pltpu.PrefetchScalarGridSpec(
             num_scalar_prefetch=2,
             grid=(near,),
-            in_specs=[fixed2(keep.shape), fixed2(keep.shape)],
+            in_specs=[fixed2(given.shape), fixed2(given.shape)],
             out_specs=[fixed2(shape)] * near,
         ),
         out_shape=[jax.ShapeDtypeStruct(shape, BF16)] * near,
-        cost_estimate=pl.CostEstimate(flops=size * width, bytes_accessed=8 * size * width, transcendentals=0),
+        cost_estimate=pl.CostEstimate(flops=size * width, bytes_accessed=size * width, transcendentals=0),
         name="qkv_tiles",
-    )(chip, found, keep, given)
+    )(chip, found, grad, given)
 
 
 def gelu_pair(u):
@@ -406,7 +385,8 @@
 
 
 def ff_kernel(seqs, plane, *refs):
-    me_ref, x_ref, att_ref, cot_ref, w_out_ref, gain_ref, shift_ref, up_ref, down_ref, *refs = refs
+    me_ref, x_ref, att_ref, cot_ref, w_out_ref, gain_ref, shift_ref, *refs = refs
+    ups, downs, refs = refs[:2], refs[2:4], refs[4:]
     out_ref, res_ref, *refs = refs
     ga_ref, norm_ref, gu_send, gu_keep, gd_send, gd_keep, gp_send, gp_keep, *refs = refs
     att_sc, residual_sc, normed_sc, normed_t, turned_sc, acc_out, acc_grad = refs
@@ -439,27 +419,33 @@
         acc_out[...] = jnp.zeros_like(acc_out)
         acc_grad[...] = jnp.zeros_like(acc_grad)
 
-    pre = jnp.dot(normed_sc[...], up_ref[...], preferred_element_type=F32)
+    up = jnp.concatenate([r[...] for r in ups], axis=1)
+    down = jnp.concatenate([r[...] for r in downs], axis=0)
+    pre = jnp.dot(normed_sc[...], up, preferred_element_type=F32)
     active, slope = gelu_pair(pre)
     active = active.astype(BF16)
-    grad_pre = (dot(cot_ref[...], down_ref[...], (1, 1)) * slope).astype(BF16)
-    acc_out[...] += jnp.dot(active, down_ref[...], preferred_element_type=F32)
-    acc_grad[...] += dot(grad_pre, up_ref[...], (1, 1))
+    grad_pre = (dot(cot_ref[...], down, (1, 1)) * slope).astype(BF16)
+    acc_out[...] += jnp.dot(active, down, preferred_element_type=F32)
+    acc_grad[...] += dot(grad_pre, up, (1, 1))
     grad_up = jnp.dot(normed_t[...], grad_pre, preferred_element_type=F32).astype(BF16)
     grad_down = jnp.dot(turned_sc[...], active, preferred_element_type=F32).astype(BF16)
-    for slot in range(near):
-        gd_send[slot, 0] = grad_down[slot * block : (slot + 1) * block]
-        gd_keep[slot, 0] = grad_down[(near + slot) * block : (near + slot + 1) * block]
-
-    @pl.when(step < near)
-    def _():
-        gu_send[0] = grad_up
-
-    @pl.when(step >= near)
-    def _():
-        gu_keep[0] = grad_up
-
-    @pl.when(step == plane - 1)
+    part = ups[0].shape[1]
+    for half in range(2):
+        spot = ((me_ref[0] >> 1) ^ half) & 1
+        cols = slice(half * part, (half + 1) * part)
+        for slot in range(near):
+            gd_send[slot, 0, spot, 0] = grad_down[slot * block : (slot + 1) * block, cols]
+            gd_keep[slot, 0, spot, 0] = grad_down[(near + slot) * block : (near + slot + 1) * block, cols]
+
+        @pl.when(step < near // 2)
+        def _():
+            gu_send[half] = grad_up[:, cols]
+
+        @pl.when(step >= near // 2)
+        def _():
+            gu_keep[half] = grad_up[:, cols]
+
+    @pl.when(step == near - 1)
     def _():
         residual = residual_sc[...]
         out_ref[...] = (residual + acc_out[...]).astype(BF16)
@@ -487,8 +473,8 @@
     hidden = w_up.shape[1]
     tokens, near, part, block = seqs * rows, plane // 2, hidden // plane, width // plane
 
-    def at(i, me):
-        return me[0] ^ (2 * (i % near) + jnp.where(i < near, 1, 0))
+    def at(i, me, half=0):
+        return me[0] ^ (4 * (i % (near // 2)) + 2 * half + jnp.where(i < near // 2, 1, 0))
 
     def fixed(shape):
         return pl.BlockSpec(shape, lambda i, me, n=len(shape): (0,) * n)
@@ -499,13 +485,15 @@
         ((tokens, width), F32, fixed((tokens, width))),
         (joined, BF16, fixed(joined)),
         ((8, width), F32, fixed((8, width))),
-        ((near, width, part), BF16, pl.BlockSpec((1, width, part), lambda i, me: (jnp.minimum(i, near - 1), 0, 0))),
-        ((near, width, part), BF16, pl.BlockSpec((1, width, part), lambda i, me: (jnp.maximum(i - near, 0), 0, 0))),
+        ((near, width, part), BF16, pl.BlockSpec((2, width, part), lambda i, me: (jnp.minimum(i, near // 2 - 1), 0, 0))),
+        ((near, width, part), BF16, pl.BlockSpec((2, width, part), lambda i, me: (jnp.maximum(i - near // 2, 0), 0, 0))),
         *[
             (
-                (near, plane, block, part),
+                (near, plane // 4, 2, 2, block, part),
                 BF16,
-                pl.BlockSpec((near, 1, block, part), lambda i, me: (0, at(i, me), 0, 0)),
+                pl.BlockSpec(
+                    (near, 1, 2, 1, block, part), lambda i, me: (0, at(i, me) >> 2, 0, at(i, me) & 1, 0, 0)
+                ),
             )
         ]
         * 2,
@@ -515,12 +503,14 @@
         functools.partial(ff_kernel, seqs, plane),
         grid_spec=pltpu.PrefetchScalarGridSpec(
             num_scalar_prefetch=1,
-            grid=(plane,),
+            grid=(near,),
             in_specs=[fixed((tokens, width))]
             + [fixed(joined), fixed((tokens, width)), fixed((width, width)), fixed((width,)), fixed((width,))]
             + [
                 pl.BlockSpec((width, part), lambda i, me: (0, at(i, me))),
+                pl.BlockSpec((width, part), lambda i, me: (0, at(i, me, 1))),
                 pl.BlockSpec((part, width), lambda i, me: (at(i, me), 0)),
+                pl.BlockSpec((part, width), lambda i, me: (at(i, me, 1), 0)),
             ],
             out_specs=[o[2] for o in outs],
             scratch_shapes=[
@@ -549,6 +539,8 @@
         gain,
         shift,
         w_up,
+        w_up,
+        w_down,
         w_down,
     )
 
@@ -603,7 +595,7 @@
     part = outs[0].shape[1]
 
     def both(a, b):
-        return (a.astype(F32) + b.astype(F32)).astype(BF16)
+        return a + b
 
     @pl.when(step < batch)
     def _():
@@ -617,7 +609,8 @@
             for k in range(near):
                 total = both(down_a[k], down_b[k])
                 slab = total.shape[0] * total.shape[1]
-                down_outs[far][k * slab : (k + 1) * slab] = total.reshape(slab, part)
+                target, at = down_outs[far in (1, 2)], (far > 1) * near * slab + k * slab
+                target[at : at + slab] = total.reshape(slab, part)
 
     @pl.when(step == 2 * batch)
     def _():
@@ -636,7 +629,7 @@
     )
     proj_spec = pl.BlockSpec((near, block, width), lambda i, m: (0, 0, 0))
     last = lambda i, m: (jnp.where(i < batch, i, jnp.where(i < 2 * batch, batch - 1, batch)), 0)
-    down_shape = (near * few * block, part)
+    down_shape = (2 * near * few * block, part)
     return pl.pallas_call(
         functools.partial(add_pair_kernel, near, batch),
         grid_spec=pltpu.PrefetchScalarGridSpec(
@@ -644,10 +637,10 @@
             grid=(2 * batch + 1,),
             in_specs=[up_spec] * 2 + [down_spec] * 2 + [proj_spec] * 2,
             out_specs=[pl.BlockSpec((tall, part), last)] * near
-            + [pl.BlockSpec(down_shape, lambda i, m: (0, 0))] * batch,
+            + [pl.BlockSpec(down_shape, lambda i, m: (0, 0))] * 2,
         ),
         out_shape=[jax.ShapeDtypeStruct((width + tall, part), BF16)] * near
-        + [jax.ShapeDtypeStruct(down_shape, BF16)] * batch,
+        + [jax.ShapeDtypeStruct(down_shape, BF16)] * 2,
         cost_estimate=pl.CostEstimate(
             flops=near * 9 * tall * part, bytes_accessed=6 * near * 9 * tall * part, transcendentals=0
         ),
@@ -663,22 +656,71 @@
 
 
 def over_batch(stacked):
-    size = lax.axis_size("batch")
-    mine = lax.axis_index("batch")
-    if size > 4:
-        return lax.psum_scatter(stacked, "batch", scatter_dimension=0, tiled=True)[0].astype(F32)
-    parts = [lax.dynamic_index_in_dim(stacked, mine, 0, False)]
-    for bit in range(1, size):
-        block = lax.dynamic_index_in_dim(stacked, mine ^ bit, 0, False)
-        parts.append(swap(block, "batch", size, bit))
-    return add_all(parts)
+    return lax.psum_scatter(stacked, "batch", scatter_dimension=0, tiled=True)[0].astype(F32)
 
 
 def over_plane(tiles, plane):
-    parts = [tiles[0]]
-    for k in range(1, len(tiles)):
-        parts.append(swap(tiles[k], ("pb", "ka"), plane, 2 * k))
-    return add_all(parts)
+    return [tiles[0]] + [swap(tiles[k], ("pb", "ka"), plane, 2 * k) for k in range(1, len(tiles))]
+
+
+def pack_kernel(batch, mine_ref, *refs):
+    early_ref, late_ref, *outs, side_sc = refs
+    width, slab = side_sc.shape[0], outs[0].shape[0] // 2
+    block = (early_ref.shape[0] - width) // 2
+    proj = jnp.concatenate([early_ref[width : width + block], early_ref[width + block :]], axis=1)
+    side_sc[...] = jnp.concatenate([late_ref[...], proj], axis=0).T
+    for far in range(batch):
+        at = pl.multiple_of((mine_ref[0] ^ far) * slab, slab)
+        outs[far][:slab] = early_ref[pl.ds(at, slab), :]
+        outs[far][slab:] = side_sc[pl.ds(at, slab), :]
+
+
+def pack(mine, early, late, batch):
+    width, part = late.shape[1], early.shape[1]
+    shape = (2 * width // batch, part)
+    return pl.pallas_call(
+        functools.partial(pack_kernel, batch),
+        grid_spec=pltpu.PrefetchScalarGridSpec(
+            num_scalar_prefetch=1,
+            grid=(1,),
+            in_specs=[fixed2(early.shape), fixed2(late.shape)],
+            out_specs=[fixed2(shape)] * batch,
+            scratch_shapes=[pltpu.VMEM((width, part), BF16)],
+        ),
+        out_shape=[jax.ShapeDtypeStruct(shape, BF16)] * batch,
+        cost_estimate=pl.CostEstimate(flops=8 * width * part, bytes_accessed=20 * width * part, transcendentals=0),
+        name="pack",
+    )(mine, early, late)
+
+
+def finish_kernel(*refs):
+    parts, (up_ref, qkv_ref, proj_ref) = refs[:-3], refs[-3:]
+    slab, owned = qkv_ref.shape
+    total = add_all([r[...] for r in parts])
+    up_ref[...] = total[:slab]
+    qkv_ref[...] = total[slab:, :owned]
+    proj_ref[...] = total[slab:, owned:]
+
+
+def finish_down_kernel(*refs):
+    parts, down_ref = refs[:-1], refs[-1]
+    total = add_all([r[...] for r in parts])
+    block, part = down_ref.shape[1], total.shape[1]
+    for at in range(total.shape[0] // block):
+        down_ref[at * part : (at + 1) * part] = total[at * block : (at + 1) * block].T
+
+
+def finish(kernel, parts, shapes):
+    rows, part = parts[0].shape
+    return pl.pallas_call(
+        kernel,
+        grid=(1,),
+        in_specs=[fixed2(a.shape) for a in parts],
+        out_specs=[fixed2(s) for s in shapes],
+        out_shape=[jax.ShapeDtypeStruct(s, F32) for s in shapes],
+        cost_estimate=pl.CostEstimate(flops=8 * rows * part, bytes_accessed=16 * rows * part, transcendentals=0),
+        name="finish",
+    )(*parts)
 
 
 def shards(
@@ -700,14 +742,12 @@
     planes = ("pb", "ka")
     batch = lax.axis_size("batch")
     near = plane // 2
-    few = batch <= 4
+    few = batch == 4
     me = lax.axis_index(planes)
     scalar = lambda value: value.astype(jnp.int32).reshape(1)
     core, chip = scalar(me & 1), scalar(me >> 1)
     part, block, slab = hidden // plane, width // plane, width // batch
     place = lax.dynamic_index_in_dim(block_place, me >> 1, 0, False)
-    spots = jnp.arange(plane, dtype=jnp.int32)
-    back = jnp.sum(jnp.where(place[None] == spots[:, None], spots[None], 0), axis=1)
     to, found = [jnp.where(core == 0, *(jnp.array(t, jnp.int32) for t in both)) for both in strips(width, plane)]
 
     mine = exchange(inputs.reshape(plane, seqs * rows // plane, width))
@@ -717,6 +757,7 @@
         scalar(me), inputs, exchange(attended), cotangent, w_out, ln2_gain, ln2_shift, w_up, w_down, plane
     )
     grad_att = exchange(grad_att)
+    grads[2:4] = [g.reshape(near, plane, block, part) for g in grads[2:4]]
     up, down, proj = [(grads[2 * i + 1], swap(grads[2 * i], planes, plane, 1)) for i in range(3)]
     if few:
         sums_up = add_pair(scalar(lax.axis_index("batch")), up, down, proj, batch)
@@ -731,57 +772,48 @@
             ).astype(BF16)
             for k in range(near)
         ]
-    tile = over_plane(tiles, plane).astype(BF16)
+    early = add_all(over_plane(tiles, plane)).astype(BF16)
     if few:
-        down_parts = [down[0]] + [swap(down[bit], "batch", batch, bit) for bit in range(1, batch)]
-        down_parts = [d.reshape(near, -1, part) for d in down_parts]
-        down_tiles = [add_all([d[k] for d in down_parts]).astype(BF16) for k in range(near)]
-
-    grad_packed, grad_qkv = attend_back(core, place, to, packed, grad_att, sums, stats, normed1)
-    grad_packed, tile = lax.optimization_barrier((grad_packed, tile))
-    stay = grad_qkv.shape[0] // 2
-    given = swap(grad_qkv[stay:], planes, plane, 1)
-    keep, send, norm = normed_back(
-        core, place, back, grad_packed, mine, other, norm2, w_qkv
+        down = add_all([down[0], swap(down[1], "batch", batch, 1)]).astype(BF16)
+
+    grad_qkv, keep, send, norm = attend_back(
+        core, place, to, packed, grad_att, sums, stats, normed1, mine, other, norm2, w_qkv
     )
-    tiles = qkv_tiles(chip, found, grad_qkv[:stay], given, near)
+    given = swap(grad_qkv[grad_qkv.shape[0] // 2 :], planes, plane, 1)
+    if few:
+        given, early, down = lax.optimization_barrier((given, early, down))
+        down = jnp.split(down, 2)
+        down[1] = swap(down[1], "batch", batch, 3)
+    late = qkv_tiles(chip, found, grad_qkv, given, near)
+    keep, late = lax.optimization_barrier((keep, late))
     returned = exchange(merge(keep, swap(send, planes, plane, 1), norm))
+    late = add_all(over_plane(late, plane)).astype(BF16)
+    owned = 3 * width // plane
     if few:
-        returned, down_tiles = lax.optimization_barrier((returned, down_tiles))
-    grad_inputs, norm = first_norm_back(inputs, ln1_gain, returned, grad_res)
-
+        along = scalar(lax.axis_index("batch"))
+        sums = pack(along, early, late, batch)
+        sums = [sums[0]] + [swap(sums[bit], "batch", batch, bit) for bit in range(1, batch)]
+        returned, down = lax.optimization_barrier((returned, add_all(down).astype(BF16)))
+        down = over_plane(jnp.split(down, near), plane)
+    grad_inputs, norms = first_norm_back(inputs, ln1_gain, returned, grad_res)
     if few:
-        grad_down = over_plane(down_tiles, plane)
+        for bit in (1, 2):
+            norms = norms + swap(norms, "batch", batch, bit)
+        grad_up, grad_qkv, grad_proj = finish(finish_kernel, sums, [(slab, part), (slab, owned), (slab, block)])
+        (grad_down,) = finish(finish_down_kernel, down, [(hidden // batch, block)])
     else:
-        cut = batch // plane
+        tile, cut = early, batch // plane
         down_tile = tile[width : 2 * width].reshape(plane, block, cut, part // cut).transpose(0, 2, 1, 3)
-        grad_down = over_batch(down_tile.reshape(batch, block, part // cut))
-    proj_tile = tile[-2 * block :].reshape(2, block, part).transpose(1, 0, 2).reshape(block, batch, slab)
-    proj_tile = proj_tile.transpose(1, 0, 2)
-    up_tile = tile[:width].reshape(batch, slab, part)
-    if few:
-        joined = jnp.concatenate([up_tile, proj_tile.reshape(batch, block * slab // part, part)], axis=1)
-        summed = over_batch(joined)
-        grad_up, grad_proj = summed[:slab], summed[slab:].reshape(block, slab)
-    else:
-        grad_up, grad_proj = over_batch(up_tile), over_batch(proj_tile)
-    grad_down = grad_down.reshape(-1, block, min(part, hidden // batch)).transpose(0, 2, 1).reshape(-1, block)
-    grad_proj = grad_proj.T
-
-    owned = 3 * width // plane
-    tile = over_plane(tiles, plane).astype(BF16)
-    qkv_tile = tile.reshape(owned, batch, slab).transpose(1, 0, 2)
-    if few:
-        norm_tile = jnp.pad(norm.astype(BF16), ((0, 8), (0, slab - PAIR)))
-        norm_tile = jnp.broadcast_to(norm_tile[None], (batch, *norm_tile.shape))
-        summed = over_batch(jnp.concatenate([qkv_tile, norm_tile], axis=1))
-        grad_qkv, norms = summed[:owned], summed[owned:]
-    else:
-        grad_qkv, norms = over_batch(qkv_tile), lax.psum(norm, "batch")
+        grad_down = over_batch(down_tile.reshape(batch, block, part // cut)).T
+        proj_tile = tile[-2 * block :].reshape(2, block, part).transpose(1, 0, 2).reshape(block, batch, slab)
+        grad_proj = over_batch(proj_tile.transpose(1, 0, 2)).T
+        grad_up = over_batch(tile[:width].reshape(batch, slab, part))
+        grad_qkv = over_batch(late.reshape(owned, batch, slab).transpose(1, 0, 2)).T
+        norms = lax.psum(norms, "batch")
     return (
         outputs.reshape(inputs.shape),
         grad_inputs.reshape(inputs.shape),
-        grad_qkv.T,
+        grad_qkv,
         grad_proj,
         grad_up,
         grad_down,

time: 256 us -> 213 us (0.83); the launches traced: 251 us -> 212 us
  waiting for transfers between devices: 60.6 us -> 30.2 us
  starting transfers between devices: 32.8 us -> 29.3 us
  other arithmetic: 10.6 us -> 7.42 us
  local copies, waits for them, and re-layouts: 13.1 us -> 10.1 us
    ppermute x24 -> x22, waiting for transfers between devices: 60.6 us -> 30.2 us  [swap(): return lax.ppermute(values, axes, [(i, i ^ bit) for i in range(size)])]
    pallas_call x1, Pallas kernels: 18.5 us -> 26 us  [attend_back(): pl.pallas_call(attend_back_kernel, grid_spec=pltpu.PrefetchScalarGridSpec...]
    pallas_call x1, Pallas kernels: 31.6 us -> 27 us  [feed_forward(): pl.pallas_call(functools.partial(ff_kernel, seqs, plane), grid_spec=pltpu...]
    ppermute x24 -> x22, starting transfers between devices: 25.2 us -> 21.7 us  [swap(): return lax.ppermute(values, axes, [(i, i ^ bit) for i in range(size)])]
    reshape x8 -> x0, local copies, waits for them, and re-layouts: 2.61 us -> none  [the longest x2 0.82 us: shards(): grad_up, grad_proj = (summed[:slab], summed[slab:].reshape(block, slab))]
    pallas_call x1 -> x3, Pallas kernels: 8.13 us -> 6.68 us  [the longest x2 4.21 us: finish(): pl.pallas_call(kernel, grid=(1,), in_specs=[fixed2(a.shape) for a in part...]
  transfers between devices with their start and end apart: 26 -> 24, of which waited for: 7 -> 9; matrix products, arithmetic and copies ran while one was open for 6% -> 5% of each run, Pallas kernels for 15% -> 24%
where the time goes in v2:
time: 213 us; the launch traced here: 212 us
  Pallas kernels  101 us (47%)
  blocking collectives  33 us (15%)
  waiting for transfers between devices  30.2 us (14%)
  starting transfers between devices  29.3 us (14%)
  local copies, waits for them, and re-layouts  10.1 us (5%)
  other arithmetic  7.42 us (3%)
    all_to_all x2, blocking collectives, exchange(): return lax.all_to_all(blocks, ('pb', 'ka'), 0, 0, tiled=True)  33 us
    ppermute x22, waiting for transfers between devices, swap(): return lax.ppermute(values, axes, [(i, i ^ bit) for i in range(size)])  30.2 us
    pallas_call x1, Pallas kernels, feed_forward(): pl.pallas_call(functools.partial(ff_kernel, seqs, plane), grid_spec=pltpu...  27 us
    pallas_call x1, Pallas kernels, attend_back(): pl.pallas_call(attend_back_kernel, grid_spec=pltpu.PrefetchScalarGridSpec...  26 us
    pallas_call x1, Pallas kernels, attend(): pl.pallas_call(attend_kernel, grid_spec=pltpu.PrefetchScalarGridSpec(num_...  21.8 us
    ppermute x22, starting transfers between devices, swap(): return lax.ppermute(values, axes, [(i, i ^ bit) for i in range(size)])  21.7 us
    pallas_call x1, Pallas kernels, add_pair(): pl.pallas_call(functools.partial(add_pair_kernel, near, batch), grid_spec...  9.4 us
    all_to_all x2, starting transfers between devices, exchange(): return lax.all_to_all(blocks, ('pb', 'ka'), 0, 0, tiled=True)  7.58 us
  transfers between devices with their start and end apart: 24, of which 9 were waited for; matrix products, arithmetic and copies ran while one was open for 5% of the time, Pallas kernels for 24%

profile of v2, /device:TPU:0, one launch (start us, length us, event | category | flops | bytes accessed | tf_op | source)
XLA Modules:
  0.0 212.1 jit_solution(2576424425213894697)
XLA Ops:
  0.6 0.0 copy-start
  0.6 17.0 %all_to_all.20.mine_ref = bf16[8,64,768]{2,1,0:T(8,128)(2,1)S(1)} all-to-all(bf16[8,64,768]{2,1,0:T(8,128)(2,1)} %bitcast.14), channel_id=1, replica_groups=mesh['batch'=4,'pb'=2,'ka'=4] {'pb','ka'}, dimensions={0} | all-to-all | bytes 1572864 | tf_op jit(solution)/shard_map/all_to_all | solution.py:584
  17.6 0.6 dynamic-slice_bitcast_fusion.place_ref
  18.3 1.6 collective-permute-done.other_ref
  19.9 0.9 copy-done.17
  20.8 21.8 %attend.1 = (bf16[8,128,384]{2,1,0:T(8,128)(2,1)}, bf16[1024,768]{1,0:T(8,128)(2,1)}, bf16[3,1024,384]{2,1,0:T(8,128)(2,1)}, f32[3,128,1024]{2,1,0:T(8,128)}, f32[3,8,1024]{2,1,0:T(8,128)}) custom-call(s32[1]{0:T(128)} %bitcast.2.core_ref, s32[8]{0:T(128)} %dynamic-slice_bitcast_fusion.place_ref, bf16[8,64,768]{2,1,0:T(8,128)(2,1)} %copy-done.6, ...), custom_call_target="tpu_custom_call" | custom-call | flops 5033164800 | bytes 6291456 | tf_op jit(solution)/shard_map/attend/pallas_call | solution.py:111
  42.7 16.0 %all_to_all.21.refs_2_ = bf16[8,128,384]{2,1,0:T(8,128)(2,1)} all-to-all(bf16[8,128,384]{2,1,0:T(8,128)(2,1)} %get-tuple-element.62), channel_id=1, replica_groups=mesh['batch'=4,'pb'=2,'ka'=4] {'pb','ka'}, dimensions={0} | all-to-all | bytes 1572864 | tf_op jit(solution)/shard_map/all_to_all | solution.py:584
  58.6 27.0 %feed_forward.1 = (bf16[512,768]{1,0:T(8,128)(2,1)}, f32[512,768]{1,0:T(8,128)}, bf16[8,128,384]{2,1,0:T(8,128)(2,1)}, f32[8,768]{1,0:T(8,128)}, bf16[4,768,384]...) custom-call(s32[1]{0:T(128)} %bitcast.refs_0_, ...), custom_call_target="tpu_custom_call" | custom-call | flops 16307453952 | bytes 18874368 | tf_op jit(solution)/shard_map/feed_forward/pallas_call | solution.py:502
  85.7 0.1 collective-permute-start.1
  85.8 0.5 collective-permute-start.2
  86.3 3.8 %all-to-all-start.2 = ((bf16[8,128,384]{2,1,0:T(8,128)(2,1)}), bf16[8,128,384]{2,1,0:T(8,128)(2,1)S(1)}, u32[]{:S(2)}, u32[]{:S(2)}) async-start(bf16[8,128,384]{2,1,0:T(8,128)(2,1)} %get-tuple-element.65), calls=%async_computation.2 | async-start | bytes 1572864 | tf_op jit(solution)/shard_map/all_to_all | solution.py:584
  90.1 0.2 collective-permute-start.3
  90.3 0.5 broadcast_select_fusion.1.to_ref
  90.8 0.5 broadcast_select_fusion.found_ref
  91.3 3.7 %collective-permute-done.3.refs_6_ = bf16[4,96,768]{2,1,0:T(8,128)(2,1)} collective-permute-done((bf16[4,96,768]{2,1,0:T(8,128)(2,1)}, bf16[4,96,768]{2,1,0:T(8,128)(2,1)}, u32[]{:S(2)}, u32[]{:S(2)}) %collective-permute-start.3) | collective-permute-done | bytes 589856 | tf_op jit(solution)/shard_map/ppermute | solution.py:588
  95.0 1.4 copy-done.3
  96.4 9.4 %add_pair.1 = (bf16[960,384]{1,0:T(8,128)(2,1)}, bf16[960,384]{1,0:T(8,128)(2,1)}, bf16[960,384]{1,0:T(8,128)(2,1)}, bf16[960,384]{1,0:T(8,128)(2,1)}, bf16[1536...) custom-call(s32[1]{0:T(128)} %bitcast.8.refs_0_.mine_ref, bf16[4,768,384]{2,1,0:T(8,128)(2,1)} %get-tuple-element.66.refs_1_, ...), custom_call_target="tpu_custom_call" | custom-call | flops 2654208 | bytes 15925248 | tf_op jit(solution)/shard_map/add_pair/pallas_call | solution.py:633
  105.9 1.6 collective-permute-start.8
  107.5 1.4 collective-permute-start.5
  108.9 0.6 collective-permute-start.6
  109.5 1.5 collective-permute-start.7
  111.0 26.0 %attend_back.1 = (bf16[1152,768]{1,0:T(8,128)(2,1)}, f32[8,64,768]{2,1,0:T(8,128)}, bf16[8,64,768]{2,1,0:T(8,128)(2,1)}, f32[8,768]{1,0:T(8,128)}) custom-call(s32[1]{0:T(128)} %bitcast.2.core_ref, s32[8]{0:T(128)} %dynamic-slice_bitcast_fusion.place_ref, s32[36]{0:T(128)} %broadcast_select_fusion.1.to_ref, bf16[3,1024,384]{2,1,0:T(8,128)(2,1)} %get-tuple-element.64.qkv_ref, ...), custom_call_target="tpu_custom_call" | custom-call | flops 11676942336 | bytes 6291456 | tf_op jit(solution)/shard_map/attend_back/pallas_call | solution.py:227
  137.0 1.3 slice.6
  138.3 0.1 collective-permute-start.4
  138.4 0.5 collective-permute-start.9
  138.9 4.2 %collective-permute-done.7 = bf16[960,384]{1,0:T(8,128)(2,1)} collective-permute-done((bf16[960,384]{1,0:T(8,128)(2,1)}, bf16[960,384]{1,0:T(8,128)(2,1)}, u32[]{:S(2)}, u32[]{:S(2)}) %collective-permute-start.7) | collective-permute-done | bytes 737312 | tf_op jit(solution)/shard_map/ppermute | solution.py:588
  143.1 2.8 %add_convert_fusion.1.refs_0_ = bf16[960,384]{1,0:T(8,128)(2,1)} fusion(bf16[960,384]{1,0:T(8,128)(2,1)} %collective-permute-done.7, bf16[960,384]{1,0:T(8,128)(2,1)} %collective-permute-done.6, bf16[960,384]{1,0:T(8,128)(2,1)} %collective-permute-done.5, bf16[960,384]{1,0:T(8,128)(2,1)S(1)} %copy-done.8), kind=kLoop, calls=%fused_computation.1 | loop fusion | flops 2949120 | bytes 3686400 | tf_op jit(solution)/shard_map/convert_element_type | solution.py:775
  145.9 0.3 add_convert_fusion
  146.2 0.9 copy-done.5
  147.2 3.7 %qkv_tiles.1 = (bf16[288,768]{1,0:T(8,128)(2,1)}, bf16[288,768]{1,0:T(8,128)(2,1)}, bf16[288,768]{1,0:T(8,128)(2,1)}, bf16[288,768]{1,0:T(8,128)(2,1)}) custom-call(s32[1]{0:T(128)} %bitcast.11.chip_ref, s32[36]{0:T(128)} %broadcast_select_fusion.found_ref, bf16[1152,768]{1,0:T(8,128)(2,1)} %get-tuple-element.84.keep_ref, bf16[576,768]{1,0:T(8,128)(2,1)} %copy-done.5), custom_call_target="tpu_custom_call" | custom-call | flops 442368 | bytes 442368 | tf_op jit(solution)/shard_map/qkv_tiles/pallas_call | solution.py:349
  150.8 1.4 collective-permute-start.11
  152.2 0.6 collective-permute-start.12
  152.8 1.5 collective-permute-start.13
  154.3 0.1 split.19
  154.4 2.5 %collective-permute-start.10 = (bf16[768,384]{1,0:T(8,128)(2,1)S(1)}, bf16[768,384]{1,0:T(8,128)(2,1)S(1)}, u32[]{:S(2)}, u32[]{:S(2)}) collective-permute-start(bf16[768,384]{1,0:T(8,128)(2,1)S(1)} %split.19), channel_id=1, source_target_pairs={{0,24},{8,16},{16,8},{24,0},{1,25},{9,17},{17,9},{25,1},{2,26},{10... | collective-permute-start | bytes 1769480 | tf_op jit(solution)/shard_map/ppermute | solution.py:588
  156.9 2.8 %merge.1 = bf16[8,72,768]{2,1,0:T(8,128)(2,1)} custom-call(f32[8,64,768]{2,1,0:T(8,128)} %get-tuple-element.96.keep_ref, bf16[8,64,768]{2,1,0:T(8,128)(2,1)} %collective-permute-done.9.other_ref, f32[8,768]{1,0:T(8,128)} %get-tuple-element.98.norm_ref), custom_call_target="tpu_custom_call" | custom-call | flops 393216 | bytes 3145728 | tf_op jit(solution)/shard_map/merge/pallas_call | solution.py:283
  159.7 3.8 %all-to-all-start.3 = ((bf16[8,72,768]{2,1,0:T(8,128)(2,1)}), bf16[8,72,768]{2,1,0:T(8,128)(2,1)S(1)}, u32[]{:S(2)}, u32[]{:S(2)}) async-start(bf16[8,72,768]{2,1,0:T(8,128)(2,1)} %merge.1), calls=%async_computation.3 | async-start | bytes 1769472 | tf_op jit(solution)/shard_map/all_to_all | solution.py:584
  163.5 2.1 collective-permute-done.12
  165.6 9.6 %collective-permute-done.13 = bf16[288,768]{1,0:T(8,128)(2,1)} collective-permute-done((bf16[288,768]{1,0:T(8,128)(2,1)}, bf16[288,768]{1,0:T(8,128)(2,1)}, u32[]{:S(2)}, u32[]{:S(2)}) %collective-permute-start.13) | collective-permute-done | bytes 442400 | tf_op jit(solution)/shard_map/ppermute | solution.py:588
  175.2 2.4 %add_convert_fusion.3.refs_1_ = bf16[288,768]{1,0:T(8,128)(2,1)} fusion(bf16[288,768]{1,0:T(8,128)(2,1)} %collective-permute-done.13, bf16[288,768]{1,0:T(8,128)(2,1)} %collective-permute-done.12, bf16[288,768]{1,0:T(8,128)(2,1)} %collective-permute-done.11, bf16[288,768]{1,0:T(8,128)(2,1)} %get-tuple-element.104), kind=kLoop, calls=%fused_computation.3 | loop fusion | flops 1769472 | bytes 2211840 | tf_op jit(solution)/shard_map/convert_element_type | solution.py:790
  177.6 2.5 %pack.1 = (bf16[384,384]{1,0:T(8,128)(2,1)}, bf16[384,384]{1,0:T(8,128)(2,1)}, bf16[384,384]{1,0:T(8,128)(2,1)}, bf16[384,384]{1,0:T(8,128)(2,1)}) custom-call(s32[1]{0:T(128)} %bitcast.8.refs_0_.mine_ref, bf16[960,384]{1,0:T(8,128)(2,1)} %add_convert_fusion.1.refs_0_, bf16[288,768]{1,0:T(8,128)(2,1)} %add_convert_fusion.3.refs_1_), custom_call_target="tpu_custom_call" | custom-call | flops 2359296 | bytes 5898240 | tf_op jit(solution)/shard_map/pack/pallas_call | solution.py:681
  180.0 0.4 collective-permute-start.14
  180.5 2.6 %collective-permute-start.15 = (bf16[384,384]{1,0:T(8,128)(2,1)}, bf16[384,384]{1,0:T(8,128)(2,1)}, u32[]{:S(2)}, u32[]{:S(2)}) collective-permute-start(bf16[384,384]{1,0:T(8,128)(2,1)} %get-tuple-element.110), channel_id=1, source_target_pairs={{0,16},{8,24},{16,0},{24,8},{1,17},{9,25},{17,1},{25,9},{2,18},{10... | collective-permute-start | bytes 884744 | tf_op jit(solution)/shard_map/ppermute | solution.py:588
  183.1 1.4 collective-permute-start.16
  184.4 0.2 add_convert_fusion.2
  184.6 0.9 copy-done.2
  185.5 3.8 %first_norm_back.1 = (bf16[512,768]{1,0:T(8,128)(2,1)}, f32[8,128]{1,0:T(8,128)}) custom-call(bf16[512,768]{1,0:T(8,128)(2,1)} %bitcast.16, f32[768]{0:T(1024)} %gain_ref.3, bf16[8,72,768]{2,1,0:T(8,128)(2,1)} %copy-done.2, f32[512,768]{1,0:T(8,128)} %get-tuple-element.101.res_ref), custom_call_target="tpu_custom_call" | custom-call | flops 7864320 | bytes 4718592 | tf_op jit(solution)/shard_map/first_norm_back/pallas_call | solution.py:572
  189.4 0.8 collective-permute-start.20
  190.1 0.7 fusion
  190.8 1.4 collective-permute-start.17
  192.3 0.2 collective-permute-done.14.refs_1_
  192.4 1.3 collective-permute-start.18
  193.7 1.3 collective-permute-done.20
  195.0 1.4 collective-permute-start.19
  196.4 0.7 add.47
  197.1 5.1 %collective-permute-done.15.refs_2_ = bf16[384,384]{1,0:T(8,128)(2,1)} collective-permute-done((bf16[384,384]{1,0:T(8,128)(2,1)}, bf16[384,384]{1,0:T(8,128)(2,1)}, u32[]{:S(2)}, u32[]{:S(2)}) %collective-permute-start.15) | collective-permute-done | bytes 294944 | tf_op jit(solution)/shard_map/ppermute | solution.py:588
  202.3 2.2 %finish.2 = (f32[192,384]{1,0:T(8,128)}, f32[192,288]{1,0:T(8,128)}, f32[192,96]{1,0:T(8,128)}) custom-call(bf16[384,384]{1,0:T(8,128)(2,1)} %get-tuple-element.108.refs_0_, bf16[384,384]{1,0:T(8,128)(2,1)} %copy-done.9, bf16[384,384]{1,0:T(8,128)(2,1)} %collective-permute-done.15.refs_2_, bf16[384,384]{1,0:T(8,128)(2,1)} %collective-permute-done.16.refs_3_), custom_call_target="tpu_custom_call" | custom-call | flops 1179648 | bytes 2359296 | tf_op jit(solution)/shard_map/finish/pallas_call | solution.py:715
  204.4 2.3 %collective-permute-done.21 = f32[8,128]{1,0:T(8,128)S(1)} collective-permute-done((f32[8,128]{1,0:T(8,128)S(1)}, f32[8,128]{1,0:T(8,128)S(1)}, u32[]{:S(2)}, u32[]{:S(2)}) %collective-permute-start.21) | collective-permute-done | bytes 4128 | tf_op jit(solution)/shard_map/ppermute | solution.py:588
  206.8 0.6 slice.7
  207.4 0.6 copy-done.10
  208.0 0.0 copy-done.11
  208.1 0.1 copy-done.12
  208.1 2.1 finish.3
  210.2 1.9 copy.22
  (46 shorter events, 0.1 us)
Async XLA Ops:
  0.6 17.0 %copy-start = (s32[4,8]{1,0:T(4,128)S(1)}, s32[4,8]{1,0:T(4,128)}, u32[]{:S(2)}) copy-start(s32[4,8]{1,0:T(4,128)} %param.16) | copy-start | bytes 388
  17.6 2.3 %copy-start.6 = (bf16[8,64,768]{2,1,0:T(8,128)(2,1)}, bf16[8,64,768]{2,1,0:T(8,128)(2,1)S(1)}, u32[]{:S(2)}) copy-start(bf16[8,64,768]{2,1,0:T(8,128)(2,1)S(1)} %all_to_all.20.mine_ref) | copy-start | bytes 2359300
  17.6 2.3 %collective-permute-start = (bf16[8,64,768]{2,1,0:T(8,128)(2,1)S(1)}, bf16[8,64,768]{2,1,0:T(8,128)(2,1)S(1)}, u32[]{:S(2)}, u32[]{:S(2)}) collective-permute-start(bf16[8,64,768]{2,1,0:T(8,128)(2,1)S(1)} %all_to_all.20.mine_ref), channel_id=1, source_target_pairs={{0,1},{1,0},{2,3},{3,2},{4,5},{5,4},{6,7},{7,6},{8,9},{9,8},{10,11... | collective-permute-start | bytes 2359304 | tf_op jit(solution)/shard_map/ppermute | solution.py:588
  19.9 0.9 copy-start.17
  85.7 4.6 %copy-start.15 = (s32[36]{0:T(128)S(1)}, s32[36]{0:T(128)}, u32[]{:S(2)}) copy-start(s32[36]{0:T(128)} %constant.31.clone) | copy-start | bytes 436
  85.7 4.6 %copy-start.16 = (s32[36]{0:T(128)S(1)}, s32[36]{0:T(128)}, u32[]{:S(2)}) copy-start(s32[36]{0:T(128)} %constant.32.clone) | copy-start | bytes 436
  85.7 5.1 %copy-start.13 = (s32[36]{0:T(128)S(1)}, s32[36]{0:T(128)}, u32[]{:S(2)}) copy-start(s32[36]{0:T(128)} %constant.33.clone) | copy-start | bytes 436
  85.7 5.1 %copy-start.14 = (s32[36]{0:T(128)S(1)}, s32[36]{0:T(128)}, u32[]{:S(2)}) copy-start(s32[36]{0:T(128)} %constant.34.clone) | copy-start | bytes 436
  85.7 9.3 %collective-permute-start.1 = (bf16[4,768,384]{2,1,0:T(8,128)(2,1)}, bf16[4,768,384]{2,1,0:T(8,128)(2,1)S(1)}, u32[]{:S(2)}, u32[]{:S(2)}) collective-permute-start(bf16[4,768,384]{2,1,0:T(8,128)(2,1)} %get-tuple-element.67), channel_id=1, source_target_pairs={{0,1},{1,0},{2,3},{3,2},{4,5},{5,4},{6,7},{7,6},{8,9},{9,8},{10,11... | collective-permute-start | bytes 7077896 | tf_op jit(solution)/shard_map/ppermute | solution.py:588
  85.8 9.2 %collective-permute-start.2 = (bf16[4,8,96,384]{3,2,1,0:T(8,128)(2,1)}, bf16[4,8,96,384]{3,2,1,0:T(8,128)(2,1)}, u32[]{:S(2)}, u32[]{:S(2)}) collective-permute-start(bf16[4,8,96,384]{3,2,1,0:T(8,128)(2,1)} %bitcast.18), channel_id=1, source_target_pairs={{0,1},{1,0},{2,3},{3,2},{4,5},{5,4},{6,7},{7,6},{8,9},{9,8},{10,11... | collective-permute-start | bytes 7077896 | tf_op jit(solution)/shard_map/ppermute | solution.py:588
  86.3 19.6 %all-to-all-start.2 = ((bf16[8,128,384]{2,1,0:T(8,128)(2,1)}), bf16[8,128,384]{2,1,0:T(8,128)(2,1)S(1)}, u32[]{:S(2)}, u32[]{:S(2)}) async-start(bf16[8,128,384]{2,1,0:T(8,128)(2,1)} %get-tuple-element.65), calls=%async_computation.2 | async-start | bytes 1572864 | tf_op jit(solution)/shard_map/all_to_all | solution.py:584
  90.1 5.0 %collective-permute-start.3 = (bf16[4,96,768]{2,1,0:T(8,128)(2,1)}, bf16[4,96,768]{2,1,0:T(8,128)(2,1)}, u32[]{:S(2)}, u32[]{:S(2)}) collective-permute-start(bf16[4,96,768]{2,1,0:T(8,128)(2,1)} %get-tuple-element.71), channel_id=1, source_target_pairs={{0,1},{1,0},{2,3},{3,2},{4,5},{5,4},{6,7},{7,6},{8,9},{9,8},{10,11... | collective-permute-start | bytes 1769480 | tf_op jit(solution)/shard_map/ppermute | solution.py:588
  95.0 1.4 copy-start.3
  105.9 5.1 %copy-start.7 = (bf16[8,128,384]{2,1,0:T(8,128)(2,1)}, bf16[8,128,384]{2,1,0:T(8,128)(2,1)S(1)}, u32[]{:S(2)}) copy-start(bf16[8,128,384]{2,1,0:T(8,128)(2,1)S(1)} %all-to-all-done.2.g_ref) | copy-start | bytes 2359300
  105.9 40.0 %collective-permute-start.8 = (bf16[1536,384]{1,0:T(8,128)(2,1)}, bf16[1536,384]{1,0:T(8,128)(2,1)S(1)}, u32[]{:S(2)}, u32[]{:S(2)}) collective-permute-start(bf16[1536,384]{1,0:T(8,128)(2,1)} %get-tuple-element.90), channel_id=1, source_target_pairs={{0,8},{8,0},{16,24},{24,16},{1,9},{9,1},{17,25},{25,17},{2,10},{10... | collective-permute-start | bytes 3538952 | tf_op jit(solution)/shard_map/ppermute | solution.py:588
  107.5 30.8 %collective-permute-start.5 = (bf16[960,384]{1,0:T(8,128)(2,1)}, bf16[960,384]{1,0:T(8,128)(2,1)}, u32[]{:S(2)}, u32[]{:S(2)}) collective-permute-start(bf16[960,384]{1,0:T(8,128)(2,1)} %get-tuple-element.86), channel_id=1, source_target_pairs={{0,2},{1,3},{2,0},{3,1},{4,6},{5,7},{6,4},{7,5},{8,10},{9,11},{10,... | collective-permute-start | bytes 2211848 | tf_op jit(solution)/shard_map/ppermute | solution.py:588
  108.9 29.9 %collective-permute-start.6 = (bf16[960,384]{1,0:T(8,128)(2,1)}, bf16[960,384]{1,0:T(8,128)(2,1)}, u32[]{:S(2)}, u32[]{:S(2)}) collective-permute-start(bf16[960,384]{1,0:T(8,128)(2,1)} %get-tuple-element.87), channel_id=1, source_target_pairs={{0,4},{1,5},{2,6},{3,7},{4,0},{5,1},{6,2},{7,3},{8,12},{9,13},{10,... | collective-permute-start | bytes 2211848 | tf_op jit(solution)/shard_map/ppermute | solution.py:588
  109.5 33.6 %collective-permute-start.7 = (bf16[960,384]{1,0:T(8,128)(2,1)}, bf16[960,384]{1,0:T(8,128)(2,1)}, u32[]{:S(2)}, u32[]{:S(2)}) collective-permute-start(bf16[960,384]{1,0:T(8,128)(2,1)} %get-tuple-element.88), channel_id=1, source_target_pairs={{0,6},{1,7},{2,4},{3,5},{4,2},{5,3},{6,0},{7,1},{8,14},{9,15},{10,... | collective-permute-start | bytes 2211848 | tf_op jit(solution)/shard_map/ppermute | solution.py:588
  137.0 6.1 %copy-start.8 = (bf16[960,384]{1,0:T(8,128)(2,1)S(1)}, bf16[960,384]{1,0:T(8,128)(2,1)}, u32[]{:S(2)}) copy-start(bf16[960,384]{1,0:T(8,128)(2,1)} %get-tuple-element.85) | copy-start | bytes 2211844
  138.3 7.9 %collective-permute-start.4 = (bf16[576,768]{1,0:T(8,128)(2,1)S(1)}, bf16[576,768]{1,0:T(8,128)(2,1)S(1)}, u32[]{:S(2)}, u32[]{:S(2)}) collective-permute-start(bf16[576,768]{1,0:T(8,128)(2,1)S(1)} %slice.6), channel_id=1, source_target_pairs={{0,1},{1,0},{2,3},{3,2},{4,5},{5,4},{6,7},{7,6},{8,9},{9,8},{10,11... | collective-permute-start | bytes 2654216 | tf_op jit(solution)/shard_map/ppermute | solution.py:588
  138.4 7.5 %copy-start.4 = (bf16[1536,384]{1,0:T(8,128)(2,1)S(1)}, bf16[1536,384]{1,0:T(8,128)(2,1)}, u32[]{:S(2)}) copy-start(bf16[1536,384]{1,0:T(8,128)(2,1)} %get-tuple-element.89) | copy-start | bytes 3538948
  138.4 18.6 %collective-permute-start.9 = (bf16[8,64,768]{2,1,0:T(8,128)(2,1)}, bf16[8,64,768]{2,1,0:T(8,128)(2,1)}, u32[]{:S(2)}, u32[]{:S(2)}) collective-permute-start(bf16[8,64,768]{2,1,0:T(8,128)(2,1)} %get-tuple-element.97), channel_id=1, source_target_pairs={{0,1},{1,0},{2,3},{3,2},{4,5},{5,4},{6,7},{7,6},{8,9},{9,8},{10,11... | collective-permute-start | bytes 2359304 | tf_op jit(solution)/shard_map/ppermute | solution.py:588
  146.2 0.9 copy-start.5
  150.8 12.7 %collective-permute-start.11 = (bf16[288,768]{1,0:T(8,128)(2,1)}, bf16[288,768]{1,0:T(8,128)(2,1)}, u32[]{:S(2)}, u32[]{:S(2)}) collective-permute-start(bf16[288,768]{1,0:T(8,128)(2,1)} %get-tuple-element.105), channel_id=1, source_target_pairs={{0,2},{1,3},{2,0},{3,1},{4,6},{5,7},{6,4},{7,5},{8,10},{9,11},{10,... | collective-permute-start | bytes 1327112 | tf_op jit(solution)/shard_map/ppermute | solution.py:588
  152.2 13.4 %collective-permute-start.12 = (bf16[288,768]{1,0:T(8,128)(2,1)}, bf16[288,768]{1,0:T(8,128)(2,1)}, u32[]{:S(2)}, u32[]{:S(2)}) collective-permute-start(bf16[288,768]{1,0:T(8,128)(2,1)} %get-tuple-element.106), channel_id=1, source_target_pairs={{0,4},{1,5},{2,6},{3,7},{4,0},{5,1},{6,2},{7,3},{8,12},{9,13},{10,... | collective-permute-start | bytes 1327112 | tf_op jit(solution)/shard_map/ppermute | solution.py:588
  152.8 22.4 %collective-permute-start.13 = (bf16[288,768]{1,0:T(8,128)(2,1)}, bf16[288,768]{1,0:T(8,128)(2,1)}, u32[]{:S(2)}, u32[]{:S(2)}) collective-permute-start(bf16[288,768]{1,0:T(8,128)(2,1)} %get-tuple-element.107), channel_id=1, source_target_pairs={{0,6},{1,7},{2,4},{3,5},{4,2},{5,3},{6,0},{7,1},{8,14},{9,15},{10,... | collective-permute-start | bytes 1327112 | tf_op jit(solution)/shard_map/ppermute | solution.py:588
  154.4 30.0 %collective-permute-start.10 = (bf16[768,384]{1,0:T(8,128)(2,1)S(1)}, bf16[768,384]{1,0:T(8,128)(2,1)S(1)}, u32[]{:S(2)}, u32[]{:S(2)}) collective-permute-start(bf16[768,384]{1,0:T(8,128)(2,1)S(1)} %split.19), channel_id=1, source_target_pairs={{0,24},{8,16},{16,8},{24,0},{1,25},{9,17},{17,9},{25,1},{2,26},{10... | collective-permute-start | bytes 1769480 | tf_op jit(solution)/shard_map/ppermute | solution.py:588
  159.7 24.9 %all-to-all-start.3 = ((bf16[8,72,768]{2,1,0:T(8,128)(2,1)}), bf16[8,72,768]{2,1,0:T(8,128)(2,1)S(1)}, u32[]{:S(2)}, u32[]{:S(2)}) async-start(bf16[8,72,768]{2,1,0:T(8,128)(2,1)} %merge.1), calls=%async_computation.3 | async-start | bytes 1769472 | tf_op jit(solution)/shard_map/all_to_all | solution.py:584
  180.0 12.4 %collective-permute-start.14 = (bf16[384,384]{1,0:T(8,128)(2,1)}, bf16[384,384]{1,0:T(8,128)(2,1)S(1)}, u32[]{:S(2)}, u32[]{:S(2)}) collective-permute-start(bf16[384,384]{1,0:T(8,128)(2,1)} %get-tuple-element.109), channel_id=1, source_target_pairs={{0,8},{8,0},{16,24},{24,16},{1,9},{9,1},{17,25},{25,17},{2,10},{10... | collective-permute-start | bytes 884744 | tf_op jit(solution)/shard_map/ppermute | solution.py:588
  180.5 21.8 %collective-permute-start.15 = (bf16[384,384]{1,0:T(8,128)(2,1)}, bf16[384,384]{1,0:T(8,128)(2,1)}, u32[]{:S(2)}, u32[]{:S(2)}) collective-permute-start(bf16[384,384]{1,0:T(8,128)(2,1)} %get-tuple-element.110), channel_id=1, source_target_pairs={{0,16},{8,24},{16,0},{24,8},{1,17},{9,25},{17,1},{25,9},{2,18},{10... | collective-permute-start | bytes 884744 | tf_op jit(solution)/shard_map/ppermute | solution.py:588
  183.1 19.2 %collective-permute-start.16 = (bf16[384,384]{1,0:T(8,128)(2,1)}, bf16[384,384]{1,0:T(8,128)(2,1)}, u32[]{:S(2)}, u32[]{:S(2)}) collective-permute-start(bf16[384,384]{1,0:T(8,128)(2,1)} %get-tuple-element.111), channel_id=1, source_target_pairs={{0,24},{8,16},{16,8},{24,0},{1,25},{9,17},{17,9},{25,1},{2,26},{10... | collective-permute-start | bytes 884744 | tf_op jit(solution)/shard_map/ppermute | solution.py:588
  184.6 0.9 copy-start.2
  189.4 5.6 %collective-permute-start.20 = (f32[8,128]{1,0:T(8,128)}, f32[8,128]{1,0:T(8,128)S(1)}, u32[]{:S(2)}, u32[]{:S(2)}) collective-permute-start(f32[8,128]{1,0:T(8,128)} %get-tuple-element.116), channel_id=1, source_target_pairs={{0,8},{8,0},{16,24},{24,16},{1,9},{9,1},{17,25},{25,17},{2,10},{10... | collective-permute-start | bytes 12296 | tf_op jit(solution)/shard_map/ppermute | solution.py:588
  190.1 21.9 %copy-start.1 = (s32[4,8]{1,0:T(4,128)S(1)}, s32[4,8]{1,0:T(4,128)}, u32[]{:S(2)}) copy-start(s32[4,8]{1,0:T(4,128)} %param.16) | copy-start | bytes 388
  190.8 16.5 %collective-permute-start.17 = (bf16[192,384]{1,0:T(8,128)(2,1)S(1)}, bf16[192,384]{1,0:T(8,128)(2,1)S(1)}, u32[]{:S(2)}, u32[]{:S(2)}) collective-permute-start(bf16[192,384]{1,0:T(8,128)(2,1)S(1)} %get-tuple-element.126), channel_id=1, source_target_pairs={{0,2},{1,3},{2,0},{3,1},{4,6},{5,7},{6,4},{7,5},{8,10},{9,11},{10,... | collective-permute-start | bytes 442376 | tf_op jit(solution)/shard_map/ppermute | solution.py:588
  192.4 9.9 %copy-start.9 = (bf16[384,384]{1,0:T(8,128)(2,1)}, bf16[384,384]{1,0:T(8,128)(2,1)S(1)}, u32[]{:S(2)}) copy-start(bf16[384,384]{1,0:T(8,128)(2,1)S(1)} %collective-permute-done.14.refs_1_) | copy-start | bytes 884740
  192.4 14.9 %collective-permute-start.18 = (bf16[192,384]{1,0:T(8,128)(2,1)S(1)}, bf16[192,384]{1,0:T(8,128)(2,1)S(1)}, u32[]{:S(2)}, u32[]{:S(2)}) collective-permute-start(bf16[192,384]{1,0:T(8,128)(2,1)S(1)} %get-tuple-element.125), channel_id=1, source_target_pairs={{0,4},{1,5},{2,6},{3,7},{4,0},{5,1},{6,2},{7,3},{8,12},{9,13},{10,... | collective-permute-start | bytes 442376 | tf_op jit(solution)/shard_map/ppermute | solution.py:588
  195.0 12.4 %collective-permute-start.19 = (bf16[192,384]{1,0:T(8,128)(2,1)S(1)}, bf16[192,384]{1,0:T(8,128)(2,1)S(1)}, u32[]{:S(2)}, u32[]{:S(2)}) collective-permute-start(bf16[192,384]{1,0:T(8,128)(2,1)S(1)} %get-tuple-element.124), channel_id=1, source_target_pairs={{0,6},{1,7},{2,4},{3,5},{4,2},{5,3},{6,0},{7,1},{8,14},{9,15},{10,... | collective-permute-start | bytes 442376 | tf_op jit(solution)/shard_map/ppermute | solution.py:588
  202.3 4.5 %collective-permute-start.21 = (f32[8,128]{1,0:T(8,128)S(1)}, f32[8,128]{1,0:T(8,128)S(1)}, u32[]{:S(2)}, u32[]{:S(2)}) collective-permute-start(f32[8,128]{1,0:T(8,128)S(1)} %add.47), channel_id=1, source_target_pairs={{0,16},{8,24},{16,0},{24,8},{1,17},{9,25},{17,1},{25,9},{2,18},{10... | collective-permute-start | bytes 12296 | tf_op jit(solution)/shard_map/ppermute | solution.py:588
  207.4 0.7 copy-start.10
  207.4 0.7 copy-start.11
  207.4 0.7 copy-start.12

commit v3 on v2

--- a/solution.py
+++ b/solution.py
@@ -327,19 +327,15 @@
 
 
 def tiles_kernel(near, owned, chip_ref, found_ref, keep_ref, given_ref, *outs):
-    step = pl.program_id(0)
     stay = keep_ref.shape[0] // STRIP
     for k in range(near):
-
-        @pl.when(step == k)
-        def _():
-            for strip in range(owned):
-                at = found_ref[(chip_ref[0] ^ k) * owned + strip]
-                here = pl.multiple_of(jnp.minimum(at, stay - 1) * STRIP, STRIP)
-                there = pl.multiple_of(jnp.maximum(at - stay, 0) * STRIP, STRIP)
-                outs[k][strip * STRIP : (strip + 1) * STRIP, :] = jnp.where(
-                    at < stay, keep_ref[pl.ds(here, STRIP), :], given_ref[pl.ds(there, STRIP), :]
-                )
+        for strip in range(owned):
+            at = found_ref[(chip_ref[0] ^ k) * owned + strip]
+            here = pl.multiple_of(jnp.minimum(at, stay - 1) * STRIP, STRIP)
+            there = pl.multiple_of(jnp.maximum(at - stay, 0) * STRIP, STRIP)
+            outs[k][strip * STRIP : (strip + 1) * STRIP, :] = jnp.where(
+                at < stay, keep_ref[pl.ds(here, STRIP), :], given_ref[pl.ds(there, STRIP), :]
+            )
 
 
 def qkv_tiles(chip, found, grad, given, near):
@@ -350,7 +346,7 @@
         functools.partial(tiles_kernel, near, owned),
         grid_spec=pltpu.PrefetchScalarGridSpec(
             num_scalar_prefetch=2,
-            grid=(near,),
+            grid=(1,),
             in_specs=[fixed2(given.shape), fixed2(given.shape)],
             out_specs=[fixed2(shape)] * near,
         ),
@@ -604,7 +600,7 @@
 
     for far in range(batch):
 
-        @pl.when(step == batch + far)
+        @pl.when(step == far)
         def _():
             for k in range(near):
                 total = both(down_a[k], down_b[k])
@@ -612,7 +608,7 @@
                 target, at = down_outs[far in (1, 2)], (far > 1) * near * slab + k * slab
                 target[at : at + slab] = total.reshape(slab, part)
 
-    @pl.when(step == 2 * batch)
+    @pl.when(step == batch)
     def _():
         for k in range(near):
             total = both(proj_a[k], proj_b[k])
@@ -625,16 +621,16 @@
     tall, few = width // batch, plane // batch
     up_spec = pl.BlockSpec((near, tall, part), lambda i, m: (0, jnp.minimum(i, batch - 1), 0))
     down_spec = pl.BlockSpec(
-        (near, few, block, part), lambda i, m: (0, m[0] ^ jnp.clip(i - batch, 0, batch - 1), 0, 0)
+        (near, few, block, part), lambda i, m: (0, m[0] ^ jnp.minimum(i, batch - 1), 0, 0)
     )
     proj_spec = pl.BlockSpec((near, block, width), lambda i, m: (0, 0, 0))
-    last = lambda i, m: (jnp.where(i < batch, i, jnp.where(i < 2 * batch, batch - 1, batch)), 0)
+    last = lambda i, m: (i, 0)
     down_shape = (2 * near * few * block, part)
     return pl.pallas_call(
         functools.partial(add_pair_kernel, near, batch),
         grid_spec=pltpu.PrefetchScalarGridSpec(
             num_scalar_prefetch=1,
-            grid=(2 * batch + 1,),
+            grid=(batch + 1,),
             in_specs=[up_spec] * 2 + [down_spec] * 2 + [proj_spec] * 2,
             out_specs=[pl.BlockSpec((tall, part), last)] * near
             + [pl.BlockSpec(down_shape, lambda i, m: (0, 0))] * 2,
@@ -705,9 +701,9 @@
 def finish_down_kernel(*refs):
     parts, down_ref = refs[:-1], refs[-1]
     total = add_all([r[...] for r in parts])
-    block, part = down_ref.shape[1], total.shape[1]
+    block, part = down_ref.shape[0], total.shape[1]
     for at in range(total.shape[0] // block):
-        down_ref[at * part : (at + 1) * part] = total[at * block : (at + 1) * block].T
+        down_ref[:, at * part : (at + 1) * part] = total[at * block : (at + 1) * block]
 
 
 def finish(kernel, parts, shapes):
@@ -800,7 +796,8 @@
         for bit in (1, 2):
             norms = norms + swap(norms, "batch", batch, bit)
         grad_up, grad_qkv, grad_proj = finish(finish_kernel, sums, [(slab, part), (slab, owned), (slab, block)])
-        (grad_down,) = finish(finish_down_kernel, down, [(hidden // batch, block)])
+        (grad_down,) = finish(finish_down_kernel, down, [(block, hidden // batch)])
+        grad_down = grad_down.T
     else:
         tile, cut = early, batch // plane
         down_tile = tile[width : 2 * width].reshape(plane, block, cut, part // cut).transpose(0, 2, 1, 3)

time: 213 us -> 208 us (0.977)
  Pallas kernels: 101 us -> 98.4 us
    pallas_call x1, Pallas kernels: 9.4 us -> 7.04 us  [add_pair(): pl.pallas_call(functools.partial(add_pair_kernel, near, batch), grid_spec...]
    unnamed x37 -> x36, local copies, waits for them, and re-layouts: 6.84 us -> 4.99 us
  transfers between devices with their start and end apart: 24 -> 24, of which waited for: 9 -> 9; matrix products, arithmetic and copies ran while one was open for 5% -> 5% of each run, Pallas kernels for 24% -> 23%
where the time goes in v3:
time: 208 us
  Pallas kernels  98.4 us (47%)
  blocking collectives  33 us (16%)
  waiting for transfers between devices  30.5 us (15%)
  starting transfers between devices  29 us (14%)
  local copies, waits for them, and re-layouts  8.28 us (4%)
  other arithmetic  7.42 us (4%)
    all_to_all x2, blocking collectives, exchange(): return lax.all_to_all(blocks, ('pb', 'ka'), 0, 0, tiled=True)  33 us
    ppermute x22, waiting for transfers between devices, swap(): return lax.ppermute(values, axes, [(i, i ^ bit) for i in range(size)])  30.5 us
    pallas_call x1, Pallas kernels, feed_forward(): pl.pallas_call(functools.partial(ff_kernel, seqs, plane), grid_spec=pltpu...  27 us
    pallas_call x1, Pallas kernels, attend_back(): pl.pallas_call(attend_back_kernel, grid_spec=pltpu.PrefetchScalarGridSpec...  25.9 us
    pallas_call x1, Pallas kernels, attend(): pl.pallas_call(attend_kernel, grid_spec=pltpu.PrefetchScalarGridSpec(num_...  21.8 us
    ppermute x22, starting transfers between devices, swap(): return lax.ppermute(values, axes, [(i, i ^ bit) for i in range(size)])  21.7 us
    all_to_all x2, starting transfers between devices, exchange(): return lax.all_to_all(blocks, ('pb', 'ka'), 0, 0, tiled=True)  7.32 us
    pallas_call x1, Pallas kernels, add_pair(): pl.pallas_call(functools.partial(add_pair_kernel, near, batch), grid_spec...  7.04 us
  transfers between devices with their start and end apart: 24, of which 9 were waited for; matrix products, arithmetic and copies ran while one was open for 5% of the time, Pallas kernels for 23%

profile of v3, /device:TPU:0, one launch (start us, length us, event | category | flops | bytes accessed | tf_op | source)
XLA Modules:
  0.0 207.5 jit_solution(6645584508933983150)
XLA Ops:
  0.6 0.0 copy-start
  0.6 17.0 %all_to_all.20.mine_ref = bf16[8,64,768]{2,1,0:T(8,128)(2,1)S(1)} all-to-all(bf16[8,64,768]{2,1,0:T(8,128)(2,1)} %bitcast.15), channel_id=1, replica_groups=mesh['batch'=4,'pb'=2,'ka'=4] {'pb','ka'}, dimensions={0} | all-to-all | bytes 1572864 | tf_op jit(solution)/shard_map/all_to_all | solution.py:580
  17.6 0.6 dynamic-slice_bitcast_fusion.place_ref
  18.3 1.6 collective-permute-done.other_ref
  19.9 0.9 copy-done.17
  20.8 21.8 %attend.1 = (bf16[8,128,384]{2,1,0:T(8,128)(2,1)}, bf16[1024,768]{1,0:T(8,128)(2,1)}, bf16[3,1024,384]{2,1,0:T(8,128)(2,1)}, f32[3,128,1024]{2,1,0:T(8,128)}, f32[3,8,1024]{2,1,0:T(8,128)}) custom-call(s32[1]{0:T(128)} %bitcast.2.core_ref, s32[8]{0:T(128)} %dynamic-slice_bitcast_fusion.place_ref, bf16[8,64,768]{2,1,0:T(8,128)(2,1)} %copy-done.6, ...), custom_call_target="tpu_custom_call" | custom-call | flops 5033164800 | bytes 6291456 | tf_op jit(solution)/shard_map/attend/pallas_call | solution.py:111
  42.7 16.0 %all_to_all.21.refs_2_ = bf16[8,128,384]{2,1,0:T(8,128)(2,1)} all-to-all(bf16[8,128,384]{2,1,0:T(8,128)(2,1)} %get-tuple-element.62), channel_id=1, replica_groups=mesh['batch'=4,'pb'=2,'ka'=4] {'pb','ka'}, dimensions={0} | all-to-all | bytes 1572864 | tf_op jit(solution)/shard_map/all_to_all | solution.py:580
  58.6 27.0 %feed_forward.1 = (bf16[512,768]{1,0:T(8,128)(2,1)}, f32[512,768]{1,0:T(8,128)}, bf16[8,128,384]{2,1,0:T(8,128)(2,1)}, f32[8,768]{1,0:T(8,128)}, bf16[4,768,384]...) custom-call(s32[1]{0:T(128)} %bitcast.refs_0_, ...), custom_call_target="tpu_custom_call" | custom-call | flops 16307453952 | bytes 18874368 | tf_op jit(solution)/shard_map/feed_forward/pallas_call | solution.py:498
  85.7 0.1 collective-permute-start.1
  85.8 0.5 collective-permute-start.2
  86.3 3.8 %all-to-all-start.2 = ((bf16[8,128,384]{2,1,0:T(8,128)(2,1)}), bf16[8,128,384]{2,1,0:T(8,128)(2,1)S(1)}, u32[]{:S(2)}, u32[]{:S(2)}) async-start(bf16[8,128,384]{2,1,0:T(8,128)(2,1)} %get-tuple-element.65), calls=%async_computation.2 | async-start | bytes 1572864 | tf_op jit(solution)/shard_map/all_to_all | solution.py:580
  90.1 0.2 collective-permute-start.3
  90.3 0.5 broadcast_select_fusion.1.to_ref
  90.8 0.5 broadcast_select_fusion.found_ref
  91.3 3.7 %collective-permute-done.3.refs_6_ = bf16[4,96,768]{2,1,0:T(8,128)(2,1)} collective-permute-done((bf16[4,96,768]{2,1,0:T(8,128)(2,1)}, bf16[4,96,768]{2,1,0:T(8,128)(2,1)}, u32[]{:S(2)}, u32[]{:S(2)}) %collective-permute-start.3) | collective-permute-done | bytes 589856 | tf_op jit(solution)/shard_map/ppermute | solution.py:584
  95.0 1.4 copy-done.3
  96.4 7.0 %add_pair.1 = (bf16[960,384]{1,0:T(8,128)(2,1)}, bf16[960,384]{1,0:T(8,128)(2,1)}, bf16[960,384]{1,0:T(8,128)(2,1)}, bf16[960,384]{1,0:T(8,128)(2,1)}, bf16[1536...) custom-call(s32[1]{0:T(128)} %bitcast.8.refs_0_.mine_ref, bf16[4,768,384]{2,1,0:T(8,128)(2,1)} %get-tuple-element.66.refs_1_, ...), custom_call_target="tpu_custom_call" | custom-call | flops 2654208 | bytes 15925248 | tf_op jit(solution)/shard_map/add_pair/pallas_call | solution.py:629
  103.5 1.6 collective-permute-start.8
  105.2 1.4 collective-permute-start.5
  106.6 0.6 collective-permute-start.6
  107.1 1.5 collective-permute-start.7
  108.6 25.9 %attend_back.1 = (bf16[1152,768]{1,0:T(8,128)(2,1)}, f32[8,64,768]{2,1,0:T(8,128)}, bf16[8,64,768]{2,1,0:T(8,128)(2,1)}, f32[8,768]{1,0:T(8,128)}) custom-call(s32[1]{0:T(128)} %bitcast.2.core_ref, s32[8]{0:T(128)} %dynamic-slice_bitcast_fusion.place_ref, s32[36]{0:T(128)} %broadcast_select_fusion.1.to_ref, bf16[3,1024,384]{2,1,0:T(8,128)(2,1)} %get-tuple-element.64.qkv_ref, ...), custom_call_target="tpu_custom_call" | custom-call | flops 11676942336 | bytes 6291456 | tf_op jit(solution)/shard_map/attend_back/pallas_call | solution.py:227
  134.6 1.3 slice.6
  135.9 0.1 collective-permute-start.4
  136.0 0.5 collective-permute-start.9
  136.5 4.2 %collective-permute-done.7 = bf16[960,384]{1,0:T(8,128)(2,1)} collective-permute-done((bf16[960,384]{1,0:T(8,128)(2,1)}, bf16[960,384]{1,0:T(8,128)(2,1)}, u32[]{:S(2)}, u32[]{:S(2)}) %collective-permute-start.7) | collective-permute-done | bytes 737312 | tf_op jit(solution)/shard_map/ppermute | solution.py:584
  140.7 2.8 %add_convert_fusion.1.refs_0_ = bf16[960,384]{1,0:T(8,128)(2,1)} fusion(bf16[960,384]{1,0:T(8,128)(2,1)} %collective-permute-done.7, bf16[960,384]{1,0:T(8,128)(2,1)} %collective-permute-done.6, bf16[960,384]{1,0:T(8,128)(2,1)} %collective-permute-done.5, bf16[960,384]{1,0:T(8,128)(2,1)S(1)} %copy-done.8), kind=kLoop, calls=%fused_computation.1 | loop fusion | flops 2949120 | bytes 3686400 | tf_op jit(solution)/shard_map/convert_element_type | solution.py:771
  143.5 0.3 add_convert_fusion
  143.9 0.9 copy-done.5
  144.8 3.5 %qkv_tiles.1 = (bf16[288,768]{1,0:T(8,128)(2,1)}, bf16[288,768]{1,0:T(8,128)(2,1)}, bf16[288,768]{1,0:T(8,128)(2,1)}, bf16[288,768]{1,0:T(8,128)(2,1)}) custom-call(s32[1]{0:T(128)} %bitcast.11.chip_ref, s32[36]{0:T(128)} %broadcast_select_fusion.found_ref, bf16[1152,768]{1,0:T(8,128)(2,1)} %get-tuple-element.84.keep_ref, bf16[576,768]{1,0:T(8,128)(2,1)} %copy-done.5), custom_call_target="tpu_custom_call" | custom-call | flops 442368 | bytes 442368 | tf_op jit(solution)/shard_map/qkv_tiles/pallas_call | solution.py:345
  148.3 1.4 collective-permute-start.11
  149.7 0.6 collective-permute-start.12
  150.3 1.5 collective-permute-start.13
  151.8 0.1 split.19
  151.8 2.5 %collective-permute-start.10 = (bf16[768,384]{1,0:T(8,128)(2,1)S(1)}, bf16[768,384]{1,0:T(8,128)(2,1)S(1)}, u32[]{:S(2)}, u32[]{:S(2)}) collective-permute-start(bf16[768,384]{1,0:T(8,128)(2,1)S(1)} %split.19), channel_id=1, source_target_pairs={{0,24},{8,16},{16,8},{24,0},{1,25},{9,17},{17,9},{25,1},{2,26},{10... | collective-permute-start | bytes 1769480 | tf_op jit(solution)/shard_map/ppermute | solution.py:584
  154.4 2.8 %merge.1 = bf16[8,72,768]{2,1,0:T(8,128)(2,1)} custom-call(f32[8,64,768]{2,1,0:T(8,128)} %get-tuple-element.96.keep_ref, bf16[8,64,768]{2,1,0:T(8,128)(2,1)} %collective-permute-done.9.other_ref, f32[8,768]{1,0:T(8,128)} %get-tuple-element.98.norm_ref), custom_call_target="tpu_custom_call" | custom-call | flops 393216 | bytes 3145728 | tf_op jit(solution)/shard_map/merge/pallas_call | solution.py:283
  157.1 3.5 %all-to-all-start.3 = ((bf16[8,72,768]{2,1,0:T(8,128)(2,1)}), bf16[8,72,768]{2,1,0:T(8,128)(2,1)S(1)}, u32[]{:S(2)}, u32[]{:S(2)}) async-start(bf16[8,72,768]{2,1,0:T(8,128)(2,1)} %merge.1), calls=%async_computation.3 | async-start | bytes 1769472 | tf_op jit(solution)/shard_map/all_to_all | solution.py:580
  160.7 0.0 collective-permute-done.11
  160.7 2.3 %collective-permute-done.12 = bf16[288,768]{1,0:T(8,128)(2,1)} collective-permute-done((bf16[288,768]{1,0:T(8,128)(2,1)}, bf16[288,768]{1,0:T(8,128)(2,1)}, u32[]{:S(2)}, u32[]{:S(2)}) %collective-permute-start.12) | collective-permute-done | bytes 442400 | tf_op jit(solution)/shard_map/ppermute | solution.py:584
  163.0 9.6 %collective-permute-done.13 = bf16[288,768]{1,0:T(8,128)(2,1)} collective-permute-done((bf16[288,768]{1,0:T(8,128)(2,1)}, bf16[288,768]{1,0:T(8,128)(2,1)}, u32[]{:S(2)}, u32[]{:S(2)}) %collective-permute-start.13) | collective-permute-done | bytes 442400 | tf_op jit(solution)/shard_map/ppermute | solution.py:584
  172.6 2.4 %add_convert_fusion.3.refs_1_ = bf16[288,768]{1,0:T(8,128)(2,1)} fusion(bf16[288,768]{1,0:T(8,128)(2,1)} %collective-permute-done.13, bf16[288,768]{1,0:T(8,128)(2,1)} %collective-permute-done.12, bf16[288,768]{1,0:T(8,128)(2,1)} %collective-permute-done.11, bf16[288,768]{1,0:T(8,128)(2,1)} %get-tuple-element.104), kind=kLoop, calls=%fused_computation.3 | loop fusion | flops 1769472 | bytes 2211840 | tf_op jit(solution)/shard_map/convert_element_type | solution.py:786
  175.0 2.5 %pack.1 = (bf16[384,384]{1,0:T(8,128)(2,1)}, bf16[384,384]{1,0:T(8,128)(2,1)}, bf16[384,384]{1,0:T(8,128)(2,1)}, bf16[384,384]{1,0:T(8,128)(2,1)}) custom-call(s32[1]{0:T(128)} %bitcast.8.refs_0_.mine_ref, bf16[960,384]{1,0:T(8,128)(2,1)} %add_convert_fusion.1.refs_0_, bf16[288,768]{1,0:T(8,128)(2,1)} %add_convert_fusion.3.refs_1_), custom_call_target="tpu_custom_call" | custom-call | flops 2359296 | bytes 5898240 | tf_op jit(solution)/shard_map/pack/pallas_call | solution.py:677
  177.5 0.4 collective-permute-start.14
  177.9 2.6 %collective-permute-start.15 = (bf16[384,384]{1,0:T(8,128)(2,1)}, bf16[384,384]{1,0:T(8,128)(2,1)}, u32[]{:S(2)}, u32[]{:S(2)}) collective-permute-start(bf16[384,384]{1,0:T(8,128)(2,1)} %get-tuple-element.110), channel_id=1, source_target_pairs={{0,16},{8,24},{16,0},{24,8},{1,17},{9,25},{17,1},{25,9},{2,18},{10... | collective-permute-start | bytes 884744 | tf_op jit(solution)/shard_map/ppermute | solution.py:584
  180.5 1.3 collective-permute-start.16
  181.9 0.2 add_convert_fusion.2
  182.1 0.9 copy-done.2
  183.0 3.8 %first_norm_back.1 = (bf16[512,768]{1,0:T(8,128)(2,1)}, f32[8,128]{1,0:T(8,128)}) custom-call(bf16[512,768]{1,0:T(8,128)(2,1)} %bitcast.17, f32[768]{0:T(1024)} %gain_ref.3, bf16[8,72,768]{2,1,0:T(8,128)(2,1)} %copy-done.2, f32[512,768]{1,0:T(8,128)} %get-tuple-element.101.res_ref), custom_call_target="tpu_custom_call" | custom-call | flops 7864320 | bytes 4718592 | tf_op jit(solution)/shard_map/first_norm_back/pallas_call | solution.py:568
  186.8 0.8 collective-permute-start.20
  187.6 0.7 fusion
  188.3 1.4 collective-permute-start.17
  189.7 0.2 collective-permute-done.14.refs_1_
  189.9 1.3 collective-permute-start.18
  191.2 1.3 collective-permute-done.20
  192.5 1.4 collective-permute-start.19
  193.9 0.7 add.47
  194.6 5.1 %collective-permute-done.15.refs_2_ = bf16[384,384]{1,0:T(8,128)(2,1)} collective-permute-done((bf16[384,384]{1,0:T(8,128)(2,1)}, bf16[384,384]{1,0:T(8,128)(2,1)}, u32[]{:S(2)}, u32[]{:S(2)}) %collective-permute-start.15) | collective-permute-done | bytes 294944 | tf_op jit(solution)/shard_map/ppermute | solution.py:584
  199.7 2.2 %finish.2 = (f32[192,384]{1,0:T(8,128)}, f32[192,288]{1,0:T(8,128)}, f32[192,96]{1,0:T(8,128)}) custom-call(bf16[384,384]{1,0:T(8,128)(2,1)} %get-tuple-element.108.refs_0_, bf16[384,384]{1,0:T(8,128)(2,1)} %copy-done.9, bf16[384,384]{1,0:T(8,128)(2,1)} %collective-permute-done.15.refs_2_, bf16[384,384]{1,0:T(8,128)(2,1)} %collective-permute-done.16.refs_3_), custom_call_target="tpu_custom_call" | custom-call | flops 1179648 | bytes 2359296 | tf_op jit(solution)/shard_map/finish/pallas_call | solution.py:711
  201.9 2.3 %collective-permute-done.21 = f32[8,128]{1,0:T(8,128)S(1)} collective-permute-done((f32[8,128]{1,0:T(8,128)S(1)}, f32[8,128]{1,0:T(8,128)S(1)}, u32[]{:S(2)}, u32[]{:S(2)}) %collective-permute-start.21) | collective-permute-done | bytes 4128 | tf_op jit(solution)/shard_map/ppermute | solution.py:584
  204.2 0.6 slice.7
  204.9 0.6 copy-done.10
  205.5 0.0 copy-done.11
  205.5 0.1 copy-done.12
  205.6 1.9 finish.3
  (45 shorter events, 0.1 us)
Async XLA Ops:
  0.6 17.0 %copy-start = (s32[4,8]{1,0:T(4,128)S(1)}, s32[4,8]{1,0:T(4,128)}, u32[]{:S(2)}) copy-start(s32[4,8]{1,0:T(4,128)} %param.16) | copy-start | bytes 388
  17.6 2.3 %copy-start.6 = (bf16[8,64,768]{2,1,0:T(8,128)(2,1)}, bf16[8,64,768]{2,1,0:T(8,128)(2,1)S(1)}, u32[]{:S(2)}) copy-start(bf16[8,64,768]{2,1,0:T(8,128)(2,1)S(1)} %all_to_all.20.mine_ref) | copy-start | bytes 2359300
  17.6 2.3 %collective-permute-start = (bf16[8,64,768]{2,1,0:T(8,128)(2,1)S(1)}, bf16[8,64,768]{2,1,0:T(8,128)(2,1)S(1)}, u32[]{:S(2)}, u32[]{:S(2)}) collective-permute-start(bf16[8,64,768]{2,1,0:T(8,128)(2,1)S(1)} %all_to_all.20.mine_ref), channel_id=1, source_target_pairs={{0,1},{1,0},{2,3},{3,2},{4,5},{5,4},{6,7},{7,6},{8,9},{9,8},{10,11... | collective-permute-start | bytes 2359304 | tf_op jit(solution)/shard_map/ppermute | solution.py:584
  19.9 0.9 copy-start.17
  85.7 4.6 %copy-start.15 = (s32[36]{0:T(128)S(1)}, s32[36]{0:T(128)}, u32[]{:S(2)}) copy-start(s32[36]{0:T(128)} %constant.31.clone) | copy-start | bytes 436
  85.7 4.6 %copy-start.16 = (s32[36]{0:T(128)S(1)}, s32[36]{0:T(128)}, u32[]{:S(2)}) copy-start(s32[36]{0:T(128)} %constant.32.clone) | copy-start | bytes 436
  85.7 5.1 %copy-start.13 = (s32[36]{0:T(128)S(1)}, s32[36]{0:T(128)}, u32[]{:S(2)}) copy-start(s32[36]{0:T(128)} %constant.33.clone) | copy-start | bytes 436
  85.7 5.1 %copy-start.14 = (s32[36]{0:T(128)S(1)}, s32[36]{0:T(128)}, u32[]{:S(2)}) copy-start(s32[36]{0:T(128)} %constant.34.clone) | copy-start | bytes 436
  85.7 9.3 %collective-permute-start.1 = (bf16[4,768,384]{2,1,0:T(8,128)(2,1)}, bf16[4,768,384]{2,1,0:T(8,128)(2,1)S(1)}, u32[]{:S(2)}, u32[]{:S(2)}) collective-permute-start(bf16[4,768,384]{2,1,0:T(8,128)(2,1)} %get-tuple-element.67), channel_id=1, source_target_pairs={{0,1},{1,0},{2,3},{3,2},{4,5},{5,4},{6,7},{7,6},{8,9},{9,8},{10,11... | collective-permute-start | bytes 7077896 | tf_op jit(solution)/shard_map/ppermute | solution.py:584
  85.8 9.2 %collective-permute-start.2 = (bf16[4,8,96,384]{3,2,1,0:T(8,128)(2,1)}, bf16[4,8,96,384]{3,2,1,0:T(8,128)(2,1)}, u32[]{:S(2)}, u32[]{:S(2)}) collective-permute-start(bf16[4,8,96,384]{3,2,1,0:T(8,128)(2,1)} %bitcast.20), channel_id=1, source_target_pairs={{0,1},{1,0},{2,3},{3,2},{4,5},{5,4},{6,7},{7,6},{8,9},{9,8},{10,11... | collective-permute-start | bytes 7077896 | tf_op jit(solution)/shard_map/ppermute | solution.py:584
  86.3 17.2 %all-to-all-start.2 = ((bf16[8,128,384]{2,1,0:T(8,128)(2,1)}), bf16[8,128,384]{2,1,0:T(8,128)(2,1)S(1)}, u32[]{:S(2)}, u32[]{:S(2)}) async-start(bf16[8,128,384]{2,1,0:T(8,128)(2,1)} %get-tuple-element.65), calls=%async_computation.2 | async-start | bytes 1572864 | tf_op jit(solution)/shard_map/all_to_all | solution.py:580
  90.1 5.0 %collective-permute-start.3 = (bf16[4,96,768]{2,1,0:T(8,128)(2,1)}, bf16[4,96,768]{2,1,0:T(8,128)(2,1)}, u32[]{:S(2)}, u32[]{:S(2)}) collective-permute-start(bf16[4,96,768]{2,1,0:T(8,128)(2,1)} %get-tuple-element.71), channel_id=1, source_target_pairs={{0,1},{1,0},{2,3},{3,2},{4,5},{5,4},{6,7},{7,6},{8,9},{9,8},{10,11... | collective-permute-start | bytes 1769480 | tf_op jit(solution)/shard_map/ppermute | solution.py:584
  95.0 1.4 copy-start.3
  103.5 5.1 %copy-start.7 = (bf16[8,128,384]{2,1,0:T(8,128)(2,1)}, bf16[8,128,384]{2,1,0:T(8,128)(2,1)S(1)}, u32[]{:S(2)}) copy-start(bf16[8,128,384]{2,1,0:T(8,128)(2,1)S(1)} %all-to-all-done.2.g_ref) | copy-start | bytes 2359300
  103.5 40.0 %collective-permute-start.8 = (bf16[1536,384]{1,0:T(8,128)(2,1)}, bf16[1536,384]{1,0:T(8,128)(2,1)S(1)}, u32[]{:S(2)}, u32[]{:S(2)}) collective-permute-start(bf16[1536,384]{1,0:T(8,128)(2,1)} %get-tuple-element.90), channel_id=1, source_target_pairs={{0,8},{8,0},{16,24},{24,16},{1,9},{9,1},{17,25},{25,17},{2,10},{10... | collective-permute-start | bytes 3538952 | tf_op jit(solution)/shard_map/ppermute | solution.py:584
  105.2 30.8 %collective-permute-start.5 = (bf16[960,384]{1,0:T(8,128)(2,1)}, bf16[960,384]{1,0:T(8,128)(2,1)}, u32[]{:S(2)}, u32[]{:S(2)}) collective-permute-start(bf16[960,384]{1,0:T(8,128)(2,1)} %get-tuple-element.86), channel_id=1, source_target_pairs={{0,2},{1,3},{2,0},{3,1},{4,6},{5,7},{6,4},{7,5},{8,10},{9,11},{10,... | collective-permute-start | bytes 2211848 | tf_op jit(solution)/shard_map/ppermute | solution.py:584
  106.6 29.9 %collective-permute-start.6 = (bf16[960,384]{1,0:T(8,128)(2,1)}, bf16[960,384]{1,0:T(8,128)(2,1)}, u32[]{:S(2)}, u32[]{:S(2)}) collective-permute-start(bf16[960,384]{1,0:T(8,128)(2,1)} %get-tuple-element.87), channel_id=1, source_target_pairs={{0,4},{1,5},{2,6},{3,7},{4,0},{5,1},{6,2},{7,3},{8,12},{9,13},{10,... | collective-permute-start | bytes 2211848 | tf_op jit(solution)/shard_map/ppermute | solution.py:584
  107.1 33.6 %collective-permute-start.7 = (bf16[960,384]{1,0:T(8,128)(2,1)}, bf16[960,384]{1,0:T(8,128)(2,1)}, u32[]{:S(2)}, u32[]{:S(2)}) collective-permute-start(bf16[960,384]{1,0:T(8,128)(2,1)} %get-tuple-element.88), channel_id=1, source_target_pairs={{0,6},{1,7},{2,4},{3,5},{4,2},{5,3},{6,0},{7,1},{8,14},{9,15},{10,... | collective-permute-start | bytes 2211848 | tf_op jit(solution)/shard_map/ppermute | solution.py:584
  134.6 6.1 %copy-start.8 = (bf16[960,384]{1,0:T(8,128)(2,1)S(1)}, bf16[960,384]{1,0:T(8,128)(2,1)}, u32[]{:S(2)}) copy-start(bf16[960,384]{1,0:T(8,128)(2,1)} %get-tuple-element.85) | copy-start | bytes 2211844
  135.9 7.9 %collective-permute-start.4 = (bf16[576,768]{1,0:T(8,128)(2,1)S(1)}, bf16[576,768]{1,0:T(8,128)(2,1)S(1)}, u32[]{:S(2)}, u32[]{:S(2)}) collective-permute-start(bf16[576,768]{1,0:T(8,128)(2,1)S(1)} %slice.6), channel_id=1, source_target_pairs={{0,1},{1,0},{2,3},{3,2},{4,5},{5,4},{6,7},{7,6},{8,9},{9,8},{10,11... | collective-permute-start | bytes 2654216 | tf_op jit(solution)/shard_map/ppermute | solution.py:584
  136.0 7.5 %copy-start.4 = (bf16[1536,384]{1,0:T(8,128)(2,1)S(1)}, bf16[1536,384]{1,0:T(8,128)(2,1)}, u32[]{:S(2)}) copy-start(bf16[1536,384]{1,0:T(8,128)(2,1)} %get-tuple-element.89) | copy-start | bytes 3538948
  136.0 18.4 %collective-permute-start.9 = (bf16[8,64,768]{2,1,0:T(8,128)(2,1)}, bf16[8,64,768]{2,1,0:T(8,128)(2,1)}, u32[]{:S(2)}, u32[]{:S(2)}) collective-permute-start(bf16[8,64,768]{2,1,0:T(8,128)(2,1)} %get-tuple-element.97), channel_id=1, source_target_pairs={{0,1},{1,0},{2,3},{3,2},{4,5},{5,4},{6,7},{7,6},{8,9},{9,8},{10,11... | collective-permute-start | bytes 2359304 | tf_op jit(solution)/shard_map/ppermute | solution.py:584
  143.9 0.9 copy-start.5
  148.3 12.4 %collective-permute-start.11 = (bf16[288,768]{1,0:T(8,128)(2,1)}, bf16[288,768]{1,0:T(8,128)(2,1)}, u32[]{:S(2)}, u32[]{:S(2)}) collective-permute-start(bf16[288,768]{1,0:T(8,128)(2,1)} %get-tuple-element.105), channel_id=1, source_target_pairs={{0,2},{1,3},{2,0},{3,1},{4,6},{5,7},{6,4},{7,5},{8,10},{9,11},{10,... | collective-permute-start | bytes 1327112 | tf_op jit(solution)/shard_map/ppermute | solution.py:584
  149.7 13.4 %collective-permute-start.12 = (bf16[288,768]{1,0:T(8,128)(2,1)}, bf16[288,768]{1,0:T(8,128)(2,1)}, u32[]{:S(2)}, u32[]{:S(2)}) collective-permute-start(bf16[288,768]{1,0:T(8,128)(2,1)} %get-tuple-element.106), channel_id=1, source_target_pairs={{0,4},{1,5},{2,6},{3,7},{4,0},{5,1},{6,2},{7,3},{8,12},{9,13},{10,... | collective-permute-start | bytes 1327112 | tf_op jit(solution)/shard_map/ppermute | solution.py:584
  150.3 22.4 %collective-permute-start.13 = (bf16[288,768]{1,0:T(8,128)(2,1)}, bf16[288,768]{1,0:T(8,128)(2,1)}, u32[]{:S(2)}, u32[]{:S(2)}) collective-permute-start(bf16[288,768]{1,0:T(8,128)(2,1)} %get-tuple-element.107), channel_id=1, source_target_pairs={{0,6},{1,7},{2,4},{3,5},{4,2},{5,3},{6,0},{7,1},{8,14},{9,15},{10,... | collective-permute-start | bytes 1327112 | tf_op jit(solution)/shard_map/ppermute | solution.py:584
  151.8 30.0 %collective-permute-start.10 = (bf16[768,384]{1,0:T(8,128)(2,1)S(1)}, bf16[768,384]{1,0:T(8,128)(2,1)S(1)}, u32[]{:S(2)}, u32[]{:S(2)}) collective-permute-start(bf16[768,384]{1,0:T(8,128)(2,1)S(1)} %split.19), channel_id=1, source_target_pairs={{0,24},{8,16},{16,8},{24,0},{1,25},{9,17},{17,9},{25,1},{2,26},{10... | collective-permute-start | bytes 1769480 | tf_op jit(solution)/shard_map/ppermute | solution.py:584
  157.1 24.9 %all-to-all-start.3 = ((bf16[8,72,768]{2,1,0:T(8,128)(2,1)}), bf16[8,72,768]{2,1,0:T(8,128)(2,1)S(1)}, u32[]{:S(2)}, u32[]{:S(2)}) async-start(bf16[8,72,768]{2,1,0:T(8,128)(2,1)} %merge.1), calls=%async_computation.3 | async-start | bytes 1769472 | tf_op jit(solution)/shard_map/all_to_all | solution.py:580
  177.5 12.4 %collective-permute-start.14 = (bf16[384,384]{1,0:T(8,128)(2,1)}, bf16[384,384]{1,0:T(8,128)(2,1)S(1)}, u32[]{:S(2)}, u32[]{:S(2)}) collective-permute-start(bf16[384,384]{1,0:T(8,128)(2,1)} %get-tuple-element.109), channel_id=1, source_target_pairs={{0,8},{8,0},{16,24},{24,16},{1,9},{9,1},{17,25},{25,17},{2,10},{10... | collective-permute-start | bytes 884744 | tf_op jit(solution)/shard_map/ppermute | solution.py:584
  177.9 21.8 %collective-permute-start.15 = (bf16[384,384]{1,0:T(8,128)(2,1)}, bf16[384,384]{1,0:T(8,128)(2,1)}, u32[]{:S(2)}, u32[]{:S(2)}) collective-permute-start(bf16[384,384]{1,0:T(8,128)(2,1)} %get-tuple-element.110), channel_id=1, source_target_pairs={{0,16},{8,24},{16,0},{24,8},{1,17},{9,25},{17,1},{25,9},{2,18},{10... | collective-permute-start | bytes 884744 | tf_op jit(solution)/shard_map/ppermute | solution.py:584
  180.5 19.2 %collective-permute-start.16 = (bf16[384,384]{1,0:T(8,128)(2,1)}, bf16[384,384]{1,0:T(8,128)(2,1)}, u32[]{:S(2)}, u32[]{:S(2)}) collective-permute-start(bf16[384,384]{1,0:T(8,128)(2,1)} %get-tuple-element.111), channel_id=1, source_target_pairs={{0,24},{8,16},{16,8},{24,0},{1,25},{9,17},{17,9},{25,1},{2,26},{10... | collective-permute-start | bytes 884744 | tf_op jit(solution)/shard_map/ppermute | solution.py:584
  182.1 0.9 copy-start.2
  186.8 20.7 %copy-start.1 = (s32[4,8]{1,0:T(4,128)S(1)}, s32[4,8]{1,0:T(4,128)}, u32[]{:S(2)}) copy-start(s32[4,8]{1,0:T(4,128)} %param.16) | copy-start | bytes 388
  186.8 5.6 %collective-permute-start.20 = (f32[8,128]{1,0:T(8,128)}, f32[8,128]{1,0:T(8,128)S(1)}, u32[]{:S(2)}, u32[]{:S(2)}) collective-permute-start(f32[8,128]{1,0:T(8,128)} %get-tuple-element.116), channel_id=1, source_target_pairs={{0,8},{8,0},{16,24},{24,16},{1,9},{9,1},{17,25},{25,17},{2,10},{10... | collective-permute-start | bytes 12296 | tf_op jit(solution)/shard_map/ppermute | solution.py:584
  188.3 16.5 %collective-permute-start.17 = (bf16[192,384]{1,0:T(8,128)(2,1)S(1)}, bf16[192,384]{1,0:T(8,128)(2,1)S(1)}, u32[]{:S(2)}, u32[]{:S(2)}) collective-permute-start(bf16[192,384]{1,0:T(8,128)(2,1)S(1)} %get-tuple-element.119), channel_id=1, source_target_pairs={{0,2},{1,3},{2,0},{3,1},{4,6},{5,7},{6,4},{7,5},{8,10},{9,11},{10,... | collective-permute-start | bytes 442376 | tf_op jit(solution)/shard_map/ppermute | solution.py:584
  189.9 9.9 %copy-start.9 = (bf16[384,384]{1,0:T(8,128)(2,1)}, bf16[384,384]{1,0:T(8,128)(2,1)S(1)}, u32[]{:S(2)}) copy-start(bf16[384,384]{1,0:T(8,128)(2,1)S(1)} %collective-permute-done.14.refs_1_) | copy-start | bytes 884740
  189.9 14.9 %collective-permute-start.18 = (bf16[192,384]{1,0:T(8,128)(2,1)S(1)}, bf16[192,384]{1,0:T(8,128)(2,1)S(1)}, u32[]{:S(2)}, u32[]{:S(2)}) collective-permute-start(bf16[192,384]{1,0:T(8,128)(2,1)S(1)} %get-tuple-element.118), channel_id=1, source_target_pairs={{0,4},{1,5},{2,6},{3,7},{4,0},{5,1},{6,2},{7,3},{8,12},{9,13},{10,... | collective-permute-start | bytes 442376 | tf_op jit(solution)/shard_map/ppermute | solution.py:584
  192.5 12.4 %collective-permute-start.19 = (bf16[192,384]{1,0:T(8,128)(2,1)S(1)}, bf16[192,384]{1,0:T(8,128)(2,1)S(1)}, u32[]{:S(2)}, u32[]{:S(2)}) collective-permute-start(bf16[192,384]{1,0:T(8,128)(2,1)S(1)} %get-tuple-element.117), channel_id=1, source_target_pairs={{0,6},{1,7},{2,4},{3,5},{4,2},{5,3},{6,0},{7,1},{8,14},{9,15},{10,... | collective-permute-start | bytes 442376 | tf_op jit(solution)/shard_map/ppermute | solution.py:584
  199.7 4.5 %collective-permute-start.21 = (f32[8,128]{1,0:T(8,128)S(1)}, f32[8,128]{1,0:T(8,128)S(1)}, u32[]{:S(2)}, u32[]{:S(2)}) collective-permute-start(f32[8,128]{1,0:T(8,128)S(1)} %add.47), channel_id=1, source_target_pairs={{0,16},{8,24},{16,0},{24,8},{1,17},{9,25},{17,1},{25,9},{2,18},{10... | collective-permute-start | bytes 12296 | tf_op jit(solution)/shard_map/ppermute | solution.py:584
  204.8 0.7 copy-start.10
  204.8 0.7 copy-start.11
  204.8 0.7 copy-start.12

commit v4 on v3

--- a/solution.py
+++ b/solution.py
@@ -10,7 +10,7 @@
 HEADS = 12
 HEAD = 64
 PAIR = 2 * HEAD
-QTILE = 256
+QTILE = 128
 STRIP = 32
 SCALE = HEAD ** (-0.5)
 HUGE = 3e38

time: 208 us -> 207 us (level)
  transfers between devices with their start and end apart: 24 -> 24, of which waited for: 9 -> 9; matrix products, arithmetic and copies ran while one was open for 5% -> 5% of each run, Pallas kernels for 23% -> 24%
where the time goes in v4:
time: 207 us; the launch traced here: 206 us
  Pallas kernels  98.6 us (48%)
  blocking collectives  33 us (16%)
  starting transfers between devices  29 us (14%)
  waiting for transfers between devices  29 us (14%)
  local copies, waits for them, and re-layouts  8.28 us (4%)
  other arithmetic  7.42 us (4%)
    all_to_all x2, blocking collectives, exchange(): return lax.all_to_all(blocks, ('pb', 'ka'), 0, 0, tiled=True)  33 us
    ppermute x22, waiting for transfers between devices, swap(): return lax.ppermute(values, axes, [(i, i ^ bit) for i in range(size)])  29 us
    pallas_call x1, Pallas kernels, attend_back(): pl.pallas_call(attend_back_kernel, grid_spec=pltpu.PrefetchScalarGridSpec...  27.4 us
    pallas_call x1, Pallas kernels, feed_forward(): pl.pallas_call(functools.partial(ff_kernel, seqs, plane), grid_spec=pltpu...  27 us
    ppermute x22, starting transfers between devices, swap(): return lax.ppermute(values, axes, [(i, i ^ bit) for i in range(size)])  21.7 us
    pallas_call x1, Pallas kernels, attend(): pl.pallas_call(attend_kernel, grid_spec=pltpu.PrefetchScalarGridSpec(num_...  20.5 us
    all_to_all x2, starting transfers between devices, exchange(): return lax.all_to_all(blocks, ('pb', 'ka'), 0, 0, tiled=True)  7.32 us
    pallas_call x1, Pallas kernels, add_pair(): pl.pallas_call(functools.partial(add_pair_kernel, near, batch), grid_spec...  7.04 us
  transfers between devices with their start and end apart: 24, of which 9 were waited for; matrix products, arithmetic and copies ran while one was open for 5% of the time, Pallas kernels for 24%

profile of v4, /device:TPU:0, one launch (start us, length us, event | category | flops | bytes accessed | tf_op | source)
XLA Modules:
  0.0 206.2 jit_solution(3672053082847315559)
XLA Ops:
  0.6 0.0 copy-start
  0.6 17.0 %all_to_all.20.mine_ref = bf16[8,64,768]{2,1,0:T(8,128)(2,1)S(1)} all-to-all(bf16[8,64,768]{2,1,0:T(8,128)(2,1)} %bitcast.15), channel_id=1, replica_groups=mesh['batch'=4,'pb'=2,'ka'=4] {'pb','ka'}, dimensions={0} | all-to-all | bytes 1572864 | tf_op jit(solution)/shard_map/all_to_all | solution.py:580
  17.6 0.6 dynamic-slice_bitcast_fusion.place_ref
  18.3 1.6 collective-permute-done.other_ref
  19.9 0.9 copy-done.17
  20.8 20.5 %attend.1 = (bf16[8,128,384]{2,1,0:T(8,128)(2,1)}, bf16[1024,768]{1,0:T(8,128)(2,1)}, bf16[3,1024,384]{2,1,0:T(8,128)(2,1)}, f32[3,128,1024]{2,1,0:T(8,128)}, f32[3,8,1024]{2,1,0:T(8,128)}) custom-call(s32[1]{0:T(128)} %bitcast.2.core_ref, s32[8]{0:T(128)} %dynamic-slice_bitcast_fusion.place_ref, bf16[8,64,768]{2,1,0:T(8,128)(2,1)} %copy-done.6, ...), custom_call_target="tpu_custom_call" | custom-call | flops 5033164800 | bytes 6291456 | tf_op jit(solution)/shard_map/attend/pallas_call | solution.py:111
  41.3 16.0 %all_to_all.21.refs_2_ = bf16[8,128,384]{2,1,0:T(8,128)(2,1)} all-to-all(bf16[8,128,384]{2,1,0:T(8,128)(2,1)} %get-tuple-element.62), channel_id=1, replica_groups=mesh['batch'=4,'pb'=2,'ka'=4] {'pb','ka'}, dimensions={0} | all-to-all | bytes 1572864 | tf_op jit(solution)/shard_map/all_to_all | solution.py:580
  57.3 27.0 %feed_forward.1 = (bf16[512,768]{1,0:T(8,128)(2,1)}, f32[512,768]{1,0:T(8,128)}, bf16[8,128,384]{2,1,0:T(8,128)(2,1)}, f32[8,768]{1,0:T(8,128)}, bf16[4,768,384]...) custom-call(s32[1]{0:T(128)} %bitcast.refs_0_, ...), custom_call_target="tpu_custom_call" | custom-call | flops 16307453952 | bytes 18874368 | tf_op jit(solution)/shard_map/feed_forward/pallas_call | solution.py:498
  84.4 0.1 collective-permute-start.1
  84.5 0.5 collective-permute-start.2
  85.0 3.8 %all-to-all-start.2 = ((bf16[8,128,384]{2,1,0:T(8,128)(2,1)}), bf16[8,128,384]{2,1,0:T(8,128)(2,1)S(1)}, u32[]{:S(2)}, u32[]{:S(2)}) async-start(bf16[8,128,384]{2,1,0:T(8,128)(2,1)} %get-tuple-element.65), calls=%async_computation.2 | async-start | bytes 1572864 | tf_op jit(solution)/shard_map/all_to_all | solution.py:580
  88.8 0.2 collective-permute-start.3
  88.9 0.5 broadcast_select_fusion.1.to_ref
  89.5 0.5 broadcast_select_fusion.found_ref
  90.0 3.7 %collective-permute-done.3.refs_6_ = bf16[4,96,768]{2,1,0:T(8,128)(2,1)} collective-permute-done((bf16[4,96,768]{2,1,0:T(8,128)(2,1)}, bf16[4,96,768]{2,1,0:T(8,128)(2,1)}, u32[]{:S(2)}, u32[]{:S(2)}) %collective-permute-start.3) | collective-permute-done | bytes 589856 | tf_op jit(solution)/shard_map/ppermute | solution.py:584
  93.7 1.4 copy-done.3
  95.1 7.0 %add_pair.1 = (bf16[960,384]{1,0:T(8,128)(2,1)}, bf16[960,384]{1,0:T(8,128)(2,1)}, bf16[960,384]{1,0:T(8,128)(2,1)}, bf16[960,384]{1,0:T(8,128)(2,1)}, bf16[1536...) custom-call(s32[1]{0:T(128)} %bitcast.8.refs_0_.mine_ref, bf16[4,768,384]{2,1,0:T(8,128)(2,1)} %get-tuple-element.66.refs_1_, ...), custom_call_target="tpu_custom_call" | custom-call | flops 2654208 | bytes 15925248 | tf_op jit(solution)/shard_map/add_pair/pallas_call | solution.py:629
  102.2 1.6 collective-permute-start.8
  103.8 1.4 collective-permute-start.5
  105.2 0.6 collective-permute-start.6
  105.8 1.5 collective-permute-start.7
  107.3 27.4 %attend_back.1 = (bf16[1152,768]{1,0:T(8,128)(2,1)}, f32[8,64,768]{2,1,0:T(8,128)}, bf16[8,64,768]{2,1,0:T(8,128)(2,1)}, f32[8,768]{1,0:T(8,128)}) custom-call(s32[1]{0:T(128)} %bitcast.2.core_ref, s32[8]{0:T(128)} %dynamic-slice_bitcast_fusion.place_ref, s32[36]{0:T(128)} %broadcast_select_fusion.1.to_ref, bf16[3,1024,384]{2,1,0:T(8,128)(2,1)} %get-tuple-element.64.qkv_ref, ...), custom_call_target="tpu_custom_call" | custom-call | flops 11676942336 | bytes 6291456 | tf_op jit(solution)/shard_map/attend_back/pallas_call | solution.py:227
  134.7 1.3 slice.6
  136.0 0.1 collective-permute-start.4
  136.1 0.5 collective-permute-start.9
  136.6 2.8 %collective-permute-done.7 = bf16[960,384]{1,0:T(8,128)(2,1)} collective-permute-done((bf16[960,384]{1,0:T(8,128)(2,1)}, bf16[960,384]{1,0:T(8,128)(2,1)}, u32[]{:S(2)}, u32[]{:S(2)}) %collective-permute-start.7) | collective-permute-done | bytes 737312 | tf_op jit(solution)/shard_map/ppermute | solution.py:584
  139.4 2.8 %add_convert_fusion.1.refs_0_ = bf16[960,384]{1,0:T(8,128)(2,1)} fusion(bf16[960,384]{1,0:T(8,128)(2,1)} %collective-permute-done.7, bf16[960,384]{1,0:T(8,128)(2,1)} %collective-permute-done.6, bf16[960,384]{1,0:T(8,128)(2,1)} %collective-permute-done.5, bf16[960,384]{1,0:T(8,128)(2,1)S(1)} %copy-done.8), kind=kLoop, calls=%fused_computation.1 | loop fusion | flops 2949120 | bytes 3686400 | tf_op jit(solution)/shard_map/convert_element_type | solution.py:771
  142.2 0.3 add_convert_fusion
  142.5 0.9 copy-done.5
  143.5 3.5 %qkv_tiles.1 = (bf16[288,768]{1,0:T(8,128)(2,1)}, bf16[288,768]{1,0:T(8,128)(2,1)}, bf16[288,768]{1,0:T(8,128)(2,1)}, bf16[288,768]{1,0:T(8,128)(2,1)}) custom-call(s32[1]{0:T(128)} %bitcast.11.chip_ref, s32[36]{0:T(128)} %broadcast_select_fusion.found_ref, bf16[1152,768]{1,0:T(8,128)(2,1)} %get-tuple-element.84.keep_ref, bf16[576,768]{1,0:T(8,128)(2,1)} %copy-done.5), custom_call_target="tpu_custom_call" | custom-call | flops 442368 | bytes 442368 | tf_op jit(solution)/shard_map/qkv_tiles/pallas_call | solution.py:345
  147.0 1.4 collective-permute-start.11
  148.4 0.6 collective-permute-start.12
  149.0 1.5 collective-permute-start.13
  150.5 0.1 split.19
  150.5 2.5 %collective-permute-start.10 = (bf16[768,384]{1,0:T(8,128)(2,1)S(1)}, bf16[768,384]{1,0:T(8,128)(2,1)S(1)}, u32[]{:S(2)}, u32[]{:S(2)}) collective-permute-start(bf16[768,384]{1,0:T(8,128)(2,1)S(1)} %split.19), channel_id=1, source_target_pairs={{0,24},{8,16},{16,8},{24,0},{1,25},{9,17},{17,9},{25,1},{2,26},{10... | collective-permute-start | bytes 1769480 | tf_op jit(solution)/shard_map/ppermute | solution.py:584
  153.1 2.8 %merge.1 = bf16[8,72,768]{2,1,0:T(8,128)(2,1)} custom-call(f32[8,64,768]{2,1,0:T(8,128)} %get-tuple-element.96.keep_ref, bf16[8,64,768]{2,1,0:T(8,128)(2,1)} %collective-permute-done.9.other_ref, f32[8,768]{1,0:T(8,128)} %get-tuple-element.98.norm_ref), custom_call_target="tpu_custom_call" | custom-call | flops 393216 | bytes 3145728 | tf_op jit(solution)/shard_map/merge/pallas_call | solution.py:283
  155.8 3.5 %all-to-all-start.3 = ((bf16[8,72,768]{2,1,0:T(8,128)(2,1)}), bf16[8,72,768]{2,1,0:T(8,128)(2,1)S(1)}, u32[]{:S(2)}, u32[]{:S(2)}) async-start(bf16[8,72,768]{2,1,0:T(8,128)(2,1)} %merge.1), calls=%async_computation.3 | async-start | bytes 1769472 | tf_op jit(solution)/shard_map/all_to_all | solution.py:580
  159.4 0.0 collective-permute-done.11
  159.4 2.3 %collective-permute-done.12 = bf16[288,768]{1,0:T(8,128)(2,1)} collective-permute-done((bf16[288,768]{1,0:T(8,128)(2,1)}, bf16[288,768]{1,0:T(8,128)(2,1)}, u32[]{:S(2)}, u32[]{:S(2)}) %collective-permute-start.12) | collective-permute-done | bytes 442400 | tf_op jit(solution)/shard_map/ppermute | solution.py:584
  161.7 9.6 %collective-permute-done.13 = bf16[288,768]{1,0:T(8,128)(2,1)} collective-permute-done((bf16[288,768]{1,0:T(8,128)(2,1)}, bf16[288,768]{1,0:T(8,128)(2,1)}, u32[]{:S(2)}, u32[]{:S(2)}) %collective-permute-start.13) | collective-permute-done | bytes 442400 | tf_op jit(solution)/shard_map/ppermute | solution.py:584
  171.3 2.4 %add_convert_fusion.3.refs_1_ = bf16[288,768]{1,0:T(8,128)(2,1)} fusion(bf16[288,768]{1,0:T(8,128)(2,1)} %collective-permute-done.13, bf16[288,768]{1,0:T(8,128)(2,1)} %collective-permute-done.12, bf16[288,768]{1,0:T(8,128)(2,1)} %collective-permute-done.11, bf16[288,768]{1,0:T(8,128)(2,1)} %get-tuple-element.104), kind=kLoop, calls=%fused_computation.3 | loop fusion | flops 1769472 | bytes 2211840 | tf_op jit(solution)/shard_map/convert_element_type | solution.py:786
  173.7 2.5 %pack.1 = (bf16[384,384]{1,0:T(8,128)(2,1)}, bf16[384,384]{1,0:T(8,128)(2,1)}, bf16[384,384]{1,0:T(8,128)(2,1)}, bf16[384,384]{1,0:T(8,128)(2,1)}) custom-call(s32[1]{0:T(128)} %bitcast.8.refs_0_.mine_ref, bf16[960,384]{1,0:T(8,128)(2,1)} %add_convert_fusion.1.refs_0_, bf16[288,768]{1,0:T(8,128)(2,1)} %add_convert_fusion.3.refs_1_), custom_call_target="tpu_custom_call" | custom-call | flops 2359296 | bytes 5898240 | tf_op jit(solution)/shard_map/pack/pallas_call | solution.py:677
  176.2 0.5 collective-permute-start.14
  176.6 2.6 %collective-permute-start.15 = (bf16[384,384]{1,0:T(8,128)(2,1)}, bf16[384,384]{1,0:T(8,128)(2,1)}, u32[]{:S(2)}, u32[]{:S(2)}) collective-permute-start(bf16[384,384]{1,0:T(8,128)(2,1)} %get-tuple-element.110), channel_id=1, source_target_pairs={{0,16},{8,24},{16,0},{24,8},{1,17},{9,25},{17,1},{25,9},{2,18},{10... | collective-permute-start | bytes 884744 | tf_op jit(solution)/shard_map/ppermute | solution.py:584
  179.2 1.3 collective-permute-start.16
  180.6 0.2 add_convert_fusion.2
  180.7 0.9 copy-done.2
  181.7 3.8 %first_norm_back.1 = (bf16[512,768]{1,0:T(8,128)(2,1)}, f32[8,128]{1,0:T(8,128)}) custom-call(bf16[512,768]{1,0:T(8,128)(2,1)} %bitcast.17, f32[768]{0:T(1024)} %gain_ref.3, bf16[8,72,768]{2,1,0:T(8,128)(2,1)} %copy-done.2, f32[512,768]{1,0:T(8,128)} %get-tuple-element.101.res_ref), custom_call_target="tpu_custom_call" | custom-call | flops 7864320 | bytes 4718592 | tf_op jit(solution)/shard_map/first_norm_back/pallas_call | solution.py:568
  185.5 0.8 collective-permute-start.20
  186.3 0.7 fusion
  187.0 1.4 collective-permute-start.17
  188.4 0.2 collective-permute-done.14.refs_1_
  188.6 1.3 collective-permute-start.18
  189.9 1.3 collective-permute-done.20
  191.2 1.4 collective-permute-start.19
  192.6 0.7 add.47
  193.3 5.2 %collective-permute-done.15.refs_2_ = bf16[384,384]{1,0:T(8,128)(2,1)} collective-permute-done((bf16[384,384]{1,0:T(8,128)(2,1)}, bf16[384,384]{1,0:T(8,128)(2,1)}, u32[]{:S(2)}, u32[]{:S(2)}) %collective-permute-start.15) | collective-permute-done | bytes 294944 | tf_op jit(solution)/shard_map/ppermute | solution.py:584
  198.4 2.2 %finish.2 = (f32[192,384]{1,0:T(8,128)}, f32[192,288]{1,0:T(8,128)}, f32[192,96]{1,0:T(8,128)}) custom-call(bf16[384,384]{1,0:T(8,128)(2,1)} %get-tuple-element.108.refs_0_, bf16[384,384]{1,0:T(8,128)(2,1)} %copy-done.9, bf16[384,384]{1,0:T(8,128)(2,1)} %collective-permute-done.15.refs_2_, bf16[384,384]{1,0:T(8,128)(2,1)} %collective-permute-done.16.refs_3_), custom_call_target="tpu_custom_call" | custom-call | flops 1179648 | bytes 2359296 | tf_op jit(solution)/shard_map/finish/pallas_call | solution.py:711
  200.6 2.3 %collective-permute-done.21 = f32[8,128]{1,0:T(8,128)S(1)} collective-permute-done((f32[8,128]{1,0:T(8,128)S(1)}, f32[8,128]{1,0:T(8,128)S(1)}, u32[]{:S(2)}, u32[]{:S(2)}) %collective-permute-start.21) | collective-permute-done | bytes 4128 | tf_op jit(solution)/shard_map/ppermute | solution.py:584
  202.9 0.6 slice.7
  203.5 0.6 copy-done.10
  204.2 0.0 copy-done.11
  204.2 0.1 copy-done.12
  204.3 1.9 finish.3
  (45 shorter events, 0.1 us)
Async XLA Ops:
  0.6 17.0 %copy-start = (s32[4,8]{1,0:T(4,128)S(1)}, s32[4,8]{1,0:T(4,128)}, u32[]{:S(2)}) copy-start(s32[4,8]{1,0:T(4,128)} %param.16) | copy-start | bytes 388
  17.6 2.3 %copy-start.6 = (bf16[8,64,768]{2,1,0:T(8,128)(2,1)}, bf16[8,64,768]{2,1,0:T(8,128)(2,1)S(1)}, u32[]{:S(2)}) copy-start(bf16[8,64,768]{2,1,0:T(8,128)(2,1)S(1)} %all_to_all.20.mine_ref) | copy-start | bytes 2359300
  17.6 2.3 %collective-permute-start = (bf16[8,64,768]{2,1,0:T(8,128)(2,1)S(1)}, bf16[8,64,768]{2,1,0:T(8,128)(2,1)S(1)}, u32[]{:S(2)}, u32[]{:S(2)}) collective-permute-start(bf16[8,64,768]{2,1,0:T(8,128)(2,1)S(1)} %all_to_all.20.mine_ref), channel_id=1, source_target_pairs={{0,1},{1,0},{2,3},{3,2},{4,5},{5,4},{6,7},{7,6},{8,9},{9,8},{10,11... | collective-permute-start | bytes 2359304 | tf_op jit(solution)/shard_map/ppermute | solution.py:584
  19.9 0.9 copy-start.17
  84.4 4.6 %copy-start.15 = (s32[36]{0:T(128)S(1)}, s32[36]{0:T(128)}, u32[]{:S(2)}) copy-start(s32[36]{0:T(128)} %constant.31.clone) | copy-start | bytes 436
  84.4 4.6 %copy-start.16 = (s32[36]{0:T(128)S(1)}, s32[36]{0:T(128)}, u32[]{:S(2)}) copy-start(s32[36]{0:T(128)} %constant.32.clone) | copy-start | bytes 436
  84.4 5.1 %copy-start.13 = (s32[36]{0:T(128)S(1)}, s32[36]{0:T(128)}, u32[]{:S(2)}) copy-start(s32[36]{0:T(128)} %constant.33.clone) | copy-start | bytes 436
  84.4 5.1 %copy-start.14 = (s32[36]{0:T(128)S(1)}, s32[36]{0:T(128)}, u32[]{:S(2)}) copy-start(s32[36]{0:T(128)} %constant.34.clone) | copy-start | bytes 436
  84.4 9.3 %collective-permute-start.1 = (bf16[4,768,384]{2,1,0:T(8,128)(2,1)}, bf16[4,768,384]{2,1,0:T(8,128)(2,1)S(1)}, u32[]{:S(2)}, u32[]{:S(2)}) collective-permute-start(bf16[4,768,384]{2,1,0:T(8,128)(2,1)} %get-tuple-element.67), channel_id=1, source_target_pairs={{0,1},{1,0},{2,3},{3,2},{4,5},{5,4},{6,7},{7,6},{8,9},{9,8},{10,11... | collective-permute-start | bytes 7077896 | tf_op jit(solution)/shard_map/ppermute | solution.py:584
  84.5 9.2 %collective-permute-start.2 = (bf16[4,8,96,384]{3,2,1,0:T(8,128)(2,1)}, bf16[4,8,96,384]{3,2,1,0:T(8,128)(2,1)}, u32[]{:S(2)}, u32[]{:S(2)}) collective-permute-start(bf16[4,8,96,384]{3,2,1,0:T(8,128)(2,1)} %bitcast.20), channel_id=1, source_target_pairs={{0,1},{1,0},{2,3},{3,2},{4,5},{5,4},{6,7},{7,6},{8,9},{9,8},{10,11... | collective-permute-start | bytes 7077896 | tf_op jit(solution)/shard_map/ppermute | solution.py:584
  85.0 17.2 %all-to-all-start.2 = ((bf16[8,128,384]{2,1,0:T(8,128)(2,1)}), bf16[8,128,384]{2,1,0:T(8,128)(2,1)S(1)}, u32[]{:S(2)}, u32[]{:S(2)}) async-start(bf16[8,128,384]{2,1,0:T(8,128)(2,1)} %get-tuple-element.65), calls=%async_computation.2 | async-start | bytes 1572864 | tf_op jit(solution)/shard_map/all_to_all | solution.py:580
  88.8 5.0 %collective-permute-start.3 = (bf16[4,96,768]{2,1,0:T(8,128)(2,1)}, bf16[4,96,768]{2,1,0:T(8,128)(2,1)}, u32[]{:S(2)}, u32[]{:S(2)}) collective-permute-start(bf16[4,96,768]{2,1,0:T(8,128)(2,1)} %get-tuple-element.71), channel_id=1, source_target_pairs={{0,1},{1,0},{2,3},{3,2},{4,5},{5,4},{6,7},{7,6},{8,9},{9,8},{10,11... | collective-permute-start | bytes 1769480 | tf_op jit(solution)/shard_map/ppermute | solution.py:584
  93.7 1.4 copy-start.3
  102.2 5.1 %copy-start.7 = (bf16[8,128,384]{2,1,0:T(8,128)(2,1)}, bf16[8,128,384]{2,1,0:T(8,128)(2,1)S(1)}, u32[]{:S(2)}) copy-start(bf16[8,128,384]{2,1,0:T(8,128)(2,1)S(1)} %all-to-all-done.2.g_ref) | copy-start | bytes 2359300
  102.2 40.0 %collective-permute-start.8 = (bf16[1536,384]{1,0:T(8,128)(2,1)}, bf16[1536,384]{1,0:T(8,128)(2,1)S(1)}, u32[]{:S(2)}, u32[]{:S(2)}) collective-permute-start(bf16[1536,384]{1,0:T(8,128)(2,1)} %get-tuple-element.90), channel_id=1, source_target_pairs={{0,8},{8,0},{16,24},{24,16},{1,9},{9,1},{17,25},{25,17},{2,10},{10... | collective-permute-start | bytes 3538952 | tf_op jit(solution)/shard_map/ppermute | solution.py:584
  103.8 32.3 %collective-permute-start.5 = (bf16[960,384]{1,0:T(8,128)(2,1)}, bf16[960,384]{1,0:T(8,128)(2,1)}, u32[]{:S(2)}, u32[]{:S(2)}) collective-permute-start(bf16[960,384]{1,0:T(8,128)(2,1)} %get-tuple-element.86), channel_id=1, source_target_pairs={{0,2},{1,3},{2,0},{3,1},{4,6},{5,7},{6,4},{7,5},{8,10},{9,11},{10,... | collective-permute-start | bytes 2211848 | tf_op jit(solution)/shard_map/ppermute | solution.py:584
  105.2 31.4 %collective-permute-start.6 = (bf16[960,384]{1,0:T(8,128)(2,1)}, bf16[960,384]{1,0:T(8,128)(2,1)}, u32[]{:S(2)}, u32[]{:S(2)}) collective-permute-start(bf16[960,384]{1,0:T(8,128)(2,1)} %get-tuple-element.87), channel_id=1, source_target_pairs={{0,4},{1,5},{2,6},{3,7},{4,0},{5,1},{6,2},{7,3},{8,12},{9,13},{10,... | collective-permute-start | bytes 2211848 | tf_op jit(solution)/shard_map/ppermute | solution.py:584
  105.8 33.6 %collective-permute-start.7 = (bf16[960,384]{1,0:T(8,128)(2,1)}, bf16[960,384]{1,0:T(8,128)(2,1)}, u32[]{:S(2)}, u32[]{:S(2)}) collective-permute-start(bf16[960,384]{1,0:T(8,128)(2,1)} %get-tuple-element.88), channel_id=1, source_target_pairs={{0,6},{1,7},{2,4},{3,5},{4,2},{5,3},{6,0},{7,1},{8,14},{9,15},{10,... | collective-permute-start | bytes 2211848 | tf_op jit(solution)/shard_map/ppermute | solution.py:584
  134.7 4.7 %copy-start.8 = (bf16[960,384]{1,0:T(8,128)(2,1)S(1)}, bf16[960,384]{1,0:T(8,128)(2,1)}, u32[]{:S(2)}) copy-start(bf16[960,384]{1,0:T(8,128)(2,1)} %get-tuple-element.85) | copy-start | bytes 2211844
  136.0 6.5 %collective-permute-start.4 = (bf16[576,768]{1,0:T(8,128)(2,1)S(1)}, bf16[576,768]{1,0:T(8,128)(2,1)S(1)}, u32[]{:S(2)}, u32[]{:S(2)}) collective-permute-start(bf16[576,768]{1,0:T(8,128)(2,1)S(1)} %slice.6), channel_id=1, source_target_pairs={{0,1},{1,0},{2,3},{3,2},{4,5},{5,4},{6,7},{7,6},{8,9},{9,8},{10,11... | collective-permute-start | bytes 2654216 | tf_op jit(solution)/shard_map/ppermute | solution.py:584
  136.1 6.1 %copy-start.4 = (bf16[1536,384]{1,0:T(8,128)(2,1)S(1)}, bf16[1536,384]{1,0:T(8,128)(2,1)}, u32[]{:S(2)}) copy-start(bf16[1536,384]{1,0:T(8,128)(2,1)} %get-tuple-element.89) | copy-start | bytes 3538948
  136.1 16.9 %collective-permute-start.9 = (bf16[8,64,768]{2,1,0:T(8,128)(2,1)}, bf16[8,64,768]{2,1,0:T(8,128)(2,1)}, u32[]{:S(2)}, u32[]{:S(2)}) collective-permute-start(bf16[8,64,768]{2,1,0:T(8,128)(2,1)} %get-tuple-element.97), channel_id=1, source_target_pairs={{0,1},{1,0},{2,3},{3,2},{4,5},{5,4},{6,7},{7,6},{8,9},{9,8},{10,11... | collective-permute-start | bytes 2359304 | tf_op jit(solution)/shard_map/ppermute | solution.py:584
  142.5 0.9 copy-start.5
  147.0 12.4 %collective-permute-start.11 = (bf16[288,768]{1,0:T(8,128)(2,1)}, bf16[288,768]{1,0:T(8,128)(2,1)}, u32[]{:S(2)}, u32[]{:S(2)}) collective-permute-start(bf16[288,768]{1,0:T(8,128)(2,1)} %get-tuple-element.105), channel_id=1, source_target_pairs={{0,2},{1,3},{2,0},{3,1},{4,6},{5,7},{6,4},{7,5},{8,10},{9,11},{10,... | collective-permute-start | bytes 1327112 | tf_op jit(solution)/shard_map/ppermute | solution.py:584
  148.4 13.4 %collective-permute-start.12 = (bf16[288,768]{1,0:T(8,128)(2,1)}, bf16[288,768]{1,0:T(8,128)(2,1)}, u32[]{:S(2)}, u32[]{:S(2)}) collective-permute-start(bf16[288,768]{1,0:T(8,128)(2,1)} %get-tuple-element.106), channel_id=1, source_target_pairs={{0,4},{1,5},{2,6},{3,7},{4,0},{5,1},{6,2},{7,3},{8,12},{9,13},{10,... | collective-permute-start | bytes 1327112 | tf_op jit(solution)/shard_map/ppermute | solution.py:584
  149.0 22.3 %collective-permute-start.13 = (bf16[288,768]{1,0:T(8,128)(2,1)}, bf16[288,768]{1,0:T(8,128)(2,1)}, u32[]{:S(2)}, u32[]{:S(2)}) collective-permute-start(bf16[288,768]{1,0:T(8,128)(2,1)} %get-tuple-element.107), channel_id=1, source_target_pairs={{0,6},{1,7},{2,4},{3,5},{4,2},{5,3},{6,0},{7,1},{8,14},{9,15},{10,... | collective-permute-start | bytes 1327112 | tf_op jit(solution)/shard_map/ppermute | solution.py:584
  150.5 30.0 %collective-permute-start.10 = (bf16[768,384]{1,0:T(8,128)(2,1)S(1)}, bf16[768,384]{1,0:T(8,128)(2,1)S(1)}, u32[]{:S(2)}, u32[]{:S(2)}) collective-permute-start(bf16[768,384]{1,0:T(8,128)(2,1)S(1)} %split.19), channel_id=1, source_target_pairs={{0,24},{8,16},{16,8},{24,0},{1,25},{9,17},{17,9},{25,1},{2,26},{10... | collective-permute-start | bytes 1769480 | tf_op jit(solution)/shard_map/ppermute | solution.py:584
  155.8 24.9 %all-to-all-start.3 = ((bf16[8,72,768]{2,1,0:T(8,128)(2,1)}), bf16[8,72,768]{2,1,0:T(8,128)(2,1)S(1)}, u32[]{:S(2)}, u32[]{:S(2)}) async-start(bf16[8,72,768]{2,1,0:T(8,128)(2,1)} %merge.1), calls=%async_computation.3 | async-start | bytes 1769472 | tf_op jit(solution)/shard_map/all_to_all | solution.py:580
  176.2 12.4 %collective-permute-start.14 = (bf16[384,384]{1,0:T(8,128)(2,1)}, bf16[384,384]{1,0:T(8,128)(2,1)S(1)}, u32[]{:S(2)}, u32[]{:S(2)}) collective-permute-start(bf16[384,384]{1,0:T(8,128)(2,1)} %get-tuple-element.109), channel_id=1, source_target_pairs={{0,8},{8,0},{16,24},{24,16},{1,9},{9,1},{17,25},{25,17},{2,10},{10... | collective-permute-start | bytes 884744 | tf_op jit(solution)/shard_map/ppermute | solution.py:584
  176.6 21.8 %collective-permute-start.15 = (bf16[384,384]{1,0:T(8,128)(2,1)}, bf16[384,384]{1,0:T(8,128)(2,1)}, u32[]{:S(2)}, u32[]{:S(2)}) collective-permute-start(bf16[384,384]{1,0:T(8,128)(2,1)} %get-tuple-element.110), channel_id=1, source_target_pairs={{0,16},{8,24},{16,0},{24,8},{1,17},{9,25},{17,1},{25,9},{2,18},{10... | collective-permute-start | bytes 884744 | tf_op jit(solution)/shard_map/ppermute | solution.py:584
  179.2 19.2 %collective-permute-start.16 = (bf16[384,384]{1,0:T(8,128)(2,1)}, bf16[384,384]{1,0:T(8,128)(2,1)}, u32[]{:S(2)}, u32[]{:S(2)}) collective-permute-start(bf16[384,384]{1,0:T(8,128)(2,1)} %get-tuple-element.111), channel_id=1, source_target_pairs={{0,24},{8,16},{16,8},{24,0},{1,25},{9,17},{17,9},{25,1},{2,26},{10... | collective-permute-start | bytes 884744 | tf_op jit(solution)/shard_map/ppermute | solution.py:584
  180.7 0.9 copy-start.2
  185.5 20.7 %copy-start.1 = (s32[4,8]{1,0:T(4,128)S(1)}, s32[4,8]{1,0:T(4,128)}, u32[]{:S(2)}) copy-start(s32[4,8]{1,0:T(4,128)} %param.16) | copy-start | bytes 388
  185.5 5.7 %collective-permute-start.20 = (f32[8,128]{1,0:T(8,128)}, f32[8,128]{1,0:T(8,128)S(1)}, u32[]{:S(2)}, u32[]{:S(2)}) collective-permute-start(f32[8,128]{1,0:T(8,128)} %get-tuple-element.116), channel_id=1, source_target_pairs={{0,8},{8,0},{16,24},{24,16},{1,9},{9,1},{17,25},{25,17},{2,10},{10... | collective-permute-start | bytes 12296 | tf_op jit(solution)/shard_map/ppermute | solution.py:584
  187.0 16.5 %collective-permute-start.17 = (bf16[192,384]{1,0:T(8,128)(2,1)S(1)}, bf16[192,384]{1,0:T(8,128)(2,1)S(1)}, u32[]{:S(2)}, u32[]{:S(2)}) collective-permute-start(bf16[192,384]{1,0:T(8,128)(2,1)S(1)} %get-tuple-element.119), channel_id=1, source_target_pairs={{0,2},{1,3},{2,0},{3,1},{4,6},{5,7},{6,4},{7,5},{8,10},{9,11},{10,... | collective-permute-start | bytes 442376 | tf_op jit(solution)/shard_map/ppermute | solution.py:584
  188.6 9.9 %copy-start.9 = (bf16[384,384]{1,0:T(8,128)(2,1)}, bf16[384,384]{1,0:T(8,128)(2,1)S(1)}, u32[]{:S(2)}) copy-start(bf16[384,384]{1,0:T(8,128)(2,1)S(1)} %collective-permute-done.14.refs_1_) | copy-start | bytes 884740
  188.6 15.0 %collective-permute-start.18 = (bf16[192,384]{1,0:T(8,128)(2,1)S(1)}, bf16[192,384]{1,0:T(8,128)(2,1)S(1)}, u32[]{:S(2)}, u32[]{:S(2)}) collective-permute-start(bf16[192,384]{1,0:T(8,128)(2,1)S(1)} %get-tuple-element.118), channel_id=1, source_target_pairs={{0,4},{1,5},{2,6},{3,7},{4,0},{5,1},{6,2},{7,3},{8,12},{9,13},{10,... | collective-permute-start | bytes 442376 | tf_op jit(solution)/shard_map/ppermute | solution.py:584
  191.2 12.4 %collective-permute-start.19 = (bf16[192,384]{1,0:T(8,128)(2,1)S(1)}, bf16[192,384]{1,0:T(8,128)(2,1)S(1)}, u32[]{:S(2)}, u32[]{:S(2)}) collective-permute-start(bf16[192,384]{1,0:T(8,128)(2,1)S(1)} %get-tuple-element.117), channel_id=1, source_target_pairs={{0,6},{1,7},{2,4},{3,5},{4,2},{5,3},{6,0},{7,1},{8,14},{9,15},{10,... | collective-permute-start | bytes 442376 | tf_op jit(solution)/shard_map/ppermute | solution.py:584
  198.4 4.5 %collective-permute-start.21 = (f32[8,128]{1,0:T(8,128)S(1)}, f32[8,128]{1,0:T(8,128)S(1)}, u32[]{:S(2)}, u32[]{:S(2)}) collective-permute-start(f32[8,128]{1,0:T(8,128)S(1)} %add.47), channel_id=1, source_target_pairs={{0,16},{8,24},{16,0},{24,8},{1,17},{9,25},{17,1},{25,9},{2,18},{10... | collective-permute-start | bytes 12296 | tf_op jit(solution)/shard_map/ppermute | solution.py:584
  203.5 0.7 copy-start.10
  203.5 0.7 copy-start.11
  203.5 0.7 copy-start.12
